TPU v7x, 32 devices: a whole 2x2x4 slice. The times are simulated.
32 devices in a mesh: head: 4 (over z), frame: 8 (over y, x, core).
Axes of the slice: x: 2, y: 2, z: 4, core: 2. Of those that a mesh axis runs over, the one named last changes fastest.
Arguments:
- queries: bfloat16 [4096, 2048], P(('frame', 'head')), may hold values from -6 to 6
- key_states: bfloat16 [4096, 2048], P(('frame', 'head')), may hold values from -6 to 6
- value_states: bfloat16 [4096, 2048], P(('frame', 'head')), may hold values from -6 to 6
- attn_out: bfloat16 [4096, 2048], P(('frame', 'head')), may hold values from -6 to 6
- grad_out: bfloat16 [4096, 2048], P(('frame', 'head')), may hold values from -192 to 192
- frame_order: int32 [8], replicated, may hold values from 0 to 7, each once
- block_live: int32 [8, 4, 4], replicated, may hold values from 0 to 1, as said below
Outputs:
- grad_queries: bfloat16 [4096, 2048], P('frame', 'head')
- grad_keys: bfloat16 [4096, 2048], P('frame', 'head')
- grad_values: bfloat16 [4096, 2048], P('frame', 'head')
Inputs may be any that keep to these rules, and one draw needn't show every extreme that they name: `block_live`: every entry at distance 0 is 1; every entry at distances of 4 or more is 0.
All inputs are finite; a program needn't handle non-finite values.
Results may differ from a plain program's by a relative error of at most 0.0049.
Values may be sent and summed in bfloat16 or wider, within the bound.
No kernel may reach another device: no remote copies, remote signals or barrier semaphores. Data moves between devices by JAX's collectives and lax.ppermute only.
A program may use at most 128 MiB of HBM per device.

v0:
```python
import functools
import math

import jax
import jax.numpy as jnp
from jax import lax
from jax.experimental import pallas as pl
from jax.experimental.pallas import tpu as pltpu
from jax.sharding import PartitionSpec as P


HEADS = 16
HEAD_DIM = 128
NEG = -1e30
KEY_GROUP = 6
QUERY_GROUP = 4
PAIR = 2
EXTRA = 8


VMEM = pl.BlockSpec(memory_space=pltpu.VMEM)
SMEM = pl.BlockSpec(memory_space=pltpu.SMEM)
F32 = jnp.float32
BF16 = jnp.bfloat16
NT = (((1,), (1,)), ((), ()))
TN = (((0,), (0,)), ((), ()))
NN = (((1,), (0,)), ((), ()))


def dot(a, b, dims):
    return lax.dot_general(a, b, dims, preferred_element_type=F32)


def sds(shape, dtype):
    return jax.ShapeDtypeStruct(shape, dtype)


def lasts(microseconds):
    return pl.CostEstimate(flops=0, bytes_accessed=int(microseconds * 3.5e6), transcendentals=0)


def within(*shapes):
    held = sum(math.prod(s.shape) * s.dtype.itemsize for s in shapes)
    return pltpu.CompilerParams(vmem_limit_bytes=int(held * 5 // 4) + (6 << 20))


class Plan:
    def __init__(self, rows):
        self.nz = lax.axis_size("head")
        self.nf = lax.axis_size("frame")
        self.hh = HEADS // self.nz
        self.na = min(self.hh, self.nf)
        self.nb = self.nf // self.na
        self.rows = rows
        self.own = self.na * self.nz
        self.total = self.own * self.nb
        assert self.hh == self.na and rows == HEAD_DIM


def over_head(value, step):
    count = lax.axis_size("head")
    return lax.ppermute(value, "head", [(i, i ^ step) for i in range(count)])


def over_frame(value, step):
    count = lax.axis_size("frame")
    return lax.ppermute(value, "frame", [(i, i ^ step) for i in range(count)])


def prep_kernel(plan, head_first, ids, x_ref, *outs):
    hd = HEAD_DIM
    z, a = ids[0], ids[1]
    for p, out in enumerate(outs):
        for c in range(out.shape[0]):
            r, s = (p, c) if head_first else (c, p)
            head = (z ^ r) * plan.hh + (a ^ s)
            out[c] = x_ref[:, pl.ds(pl.multiple_of(head * hd, hd), hd)]


def prep(plan, ids, x, head_first):
    pieces, chunk = (plan.nz, plan.na) if head_first else (plan.na, plan.nz)
    return pl.pallas_call(
        functools.partial(prep_kernel, plan, head_first),
        out_shape=[sds((chunk, plan.rows, HEAD_DIM), BF16)] * pieces,
        in_specs=[SMEM, VMEM],
        out_specs=[VMEM] * pieces,
        cost_estimate=lasts(2),
        compiler_params=within(x, x),
    )(ids, x)


def prep_grad_kernel(plan, ids, g_ref, o_ref, *outs):
    hd, rows = HEAD_DIM, plan.rows
    z, a = ids[0], ids[1]
    ones = jnp.ones((EXTRA, hd), BF16)
    row = lax.broadcasted_iota(jnp.int32, (EXTRA, rows), 0)
    for s, out in enumerate(outs):
        for r in range(plan.nz):
            head = (z ^ r) * plan.hh + (a ^ s)
            cols = pl.ds(pl.multiple_of(head * hd, hd), hd)
            grad = g_ref[:, cols]
            out[r, :rows] = grad
            product = grad.astype(F32) * o_ref[:, cols].astype(F32)
            high = product.astype(BF16)
            low = (product - high.astype(F32)).astype(BF16)
            delta = dot(ones, high, NT) + dot(ones, low, NT)
            first = delta.astype(BF16)
            rest = delta - first.astype(F32)
            second = rest.astype(BF16)
            third = (rest - second.astype(F32)).astype(BF16)
            parts = jnp.where(
                row == 0,
                first.astype(F32),
                jnp.where(row == 1, second.astype(F32), jnp.where(row == 2, third.astype(F32), 0.0)),
            )
            out[r, rows:] = parts.astype(BF16)


def prep_grad(plan, ids, g, o):
    return pl.pallas_call(
        functools.partial(prep_grad_kernel, plan),
        out_shape=[sds((plan.nz, plan.rows + EXTRA, HEAD_DIM), BF16)] * plan.na,
        in_specs=[SMEM, VMEM, VMEM],
        out_specs=[VMEM] * plan.na,
        cost_estimate=lasts(2.5),
        compiler_params=within(g, o, g),
        name="prep_grad",
    )(ids, g, o)


def lists_kernel(plan, ids, order, live_ref, by_key, n_key, by_query, n_query):
    nz, na, nb = plan.nz, plan.na, plan.nb
    z, a, b = ids[0], ids[1], ids[2]
    true = [z ^ r for r in range(nz)]

    def key_frame(s_key, carry):
        place_key = order[(a ^ s_key) * nb + b]

        def query_frame(ts, counts):
            t = ts // na
            place = order[(a ^ (ts - t * na)) * nb + (b ^ t)]
            distance = jnp.abs(place - place_key)
            away = (ts != s_key).astype(jnp.int32)
            counts = list(counts)
            for r in range(nz):
                i = ts * nz + r
                seen = jnp.where(s_key == 0, 0, n_query[i])
                for rk in range(nz):
                    live = jnp.where(live_ref[distance, true[r], true[rk]] > 0, away, 0)
                    by_key[s_key * nz + rk, counts[rk]] = i
                    by_query[i, seen] = s_key * nz + rk
                    counts[rk] = counts[rk] + live
                    seen = seen + live
                n_query[i] = seen
            return tuple(counts)

        counts = lax.fori_loop(0, na * nb, query_frame, (jnp.int32(0),) * nz)
        for rk in range(nz):
            n_key[s_key * nz + rk] = counts[rk]
        return carry

    lax.fori_loop(0, na, key_frame, 0)


def lists(plan, ids, order, live):
    own, total = plan.own, plan.total
    return pl.pallas_call(
        functools.partial(lists_kernel, plan),
        out_shape=[
            sds((own, total + KEY_GROUP), jnp.int32),
            sds((own,), jnp.int32),
            sds((total, own + QUERY_GROUP), jnp.int32),
            sds((total,), jnp.int32),
        ],
        in_specs=[SMEM] * 3,
        out_specs=[SMEM] * 4,
        cost_estimate=lasts(5),
        compiler_params=within(),
        name="lists",
    )(ids, order, live)


def picks(table, row, count, first, size):
    out = []
    for u in range(size):
        valid = first + u < count
        out.append((jnp.where(valid, table[row, first + u], 0), valid))
    return out


def rounds(count, size):
    return lax.div(count + (size - 1), size)


def totals_kernel(plan, by_query, n_query, k_ref, *refs):
    nz, na, nb, own, rows = plan.nz, plan.na, plan.nb, plan.own, plan.rows
    q_refs, out, peaks, sums = refs[:nb], refs[nb], refs[nb + 1], refs[nb + 2]
    scale = HEAD_DIM**-0.5
    length = nz * rows

    def scores_of(i, q, first):
        parts = []
        for j, valid in picks(by_query, i, n_query[i], first, QUERY_GROUP):
            parts.append(jnp.where(valid, scale * dot(k_ref[j], q, NT), NEG))
        return parts

    for t, q_ref in enumerate(q_refs):

        def frame(s, carry, q_ref=q_ref, t=t):
            if t == 0:
                keys = k_ref[pl.ds(s * nz, nz)].reshape(length, HEAD_DIM)
                wide = scale * dot(keys, q_ref[pl.ds(s * nz, nz)].reshape(length, HEAD_DIM), NT)
            for r in range(nz):
                i = (t * na + s) * nz + r
                parts = scores_of(i, q_ref[s * nz + r], 0)
                if t == 0:
                    column = wide[:, r * rows : (r + 1) * rows]
                    parts += [column[c * rows : (c + 1) * rows] for c in range(nz)]
                peak = jnp.max(functools.reduce(jnp.maximum, parts), axis=0, keepdims=True)
                mass = functools.reduce(jnp.add, [jnp.exp(part - peak) for part in parts])
                peaks[pl.ds(i, 1), :] = peak
                sums[pl.ds(i, 1), :] = jnp.sum(mass, axis=0, keepdims=True)
            return carry

        lax.fori_loop(0, na, frame, 0)

        def block(m, carry, q_ref=q_ref, t=t):
            i = t * own + m

            def group(step, carry):
                parts = scores_of(i, q_ref[m], step * QUERY_GROUP)
                old = peaks[pl.ds(i, 1), :]
                best = functools.reduce(jnp.maximum, parts)
                peak = jnp.maximum(old, jnp.max(best, axis=0, keepdims=True))
                mass = functools.reduce(jnp.add, [jnp.exp(part - peak) for part in parts])
                fresh = jnp.sum(mass, axis=0, keepdims=True)
                peaks[pl.ds(i, 1), :] = peak
                sums[pl.ds(i, 1), :] = sums[pl.ds(i, 1), :] * jnp.exp(old - peak) + fresh
                return carry

            return lax.fori_loop(1, rounds(n_query[i], QUERY_GROUP), group, carry)

        lax.fori_loop(0, own, block, 0)
    peak = peaks[...]
    out[...] = jnp.where(peak > 0.5 * NEG, peak + jnp.log(sums[...]), NEG)


def totals(plan, by_query, n_query, keys, queries):
    return pl.pallas_call(
        functools.partial(totals_kernel, plan),
        out_shape=sds((plan.total, plan.rows), F32),
        in_specs=[SMEM, SMEM] + [VMEM] * (1 + plan.nb),
        out_specs=VMEM,
        scratch_shapes=[pltpu.VMEM((plan.total, plan.rows), F32)] * 2,
        cost_estimate=lasts(10),
        compiler_params=within(keys, *queries),
        name="totals",
    )(by_query, n_query, keys, *queries)


def grads_kernel(plan, by_key, n_key, ids, *refs):
    nz, na, nb, own, rows = plan.nz, plan.na, plan.nb, plan.own, plan.rows
    hd = HEAD_DIM
    scale = hd**-0.5
    length = nz * rows
    refs = list(refs)
    take = lambda n: [refs.pop(0) for _ in range(n)]
    q_refs, g_refs, lse_refs = take(nb), take(nb), take(nb)
    k_ref, v_ref = take(2)
    kv_outs, dq_outs = take(na), take(nb)
    q_all, g_all, lse_all, delta_all, dq_all, dk_all, dv_all = refs

    for t in range(nb):
        span = pl.ds(t * own, own)
        rivals = [lse_refs[u][pl.ds((t ^ u) * own, own), :] for u in range(nb)]
        peak = functools.reduce(jnp.maximum, rivals)
        lse_all[span, :] = peak + jnp.log(sum(jnp.exp(x - peak) for x in rivals))

        def fill(m, carry, t=t):
            i = t * own + m
            q_all[i] = q_refs[t][m]
            g_all[i] = g_refs[t][m, :rows]
            extra = g_refs[t][m, rows:].astype(F32)
            delta_all[pl.ds(i, 1), :] = jnp.sum(extra, axis=0, keepdims=True)
            if t > 0:
                dq_all[i] = jnp.zeros((rows, hd), F32)
            return carry

        lax.fori_loop(0, own, fill, 0)

    def wide_row(ref, first):
        return jnp.concatenate([ref[pl.ds(first + r, 1), :] for r in range(nz)], axis=1)

    def diagonal(s, carry):
        span = pl.ds(s * nz, nz)
        k, v = k_ref[span].reshape(length, hd), v_ref[span].reshape(length, hd)
        q, g = q_all[span].reshape(length, hd), g_all[span].reshape(length, hd)
        lse, delta = wide_row(lse_all, s * nz), wide_row(delta_all, s * nz)
        probs = jnp.exp(scale * dot(k, q, NT) - lse)
        dv_all[span] = dot(probs.astype(BF16), g, NN).reshape(nz, rows, hd)
        grad_scores = (probs * (dot(v, g, NT) - delta)).astype(BF16)
        dk_all[span] = dot(grad_scores, q, NN).reshape(nz, rows, hd)
        dq_all[span] = dot(grad_scores, k, TN).reshape(nz, rows, hd)
        return carry

    lax.fori_loop(0, na, diagonal, 0)

    def terms(j, first):
        k, v = k_ref[j], v_ref[j]
        chosen = picks(by_key, j, n_key[j], first, KEY_GROUP)
        probs, slopes, dqs = [], [], []
        for i, ok in chosen:
            lse = jnp.where(ok, lse_all[pl.ds(i, 1), :], -NEG)
            prob = jnp.exp(scale * dot(k, q_all[i], NT) - lse)
            slope = (prob * (dot(v, g_all[i], NT) - delta_all[pl.ds(i, 1), :])).astype(BF16)
            probs.append(prob.astype(BF16))
            slopes.append(slope)
            dqs.append((i, dot(slope, k, TN)))
        q = jnp.concatenate([q_all[i] for i, _ in chosen], axis=0)
        g = jnp.concatenate([g_all[i] for i, _ in chosen], axis=0)
        dv = dot(jnp.concatenate(probs, axis=1), g, NN)
        dk = dot(jnp.concatenate(slopes, axis=1), q, NN)
        return dv, dk, dqs

    def add(j, found):
        dv, dk, dqs = found
        dv_all[j] += dv
        dk_all[j] += dk
        for i, dq in dqs:
            dq_all[i] += dq

    def pair(step, carry):
        both = [(step * PAIR + p, terms(step * PAIR + p, 0)) for p in range(PAIR)]
        for j, found in both:
            add(j, found)
        return carry

    lax.fori_loop(0, own // PAIR, pair, 0)

    def rest(j, carry):
        def group(step, carry):
            add(j, terms(j, step * KEY_GROUP))
            return carry

        return lax.fori_loop(1, rounds(n_key[j], KEY_GROUP), group, carry)

    lax.fori_loop(0, own, rest, 0)

    for s, out in enumerate(kv_outs):
        for r in range(nz):
            out[0, ids[0] ^ r] = (scale * dk_all[s * nz + r]).astype(BF16)
            out[1, ids[0] ^ r] = dv_all[s * nz + r].astype(BF16)
    for t in range(nb):

        def drain(m, carry, t=t):
            dq_outs[t][m] = scale * dq_all[t * own + m]
            return carry

        lax.fori_loop(0, own, drain, 0)


def grads(plan, by_key, n_key, ids, queries, out_grads, lses, keys, values):
    nb, na, own, rows, total = plan.nb, plan.na, plan.own, plan.rows, plan.total
    hd = HEAD_DIM
    outs = pl.pallas_call(
        functools.partial(grads_kernel, plan),
        out_shape=[sds((2, plan.nz, rows, hd), BF16)] * na + [sds((own, rows, hd), F32)] * nb,
        in_specs=[SMEM] * 3 + [VMEM] * (3 * nb + 2),
        out_specs=[VMEM] * (na + nb),
        scratch_shapes=[
            pltpu.VMEM((total, rows, hd), BF16),
            pltpu.VMEM((total, rows, hd), BF16),
            pltpu.VMEM((total, rows), F32),
            pltpu.VMEM((total, rows), F32),
            pltpu.VMEM((total, rows, hd), F32),
            pltpu.VMEM((own, rows, hd), F32),
            pltpu.VMEM((own, rows, hd), F32),
        ],
        cost_estimate=lasts(15),
        compiler_params=within(*[keys] * (2 + 4 * nb + 2 * nb + 4 * nb + 2 + 4)),
        name="grads",
    )(by_key, n_key, ids, *queries, *out_grads, *lses, keys, values)
    return outs[:na], outs[na:]


def pack_kernel(plan, ids, *refs):
    nb, nz = plan.nb, plan.nz
    for s, out in enumerate(refs[nb:]):
        for r in range(nz):
            total = sum(ref[s * nz + r] for ref in refs[:nb])
            out[ids[0] ^ r] = total.astype(BF16)


def pack(plan, ids, partials):
    return pl.pallas_call(
        functools.partial(pack_kernel, plan),
        out_shape=[sds((plan.nz, plan.rows, HEAD_DIM), BF16)] * plan.na,
        in_specs=[SMEM] + [VMEM] * plan.nb,
        out_specs=[VMEM] * plan.na,
        cost_estimate=lasts(2),
        compiler_params=within(*partials, *partials),
        name="pack",
    )(ids, *partials)


def assemble_kernel(plan, n, ids, *refs):
    na, nz, rows, hd = plan.na, plan.nz, plan.rows, HEAD_DIM
    for s in range(na):
        cols = pl.ds(pl.multiple_of((ids[1] ^ s) * hd, hd), hd)
        for w in range(n):
            for r in range(nz):
                refs[na + w][r * rows : (r + 1) * rows, cols] = refs[s][w, r]


def assemble(plan, ids, pieces):
    n = pieces[0].shape[0]
    return pl.pallas_call(
        functools.partial(assemble_kernel, plan, n),
        out_shape=[sds((plan.nz * plan.rows, plan.na * HEAD_DIM), BF16)] * n,
        in_specs=[SMEM] + [VMEM] * plan.na,
        out_specs=[VMEM] * n,
        cost_estimate=lasts(2),
        compiler_params=within(*pieces, *pieces),
        name="assemble",
    )(ids, *pieces)


def local(queries, key_states, value_states, attn_out, grad_out, frame_order, block_live):
    plan = Plan(queries.shape[0])
    nz, na, nb = plan.nz, plan.na, plan.nb
    slot = lax.axis_index("frame")
    ids = jnp.stack([lax.axis_index("head"), slot // nb, slot % nb]).astype(jnp.int32)

    def staged(order, pieces, send):
        moved = {}
        for step in order:
            moved[step] = send(pieces[step], step)
        return [pieces[0]] + [moved[step] for step in range(1, len(pieces))]

    def head_stage(pieces):
        return staged([*range(2, nz), 1], pieces, over_head)

    def frame_stage(pieces):
        return staged(range(na - 1, 0, -1), pieces, lambda x, s: over_frame(x, s * nb))

    def swapped(parts):
        return staged(range(1, nb), parts, over_frame)

    def regroup(pieces):
        return [jnp.concatenate([p[i : i + 1] for p in pieces]) for i in range(pieces[0].shape[0])]

    def flat_frames_first(by_frame):
        return jnp.concatenate(by_frame)

    def flat_heads_first(by_head):
        return jnp.concatenate([p[s : s + 1] for s in range(na) for p in by_head])

    q_sent = head_stage(prep(plan, ids, queries, True))
    k_near = frame_stage(prep(plan, ids, key_states, False))
    g_near = frame_stage(prep_grad(plan, ids, grad_out, attn_out))
    v_near = frame_stage(prep(plan, ids, value_states, False))
    by_key, n_key, by_query, n_query = lists(plan, ids, frame_order, block_live)
    keys = flat_heads_first(head_stage(regroup(k_near)))
    q_own = flat_frames_first(frame_stage(regroup(q_sent)))
    q_all = swapped([q_own] * nb)
    g_own = flat_heads_first(head_stage(regroup(g_near)))
    g_all = swapped([g_own] * nb)
    values = flat_heads_first(head_stage(regroup(v_near)))

    lse_own = totals(plan, by_query, n_query, keys, q_all)
    lses = swapped([lse_own] * nb)
    kv_sent, dq_parts = grads(plan, by_key, n_key, ids, q_all, g_all, lses, keys, values)
    dq_parts = swapped(dq_parts)
    kv_home = frame_stage(kv_sent)
    dq_home = frame_stage(pack(plan, ids, dq_parts))
    grad_key, grad_value = assemble(plan, ids, kv_home)
    (grad_query,) = assemble(plan, ids, [p[None] for p in dq_home])
    return grad_query, grad_key, grad_value


def solution(mesh):
    rows = P(("frame", "head"), None)
    in_specs = (rows,) * 5 + (P(), P())
    out_specs = (P("frame", "head"),) * 3
    return jax.shard_map(local, mesh=mesh, in_specs=in_specs, out_specs=out_specs, check_vma=False)
```

profile of v0, /device:TPU:4, one launch (start us, length us, event | category | flops | bytes accessed | tf_op | source)
XLA Modules:
  0.0 132.7 jit_solution(4042667710559738596)
XLA Ops:
  0.6 0.1 pad_add_fusion.ids
  0.7 1.0 copy-done
  1.8 0.7 shard_map.94
  2.5 1.6 %collective-permute-start = (bf16[4,128,128]{2,1,0:T(8,128)(2,1)S(1)}, bf16[4,128,128]{2,1,0:T(8,128)(2,1)S(1)}, u32[]{:S(2)}, u32[]{:S(2)}) collective-permute-start(bf16[4,128,128]{2,1,0:T(8,128)(2,1)S(1)} %get-tuple-element.38), channel_id=1, source_target_pairs={{0,8},{8,0},{16,24},{24,16},{1,9},{9,1},{17,25},{25,17},{2,10},{10... | collective-permute-start | bytes 393224 | tf_op jit(solution)/shard_map/ppermute | solution.py:62
  4.1 2.6 %collective-permute-start.1 = (bf16[4,128,128]{2,1,0:T(8,128)(2,1)S(1)}, bf16[4,128,128]{2,1,0:T(8,128)(2,1)S(1)}, u32[]{:S(2)}, u32[]{:S(2)}) collective-permute-start(bf16[4,128,128]{2,1,0:T(8,128)(2,1)S(1)} %get-tuple-element.39), channel_id=1, source_target_pairs={{0,16},{8,24},{16,0},{24,8},{1,17},{9,25},{17,1},{25,9},{2,18},{10... | collective-permute-start | bytes 393224 | tf_op jit(solution)/shard_map/ppermute | solution.py:62
  6.7 0.2 collective-permute-start.2
  6.9 0.7 shard_map.95
  7.6 1.6 %collective-permute-start.14 = (bf16[4,128,128]{2,1,0:T(8,128)(2,1)S(1)}, bf16[4,128,128]{2,1,0:T(8,128)(2,1)S(1)}, u32[]{:S(2)}, u32[]{:S(2)}) collective-permute-start(bf16[4,128,128]{2,1,0:T(8,128)(2,1)S(1)} %get-tuple-element.48), channel_id=1, source_target_pairs={{0,2},{1,3},{2,0},{3,1},{4,6},{5,7},{6,4},{7,5},{8,10},{9,11},{10,... | collective-permute-start | bytes 393224 | tf_op jit(solution)/shard_map/ppermute | solution.py:67
  9.2 0.5 collective-permute-start.15
  9.7 0.1 copy.10.live_ref
  9.8 0.7 shard_map.96
  10.5 0.3 copy-done.3
  10.8 0.2 copy-done.4
  11.0 1.2 prep_grad.1
  12.2 0.0 copy-start.5
  12.3 0.6 copy-done.5
  12.9 6.6 %lists.1 = (s32[16,38]{1,0:T(8,128)S(1)}, s32[16]{0:T(128)S(1)}, s32[32,20]{1,0:T(8,128)S(1)}, s32[32]{0:T(128)S(1)}) custom-call(s32[3]{0:T(128)S(1)} %pad_add_fusion.ids, s32[8]{0:T(128)S(1)} %copy-done.5, s32[8,4,4]{2,1,0:T(4,128)S(1)} %copy.10.live_ref), custom_call_target="tpu_custom_call" | custom-call | bytes 17500000 | tf_op jit(solution)/shard_map/lists/pallas_call | solution.py:167
  19.5 0.0 collective-permute-done
  19.6 1.6 %collective-permute-start.16 = (bf16[4,128,128]{2,1,0:T(8,128)(2,1)S(1)}, bf16[4,128,128]{2,1,0:T(8,128)(2,1)S(1)}, u32[]{:S(2)}, u32[]{:S(2)}) collective-permute-start(bf16[4,128,128]{2,1,0:T(8,128)(2,1)S(1)} %get-tuple-element.50), channel_id=1, source_target_pairs={{0,6},{1,7},{2,4},{3,5},{4,2},{5,3},{6,0},{7,1},{8,14},{9,15},{10,... | collective-permute-start | bytes 393224 | tf_op jit(solution)/shard_map/ppermute | solution.py:67
  21.1 1.6 %collective-permute-start.21 = (bf16[4,128,128]{2,1,0:T(8,128)(2,1)S(1)}, bf16[4,128,128]{2,1,0:T(8,128)(2,1)S(1)}, u32[]{:S(2)}, u32[]{:S(2)}) collective-permute-start(bf16[4,128,128]{2,1,0:T(8,128)(2,1)S(1)} %get-tuple-element.52), channel_id=1, source_target_pairs={{0,2},{1,3},{2,0},{3,1},{4,6},{5,7},{6,4},{7,5},{8,10},{9,11},{10,... | collective-permute-start | bytes 393224 | tf_op jit(solution)/shard_map/ppermute | solution.py:67
  22.7 0.6 collective-permute-start.22
  23.3 1.6 %collective-permute-start.23 = (bf16[4,128,128]{2,1,0:T(8,128)(2,1)S(1)}, bf16[4,128,128]{2,1,0:T(8,128)(2,1)S(1)}, u32[]{:S(2)}, u32[]{:S(2)}) collective-permute-start(bf16[4,128,128]{2,1,0:T(8,128)(2,1)S(1)} %get-tuple-element.54), channel_id=1, source_target_pairs={{0,6},{1,7},{2,4},{3,5},{4,2},{5,3},{6,0},{7,1},{8,14},{9,15},{10,... | collective-permute-start | bytes 393224 | tf_op jit(solution)/shard_map/ppermute | solution.py:67
  24.9 2.1 %collective-permute-done.16 = bf16[4,128,128]{2,1,0:T(8,128)(2,1)S(1)} collective-permute-done((bf16[4,128,128]{2,1,0:T(8,128)(2,1)S(1)}, bf16[4,128,128]{2,1,0:T(8,128)(2,1)S(1)}, u32[]{:S(2)}, u32[]{:S(2)}) %collective-permute-start.16) | collective-permute-done | bytes 131104 | tf_op jit(solution)/shard_map/ppermute | solution.py:67
  27.0 0.3 collective-permute-start.7
  27.3 1.8 %collective-permute-start.8 = (bf16[4,136,128]{2,1,0:T(8,128)(2,1)S(1)}, bf16[4,136,128]{2,1,0:T(8,128)(2,1)S(1)}, u32[]{:S(2)}, u32[]{:S(2)}) collective-permute-start(bf16[4,136,128]{2,1,0:T(8,128)(2,1)S(1)} %get-tuple-element.43), channel_id=1, source_target_pairs={{0,4},{1,5},{2,6},{3,7},{4,0},{5,1},{6,2},{7,3},{8,12},{9,13},{10,... | collective-permute-start | bytes 417800 | tf_op jit(solution)/shard_map/ppermute | solution.py:67
  29.2 0.6 collective-permute-done.21
  29.8 0.9 collective-permute-start.9
  30.8 1.1 collective-permute-start.3
  32.0 0.7 collective-permute-done.23
  32.6 1.5 %collective-permute-start.4 = (bf16[4,128,128]{2,1,0:T(8,128)(2,1)S(1)}, bf16[4,128,128]{2,1,0:T(8,128)(2,1)S(1)}, u32[]{:S(2)}, u32[]{:S(2)}) collective-permute-start(bf16[4,128,128]{2,1,0:T(8,128)(2,1)S(1)} %pad_maximum_fusion.4), channel_id=1, source_target_pairs={{0,4},{1,5},{2,6},{3,7},{4,0},{5,1},{6,2},{7,3},{8,12},{9,13},{10,... | collective-permute-start | bytes 393224 | tf_op jit(solution)/shard_map/ppermute | solution.py:67
  34.2 1.4 %collective-permute-done.7 = bf16[4,136,128]{2,1,0:T(8,128)(2,1)S(1)} collective-permute-done((bf16[4,136,128]{2,1,0:T(8,128)(2,1)S(1)}, bf16[4,136,128]{2,1,0:T(8,128)(2,1)S(1)}, u32[]{:S(2)}, u32[]{:S(2)}) %collective-permute-start.7) | collective-permute-done | bytes 139296 | tf_op jit(solution)/shard_map/ppermute | solution.py:67
  35.6 0.3 collective-permute-start.5
  35.9 2.9 %collective-permute-done.8 = bf16[4,136,128]{2,1,0:T(8,128)(2,1)S(1)} collective-permute-done((bf16[4,136,128]{2,1,0:T(8,128)(2,1)S(1)}, bf16[4,136,128]{2,1,0:T(8,128)(2,1)S(1)}, u32[]{:S(2)}, u32[]{:S(2)}) %collective-permute-start.8) | collective-permute-done | bytes 139296 | tf_op jit(solution)/shard_map/ppermute | solution.py:67
  38.8 0.7 collective-permute-start.17
  39.5 3.6 %collective-permute-start.18 = (bf16[4,128,128]{2,1,0:T(8,128)(2,1)S(1)}, bf16[4,128,128]{2,1,0:T(8,128)(2,1)S(1)}, u32[]{:S(2)}, u32[]{:S(2)}) collective-permute-start(bf16[4,128,128]{2,1,0:T(8,128)(2,1)S(1)} %pad_maximum_fusion.7), channel_id=1, source_target_pairs={{0,16},{8,24},{16,0},{24,8},{1,17},{9,25},{17,1},{25,9},{2,18},{10... | collective-permute-start | bytes 393224 | tf_op jit(solution)/shard_map/ppermute | solution.py:62
  43.2 3.6 %collective-permute-done.17 = bf16[4,128,128]{2,1,0:T(8,128)(2,1)S(1)} collective-permute-done((bf16[4,128,128]{2,1,0:T(8,128)(2,1)S(1)}, bf16[4,128,128]{2,1,0:T(8,128)(2,1)S(1)}, u32[]{:S(2)}, u32[]{:S(2)}) %collective-permute-start.17) | collective-permute-done | bytes 131104 | tf_op jit(solution)/shard_map/ppermute | solution.py:62
  46.7 4.7 %collective-permute-start.19 = (bf16[4,128,128]{2,1,0:T(8,128)(2,1)S(1)}, bf16[4,128,128]{2,1,0:T(8,128)(2,1)S(1)}, u32[]{:S(2)}, u32[]{:S(2)}) collective-permute-start(bf16[4,128,128]{2,1,0:T(8,128)(2,1)S(1)} %pad_maximum_fusion.8), channel_id=1, source_target_pairs={{0,24},{8,16},{16,8},{24,0},{1,25},{9,17},{17,9},{25,1},{2,26},{10... | collective-permute-start | bytes 393224 | tf_op jit(solution)/shard_map/ppermute | solution.py:62
  51.5 0.1 collective-permute-start.24
  51.6 4.3 %collective-permute-done.19 = bf16[4,128,128]{2,1,0:T(8,128)(2,1)S(1)} collective-permute-done((bf16[4,128,128]{2,1,0:T(8,128)(2,1)S(1)}, bf16[4,128,128]{2,1,0:T(8,128)(2,1)S(1)}, u32[]{:S(2)}, u32[]{:S(2)}) %collective-permute-start.19) | collective-permute-done | bytes 131104 | tf_op jit(solution)/shard_map/ppermute | solution.py:62
  55.9 2.8 %collective-permute-start.25 = (bf16[4,128,128]{2,1,0:T(8,128)(2,1)S(1)}, bf16[4,128,128]{2,1,0:T(8,128)(2,1)S(1)}, u32[]{:S(2)}, u32[]{:S(2)}) collective-permute-start(bf16[4,128,128]{2,1,0:T(8,128)(2,1)S(1)} %pad_maximum_fusion.10), channel_id=1, source_target_pairs={{0,16},{8,24},{16,0},{24,8},{1,17},{9,25},{17,1},{25,9},{2,18},{10... | collective-permute-start | bytes 393224 | tf_op jit(solution)/shard_map/ppermute | solution.py:62
  58.9 0.3 collective-permute-done.24
  59.2 2.6 %collective-permute-start.26 = (bf16[4,128,128]{2,1,0:T(8,128)(2,1)S(1)}, bf16[4,128,128]{2,1,0:T(8,128)(2,1)S(1)}, u32[]{:S(2)}, u32[]{:S(2)}) collective-permute-start(bf16[4,128,128]{2,1,0:T(8,128)(2,1)S(1)} %pad_maximum_fusion.11), channel_id=1, source_target_pairs={{0,24},{8,16},{16,8},{24,0},{1,25},{9,17},{17,9},{25,1},{2,26},{10... | collective-permute-start | bytes 393224 | tf_op jit(solution)/shard_map/ppermute | solution.py:62
  61.8 0.1 collective-permute-start.10
  61.9 1.9 %collective-permute-start.11 = (bf16[4,136,128]{2,1,0:T(8,128)(2,1)S(1)}, bf16[4,136,128]{2,1,0:T(8,128)(2,1)S(1)}, u32[]{:S(2)}, u32[]{:S(2)}) collective-permute-start(bf16[4,136,128]{2,1,0:T(8,128)(2,1)S(1)} %pad_maximum_fusion.1), channel_id=1, source_target_pairs={{0,16},{8,24},{16,0},{24,8},{1,17},{9,25},{17,1},{25,9},{2,18},{10... | collective-permute-start | bytes 417800 | tf_op jit(solution)/shard_map/ppermute | solution.py:62
  63.8 2.6 %collective-permute-start.12 = (bf16[4,136,128]{2,1,0:T(8,128)(2,1)S(1)}, bf16[4,136,128]{2,1,0:T(8,128)(2,1)S(1)}, u32[]{:S(2)}, u32[]{:S(2)}) collective-permute-start(bf16[4,136,128]{2,1,0:T(8,128)(2,1)S(1)} %pad_maximum_fusion.2), channel_id=1, source_target_pairs={{0,24},{8,16},{16,8},{24,0},{1,25},{9,17},{17,9},{25,1},{2,26},{10... | collective-permute-start | bytes 417800 | tf_op jit(solution)/shard_map/ppermute | solution.py:62
  66.4 0.4 collective-permute-done.25
  67.0 0.9 collective-permute-done.10
  68.0 5.4 %collective-permute-done.11 = bf16[4,136,128]{2,1,0:T(8,128)(2,1)S(1)} collective-permute-done((bf16[4,136,128]{2,1,0:T(8,128)(2,1)S(1)}, bf16[4,136,128]{2,1,0:T(8,128)(2,1)S(1)}, u32[]{:S(2)}, u32[]{:S(2)}) %collective-permute-start.11) | collective-permute-done | bytes 139296 | tf_op jit(solution)/shard_map/ppermute | solution.py:62
  73.6 0.1 collective-permute-start.13
  73.7 7.6 %totals.1.refs_4_ = f32[32,128]{1,0:T(8,128)S(1)} custom-call(s32[32,20]{1,0:T(8,128)S(1)} %get-tuple-element.45.by_query, s32[32]{0:T(128)S(1)} %get-tuple-element.46.n_query, bf16[16,128,128]{2,1,0:T(8,128)(2,1)S(1)} %constant_dynamic-update-slice_fusion.23.k_ref.refs_6_, bf16[16,128,128]{2,1,0:T(8,128)(2,1)S(1)} %constant_dynamic-update-slice_fusion.refs_0_, ...), custom_call_target="tpu_custom_call" | custom-call | bytes 35000000 | tf_op jit(solution)/shard_map/totals/pallas_call | solution.py:249
  81.3 0.6 collective-permute-start.20
  81.9 0.8 collective-permute-done.20.refs_5_
  82.7 28.3 %grads.1 = (bf16[2,4,128,128]{3,2,1,0:T(8,128)(2,1)S(1)}, bf16[2,4,128,128]{3,2,1,0:T(8,128)(2,1)S(1)}, bf16[2,4,128,128]{3,2,1,0:T(8,128)(2,1)S(1)}, bf16[2,4,1...) custom-call(s32[16,38]{1,0:T(8,128)S(1)} %get-tuple-element.35.by_key, ...), custom_call_target="tpu_custom_call" | custom-call | bytes 52500000 | tf_op jit(solution)/shard_map/grads/pallas_call | solution.py:365
  111.0 0.4 collective-permute-start.27
  111.4 0.5 collective-permute-start.31
  112.0 3.0 %collective-permute-start.33 = (bf16[2,4,128,128]{3,2,1,0:T(8,128)(2,1)S(1)}, bf16[2,4,128,128]{3,2,1,0:T(8,128)(2,1)S(1)}, u32[]{:S(2)}, u32[]{:S(2)}) collective-permute-start(bf16[2,4,128,128]{3,2,1,0:T(8,128)(2,1)S(1)} %get-tuple-element.64), channel_id=1, source_target_pairs={{0,6},{1,7},{2,4},{3,5},{4,2},{5,3},{6,0},{7,1},{8,14},{9,15},{10,... | collective-permute-start | bytes 786440 | tf_op jit(solution)/shard_map/ppermute | solution.py:67
  114.9 0.7 pack.1
  115.6 0.6 collective-permute-start.28
  116.2 0.0 collective-permute-start.29
  116.3 4.3 %collective-permute-done.31.refs_1_ = bf16[2,4,128,128]{3,2,1,0:T(8,128)(2,1)S(1)} collective-permute-done((bf16[2,4,128,128]{3,2,1,0:T(8,128)(2,1)S(1)}, bf16[2,4,128,128]{3,2,1,0:T(8,128)(2,1)S(1)}, u32[]{:S(2)}, u32[]{:S(2)}) %collective-permute-start.31) | collective-permute-done | bytes 262176 | tf_op jit(solution)/shard_map/ppermute | solution.py:67
  120.6 9.0 %collective-permute-done.32.refs_2_ = bf16[2,4,128,128]{3,2,1,0:T(8,128)(2,1)S(1)} collective-permute-done((bf16[2,4,128,128]{3,2,1,0:T(8,128)(2,1)S(1)}, bf16[2,4,128,128]{3,2,1,0:T(8,128)(2,1)S(1)}, u32[]{:S(2)}, u32[]{:S(2)}) %collective-permute-start.32) | collective-permute-done | bytes 262176 | tf_op jit(solution)/shard_map/ppermute | solution.py:67
  129.6 1.7 %assemble.3 = (bf16[512,512]{1,0:T(8,128)(2,1)}, bf16[512,512]{1,0:T(8,128)(2,1)}) custom-call(s32[3]{0:T(128)S(1)} %pad_add_fusion.ids, bf16[2,4,128,128]{3,2,1,0:T(8,128)(2,1)S(1)} %get-tuple-element.61.refs_0_, bf16[2,4,128,128]{3,2,1,0:T(8,128)(2,1)S(1)} %collective-permute-done.31.refs_1_, bf16[2,4,128,128]{3,2,1,0:T(8,128)(2,1)S(1)} %collective-permute-done.32.refs_2_, ...), custom_call_target="tpu_custom_call" | custom-call | bytes 7000000 | tf_op jit(solution)/shard_map/assemble/pallas_call | solution.py:417
  131.2 0.0 collective-permute-done.29
  131.3 1.4 %assemble.2 = bf16[512,512]{1,0:T(8,128)(2,1)} custom-call(s32[3]{0:T(128)S(1)} %pad_add_fusion.ids, bf16[1,4,128,128]{3,2,1,0:T(8,128)(2,1)S(1)} %bitcast.7, bf16[1,4,128,128]{3,2,1,0:T(8,128)(2,1)S(1)} %bitcast.8, bf16[1,4,128,128]{3,2,1,0:T(8,128)(2,1)S(1)} %bitcast.9, bf16[1,4,128,128]{3,2,1,0:T(8,128)(2,1)S(1)} %bitcast.10), custom_call_target="tpu_custom_call" | custom-call | bytes 7000000 | tf_op jit(solution)/shard_map/assemble/pallas_call | solution.py:417
  (106 shorter events, 1.0 us)
Async XLA Ops:
  0.7 1.0 copy-start
  1.8 5.2 %copy-start.1 = (bf16[128,2048]{1,0:T(8,128)(2,1)S(1)}, bf16[128,2048]{1,0:T(8,128)(2,1)}, u32[]{:S(2)}) copy-start(bf16[128,2048]{1,0:T(8,128)(2,1)} %x_ref.4) | copy-start | bytes 1572868
  1.8 7.9 %copy-start.6 = (s32[8,4,4]{0,2,1:T(4,128)S(1)}, s32[8,4,4]{0,2,1:T(4,128)}, u32[]{:S(2)}) copy-start(s32[8,4,4]{0,2,1:T(4,128)} %param.13) | copy-start | bytes 1540
  2.5 17.1 %collective-permute-start = (bf16[4,128,128]{2,1,0:T(8,128)(2,1)S(1)}, bf16[4,128,128]{2,1,0:T(8,128)(2,1)S(1)}, u32[]{:S(2)}, u32[]{:S(2)}) collective-permute-start(bf16[4,128,128]{2,1,0:T(8,128)(2,1)S(1)} %get-tuple-element.38), channel_id=1, source_target_pairs={{0,8},{8,0},{16,24},{24,16},{1,9},{9,1},{17,25},{25,17},{2,10},{10... | collective-permute-start | bytes 393224 | tf_op jit(solution)/shard_map/ppermute | solution.py:62
  4.1 17.0 %collective-permute-start.1 = (bf16[4,128,128]{2,1,0:T(8,128)(2,1)S(1)}, bf16[4,128,128]{2,1,0:T(8,128)(2,1)S(1)}, u32[]{:S(2)}, u32[]{:S(2)}) collective-permute-start(bf16[4,128,128]{2,1,0:T(8,128)(2,1)S(1)} %get-tuple-element.39), channel_id=1, source_target_pairs={{0,16},{8,24},{16,0},{24,8},{1,17},{9,25},{17,1},{25,9},{2,18},{10... | collective-permute-start | bytes 393224 | tf_op jit(solution)/shard_map/ppermute | solution.py:62
  6.7 3.1 %copy-start.2 = (bf16[128,2048]{1,0:T(8,128)(2,1)S(1)}, bf16[128,2048]{1,0:T(8,128)(2,1)}, u32[]{:S(2)}) copy-start(bf16[128,2048]{1,0:T(8,128)(2,1)} %x_ref.5) | copy-start | bytes 1572868
  6.7 20.6 %collective-permute-start.2 = (bf16[4,128,128]{2,1,0:T(8,128)(2,1)S(1)}, bf16[4,128,128]{2,1,0:T(8,128)(2,1)S(1)}, u32[]{:S(2)}, u32[]{:S(2)}) collective-permute-start(bf16[4,128,128]{2,1,0:T(8,128)(2,1)S(1)} %get-tuple-element.40), channel_id=1, source_target_pairs={{0,24},{8,16},{16,8},{24,0},{1,25},{9,17},{17,9},{25,1},{2,26},{10... | collective-permute-start | bytes 393224 | tf_op jit(solution)/shard_map/ppermute | solution.py:62
  7.6 15.1 %collective-permute-start.14 = (bf16[4,128,128]{2,1,0:T(8,128)(2,1)S(1)}, bf16[4,128,128]{2,1,0:T(8,128)(2,1)S(1)}, u32[]{:S(2)}, u32[]{:S(2)}) collective-permute-start(bf16[4,128,128]{2,1,0:T(8,128)(2,1)S(1)} %get-tuple-element.48), channel_id=1, source_target_pairs={{0,2},{1,3},{2,0},{3,1},{4,6},{5,7},{6,4},{7,5},{8,10},{9,11},{10,... | collective-permute-start | bytes 393224 | tf_op jit(solution)/shard_map/ppermute | solution.py:67
  9.2 14.1 %collective-permute-start.15 = (bf16[4,128,128]{2,1,0:T(8,128)(2,1)S(1)}, bf16[4,128,128]{2,1,0:T(8,128)(2,1)S(1)}, u32[]{:S(2)}, u32[]{:S(2)}) collective-permute-start(bf16[4,128,128]{2,1,0:T(8,128)(2,1)S(1)} %get-tuple-element.49), channel_id=1, source_target_pairs={{0,4},{1,5},{2,6},{3,7},{4,0},{5,1},{6,2},{7,3},{8,12},{9,13},{10,... | collective-permute-start | bytes 393224 | tf_op jit(solution)/shard_map/ppermute | solution.py:67
  9.8 1.0 copy-start.3
  9.8 1.2 copy-start.4
  12.2 0.7 copy-start.5
  19.6 7.4 %collective-permute-start.16 = (bf16[4,128,128]{2,1,0:T(8,128)(2,1)S(1)}, bf16[4,128,128]{2,1,0:T(8,128)(2,1)S(1)}, u32[]{:S(2)}, u32[]{:S(2)}) collective-permute-start(bf16[4,128,128]{2,1,0:T(8,128)(2,1)S(1)} %get-tuple-element.50), channel_id=1, source_target_pairs={{0,6},{1,7},{2,4},{3,5},{4,2},{5,3},{6,0},{7,1},{8,14},{9,15},{10,... | collective-permute-start | bytes 393224 | tf_op jit(solution)/shard_map/ppermute | solution.py:67
  21.1 8.6 %collective-permute-start.21 = (bf16[4,128,128]{2,1,0:T(8,128)(2,1)S(1)}, bf16[4,128,128]{2,1,0:T(8,128)(2,1)S(1)}, u32[]{:S(2)}, u32[]{:S(2)}) collective-permute-start(bf16[4,128,128]{2,1,0:T(8,128)(2,1)S(1)} %get-tuple-element.52), channel_id=1, source_target_pairs={{0,2},{1,3},{2,0},{3,1},{4,6},{5,7},{6,4},{7,5},{8,10},{9,11},{10,... | collective-permute-start | bytes 393224 | tf_op jit(solution)/shard_map/ppermute | solution.py:67
  22.7 8.0 %collective-permute-start.22 = (bf16[4,128,128]{2,1,0:T(8,128)(2,1)S(1)}, bf16[4,128,128]{2,1,0:T(8,128)(2,1)S(1)}, u32[]{:S(2)}, u32[]{:S(2)}) collective-permute-start(bf16[4,128,128]{2,1,0:T(8,128)(2,1)S(1)} %get-tuple-element.53), channel_id=1, source_target_pairs={{0,4},{1,5},{2,6},{3,7},{4,0},{5,1},{6,2},{7,3},{8,12},{9,13},{10,... | collective-permute-start | bytes 393224 | tf_op jit(solution)/shard_map/ppermute | solution.py:67
  23.3 9.3 %collective-permute-start.23 = (bf16[4,128,128]{2,1,0:T(8,128)(2,1)S(1)}, bf16[4,128,128]{2,1,0:T(8,128)(2,1)S(1)}, u32[]{:S(2)}, u32[]{:S(2)}) collective-permute-start(bf16[4,128,128]{2,1,0:T(8,128)(2,1)S(1)} %get-tuple-element.54), channel_id=1, source_target_pairs={{0,6},{1,7},{2,4},{3,5},{4,2},{5,3},{6,0},{7,1},{8,14},{9,15},{10,... | collective-permute-start | bytes 393224 | tf_op jit(solution)/shard_map/ppermute | solution.py:67
  27.0 8.6 %collective-permute-start.7 = (bf16[4,136,128]{2,1,0:T(8,128)(2,1)S(1)}, bf16[4,136,128]{2,1,0:T(8,128)(2,1)S(1)}, u32[]{:S(2)}, u32[]{:S(2)}) collective-permute-start(bf16[4,136,128]{2,1,0:T(8,128)(2,1)S(1)} %get-tuple-element.42), channel_id=1, source_target_pairs={{0,2},{1,3},{2,0},{3,1},{4,6},{5,7},{6,4},{7,5},{8,10},{9,11},{10,... | collective-permute-start | bytes 417800 | tf_op jit(solution)/shard_map/ppermute | solution.py:67
  27.3 11.5 %collective-permute-start.8 = (bf16[4,136,128]{2,1,0:T(8,128)(2,1)S(1)}, bf16[4,136,128]{2,1,0:T(8,128)(2,1)S(1)}, u32[]{:S(2)}, u32[]{:S(2)}) collective-permute-start(bf16[4,136,128]{2,1,0:T(8,128)(2,1)S(1)} %get-tuple-element.43), channel_id=1, source_target_pairs={{0,4},{1,5},{2,6},{3,7},{4,0},{5,1},{6,2},{7,3},{8,12},{9,13},{10,... | collective-permute-start | bytes 417800 | tf_op jit(solution)/shard_map/ppermute | solution.py:67
  29.8 9.7 %collective-permute-start.9 = (bf16[4,136,128]{2,1,0:T(8,128)(2,1)S(1)}, bf16[4,136,128]{2,1,0:T(8,128)(2,1)S(1)}, u32[]{:S(2)}, u32[]{:S(2)}) collective-permute-start(bf16[4,136,128]{2,1,0:T(8,128)(2,1)S(1)} %get-tuple-element.44), channel_id=1, source_target_pairs={{0,6},{1,7},{2,4},{3,5},{4,2},{5,3},{6,0},{7,1},{8,14},{9,15},{10,... | collective-permute-start | bytes 417800 | tf_op jit(solution)/shard_map/ppermute | solution.py:67
  30.8 31.0 %collective-permute-start.3 = (bf16[4,128,128]{2,1,0:T(8,128)(2,1)S(1)}, bf16[4,128,128]{2,1,0:T(8,128)(2,1)S(1)}, u32[]{:S(2)}, u32[]{:S(2)}) collective-permute-start(bf16[4,128,128]{2,1,0:T(8,128)(2,1)S(1)} %pad_maximum_fusion.3), channel_id=1, source_target_pairs={{0,2},{1,3},{2,0},{3,1},{4,6},{5,7},{6,4},{7,5},{8,10},{9,11},{10,... | collective-permute-start | bytes 393224 | tf_op jit(solution)/shard_map/ppermute | solution.py:67
  32.6 29.2 %collective-permute-start.4 = (bf16[4,128,128]{2,1,0:T(8,128)(2,1)S(1)}, bf16[4,128,128]{2,1,0:T(8,128)(2,1)S(1)}, u32[]{:S(2)}, u32[]{:S(2)}) collective-permute-start(bf16[4,128,128]{2,1,0:T(8,128)(2,1)S(1)} %pad_maximum_fusion.4), channel_id=1, source_target_pairs={{0,4},{1,5},{2,6},{3,7},{4,0},{5,1},{6,2},{7,3},{8,12},{9,13},{10,... | collective-permute-start | bytes 393224 | tf_op jit(solution)/shard_map/ppermute | solution.py:67
  35.6 28.2 %collective-permute-start.5 = (bf16[4,128,128]{2,1,0:T(8,128)(2,1)S(1)}, bf16[4,128,128]{2,1,0:T(8,128)(2,1)S(1)}, u32[]{:S(2)}, u32[]{:S(2)}) collective-permute-start(bf16[4,128,128]{2,1,0:T(8,128)(2,1)S(1)} %pad_maximum_fusion.5), channel_id=1, source_target_pairs={{0,6},{1,7},{2,4},{3,5},{4,2},{5,3},{6,0},{7,1},{8,14},{9,15},{10,... | collective-permute-start | bytes 393224 | tf_op jit(solution)/shard_map/ppermute | solution.py:67
  38.8 7.9 %collective-permute-start.17 = (bf16[4,128,128]{2,1,0:T(8,128)(2,1)S(1)}, bf16[4,128,128]{2,1,0:T(8,128)(2,1)S(1)}, u32[]{:S(2)}, u32[]{:S(2)}) collective-permute-start(bf16[4,128,128]{2,1,0:T(8,128)(2,1)S(1)} %pad_maximum_fusion.6), channel_id=1, source_target_pairs={{0,8},{8,0},{16,24},{24,16},{1,9},{9,1},{17,25},{25,17},{2,10},{10... | collective-permute-start | bytes 393224 | tf_op jit(solution)/shard_map/ppermute | solution.py:62
  39.5 12.0 %collective-permute-start.18 = (bf16[4,128,128]{2,1,0:T(8,128)(2,1)S(1)}, bf16[4,128,128]{2,1,0:T(8,128)(2,1)S(1)}, u32[]{:S(2)}, u32[]{:S(2)}) collective-permute-start(bf16[4,128,128]{2,1,0:T(8,128)(2,1)S(1)} %pad_maximum_fusion.7), channel_id=1, source_target_pairs={{0,16},{8,24},{16,0},{24,8},{1,17},{9,25},{17,1},{25,9},{2,18},{10... | collective-permute-start | bytes 393224 | tf_op jit(solution)/shard_map/ppermute | solution.py:62
  46.7 9.1 %collective-permute-start.19 = (bf16[4,128,128]{2,1,0:T(8,128)(2,1)S(1)}, bf16[4,128,128]{2,1,0:T(8,128)(2,1)S(1)}, u32[]{:S(2)}, u32[]{:S(2)}) collective-permute-start(bf16[4,128,128]{2,1,0:T(8,128)(2,1)S(1)} %pad_maximum_fusion.8), channel_id=1, source_target_pairs={{0,24},{8,16},{16,8},{24,0},{1,25},{9,17},{17,9},{25,1},{2,26},{10... | collective-permute-start | bytes 393224 | tf_op jit(solution)/shard_map/ppermute | solution.py:62
  51.5 7.7 %collective-permute-start.24 = (bf16[4,128,128]{2,1,0:T(8,128)(2,1)S(1)}, bf16[4,128,128]{2,1,0:T(8,128)(2,1)S(1)}, u32[]{:S(2)}, u32[]{:S(2)}) collective-permute-start(bf16[4,128,128]{2,1,0:T(8,128)(2,1)S(1)} %pad_maximum_fusion.9), channel_id=1, source_target_pairs={{0,8},{8,0},{16,24},{24,16},{1,9},{9,1},{17,25},{25,17},{2,10},{10... | collective-permute-start | bytes 393224 | tf_op jit(solution)/shard_map/ppermute | solution.py:62
  55.9 11.0 %collective-permute-start.25 = (bf16[4,128,128]{2,1,0:T(8,128)(2,1)S(1)}, bf16[4,128,128]{2,1,0:T(8,128)(2,1)S(1)}, u32[]{:S(2)}, u32[]{:S(2)}) collective-permute-start(bf16[4,128,128]{2,1,0:T(8,128)(2,1)S(1)} %pad_maximum_fusion.10), channel_id=1, source_target_pairs={{0,16},{8,24},{16,0},{24,8},{1,17},{9,25},{17,1},{25,9},{2,18},{10... | collective-permute-start | bytes 393224 | tf_op jit(solution)/shard_map/ppermute | solution.py:62
  59.2 7.7 %collective-permute-start.26 = (bf16[4,128,128]{2,1,0:T(8,128)(2,1)S(1)}, bf16[4,128,128]{2,1,0:T(8,128)(2,1)S(1)}, u32[]{:S(2)}, u32[]{:S(2)}) collective-permute-start(bf16[4,128,128]{2,1,0:T(8,128)(2,1)S(1)} %pad_maximum_fusion.11), channel_id=1, source_target_pairs={{0,24},{8,16},{16,8},{24,0},{1,25},{9,17},{17,9},{25,1},{2,26},{10... | collective-permute-start | bytes 393224 | tf_op jit(solution)/shard_map/ppermute | solution.py:62
  61.8 6.2 %collective-permute-start.10 = (bf16[4,136,128]{2,1,0:T(8,128)(2,1)S(1)}, bf16[4,136,128]{2,1,0:T(8,128)(2,1)S(1)}, u32[]{:S(2)}, u32[]{:S(2)}) collective-permute-start(bf16[4,136,128]{2,1,0:T(8,128)(2,1)S(1)} %pad_maximum_fusion), channel_id=1, source_target_pairs={{0,8},{8,0},{16,24},{24,16},{1,9},{9,1},{17,25},{25,17},{2,10},{10... | collective-permute-start | bytes 417800 | tf_op jit(solution)/shard_map/ppermute | solution.py:62
  61.9 11.5 %collective-permute-start.11 = (bf16[4,136,128]{2,1,0:T(8,128)(2,1)S(1)}, bf16[4,136,128]{2,1,0:T(8,128)(2,1)S(1)}, u32[]{:S(2)}, u32[]{:S(2)}) collective-permute-start(bf16[4,136,128]{2,1,0:T(8,128)(2,1)S(1)} %pad_maximum_fusion.1), channel_id=1, source_target_pairs={{0,16},{8,24},{16,0},{24,8},{1,17},{9,25},{17,1},{25,9},{2,18},{10... | collective-permute-start | bytes 417800 | tf_op jit(solution)/shard_map/ppermute | solution.py:62
  63.8 9.6 %collective-permute-start.12 = (bf16[4,136,128]{2,1,0:T(8,128)(2,1)S(1)}, bf16[4,136,128]{2,1,0:T(8,128)(2,1)S(1)}, u32[]{:S(2)}, u32[]{:S(2)}) collective-permute-start(bf16[4,136,128]{2,1,0:T(8,128)(2,1)S(1)} %pad_maximum_fusion.2), channel_id=1, source_target_pairs={{0,24},{8,16},{16,8},{24,0},{1,25},{9,17},{17,9},{25,1},{2,26},{10... | collective-permute-start | bytes 417800 | tf_op jit(solution)/shard_map/ppermute | solution.py:62
  66.9 6.8 %collective-permute-start.6 = (bf16[16,128,128]{2,1,0:T(8,128)(2,1)S(1)}, bf16[16,128,128]{2,1,0:T(8,128)(2,1)S(1)}, u32[]{:S(2)}, u32[]{:S(2)}) collective-permute-start(bf16[16,128,128]{2,1,0:T(8,128)(2,1)S(1)} %constant_dynamic-update-slice_fusion.refs_0_), channel_id=1, source_target_pairs={{0,1},{1,0},{2,3},{3,2},{4,5},{5,4},{6,7},{7,6},{8,9},{9,8},{10,11... | collective-permute-start | bytes 1572872 | tf_op jit(solution)/shard_map/ppermute | solution.py:67
  73.6 9.1 %collective-permute-start.13 = (bf16[16,136,128]{2,1,0:T(8,128)(2,1)S(1)}, bf16[16,136,128]{2,1,0:T(8,128)(2,1)S(1)}, u32[]{:S(2)}, u32[]{:S(2)}) collective-permute-start(bf16[16,136,128]{2,1,0:T(8,128)(2,1)S(1)} %constant_dynamic-update-slice_fusion.7.refs_2_), channel_id=1, source_target_pairs={{0,1},{1,0},{2,3},{3,2},{4,5},{5,4},{6,7},{7,6},{8,9},{9,8},{10,11... | collective-permute-start | bytes 1671176 | tf_op jit(solution)/shard_map/ppermute | solution.py:67
  81.3 1.4 %collective-permute-start.20 = (f32[32,128]{1,0:T(8,128)S(1)}, f32[32,128]{1,0:T(8,128)S(1)}, u32[]{:S(2)}, u32[]{:S(2)}) collective-permute-start(f32[32,128]{1,0:T(8,128)S(1)} %totals.1.refs_4_), channel_id=1, source_target_pairs={{0,1},{1,0},{2,3},{3,2},{4,5},{5,4},{6,7},{7,6},{8,9},{9,8},{10,11... | collective-permute-start | bytes 49160 | tf_op jit(solution)/shard_map/ppermute | solution.py:67
  111.0 3.9 %collective-permute-start.27 = (f32[16,128,128]{2,1,0:T(8,128)S(1)}, f32[16,128,128]{2,1,0:T(8,128)S(1)}, u32[]{:S(2)}, u32[]{:S(2)}) collective-permute-start(f32[16,128,128]{2,1,0:T(8,128)S(1)} %get-tuple-element.56), channel_id=1, source_target_pairs={{0,1},{1,0},{2,3},{3,2},{4,5},{5,4},{6,7},{7,6},{8,9},{9,8},{10,11... | collective-permute-start | bytes 3145736 | tf_op jit(solution)/shard_map/ppermute | solution.py:67
  111.4 9.2 %collective-permute-start.31 = (bf16[2,4,128,128]{3,2,1,0:T(8,128)(2,1)S(1)}, bf16[2,4,128,128]{3,2,1,0:T(8,128)(2,1)S(1)}, u32[]{:S(2)}, u32[]{:S(2)}) collective-permute-start(bf16[2,4,128,128]{3,2,1,0:T(8,128)(2,1)S(1)} %get-tuple-element.62), channel_id=1, source_target_pairs={{0,2},{1,3},{2,0},{3,1},{4,6},{5,7},{6,4},{7,5},{8,10},{9,11},{10,... | collective-permute-start | bytes 786440 | tf_op jit(solution)/shard_map/ppermute | solution.py:67
  112.0 17.6 %collective-permute-start.32 = (bf16[2,4,128,128]{3,2,1,0:T(8,128)(2,1)S(1)}, bf16[2,4,128,128]{3,2,1,0:T(8,128)(2,1)S(1)}, u32[]{:S(2)}, u32[]{:S(2)}) collective-permute-start(bf16[2,4,128,128]{3,2,1,0:T(8,128)(2,1)S(1)} %get-tuple-element.63), channel_id=1, source_target_pairs={{0,4},{1,5},{2,6},{3,7},{4,0},{5,1},{6,2},{7,3},{8,12},{9,13},{10,... | collective-permute-start | bytes 786440 | tf_op jit(solution)/shard_map/ppermute | solution.py:67
  112.0 17.6 %collective-permute-start.33 = (bf16[2,4,128,128]{3,2,1,0:T(8,128)(2,1)S(1)}, bf16[2,4,128,128]{3,2,1,0:T(8,128)(2,1)S(1)}, u32[]{:S(2)}, u32[]{:S(2)}) collective-permute-start(bf16[2,4,128,128]{3,2,1,0:T(8,128)(2,1)S(1)} %get-tuple-element.64), channel_id=1, source_target_pairs={{0,6},{1,7},{2,4},{3,5},{4,2},{5,3},{6,0},{7,1},{8,14},{9,15},{10,... | collective-permute-start | bytes 786440 | tf_op jit(solution)/shard_map/ppermute | solution.py:67
  115.6 15.6 %collective-permute-start.28 = (bf16[4,128,128]{2,1,0:T(8,128)(2,1)S(1)}, bf16[4,128,128]{2,1,0:T(8,128)(2,1)S(1)}, u32[]{:S(2)}, u32[]{:S(2)}) collective-permute-start(bf16[4,128,128]{2,1,0:T(8,128)(2,1)S(1)} %get-tuple-element.58), channel_id=1, source_target_pairs={{0,2},{1,3},{2,0},{3,1},{4,6},{5,7},{6,4},{7,5},{8,10},{9,11},{10,... | collective-permute-start | bytes 393224 | tf_op jit(solution)/shard_map/ppermute | solution.py:67
  116.2 15.0 %collective-permute-start.29 = (bf16[4,128,128]{2,1,0:T(8,128)(2,1)S(1)}, bf16[4,128,128]{2,1,0:T(8,128)(2,1)S(1)}, u32[]{:S(2)}, u32[]{:S(2)}) collective-permute-start(bf16[4,128,128]{2,1,0:T(8,128)(2,1)S(1)} %get-tuple-element.59), channel_id=1, source_target_pairs={{0,4},{1,5},{2,6},{3,7},{4,0},{5,1},{6,2},{7,3},{8,12},{9,13},{10,... | collective-permute-start | bytes 393224 | tf_op jit(solution)/shard_map/ppermute | solution.py:67
  120.6 10.7 %collective-permute-start.30 = (bf16[4,128,128]{2,1,0:T(8,128)(2,1)S(1)}, bf16[4,128,128]{2,1,0:T(8,128)(2,1)S(1)}, u32[]{:S(2)}, u32[]{:S(2)}) collective-permute-start(bf16[4,128,128]{2,1,0:T(8,128)(2,1)S(1)} %get-tuple-element.60), channel_id=1, source_target_pairs={{0,6},{1,7},{2,4},{3,5},{4,2},{5,3},{6,0},{7,1},{8,14},{9,15},{10,... | collective-permute-start | bytes 393224 | tf_op jit(solution)/shard_map/ppermute | solution.py:67
where the time goes:
time: 135 us; the launch traced here: 133 us
  Pallas kernels  49.6 us (37%)
  starting transfers between devices  41.9 us (31%)
  waiting for transfers between devices  36.7 us (27%)
  local copies, waits for them, and re-layouts  2.94 us (2%)
    pallas_call x1, Pallas kernels, grads(): pl.pallas_call(functools.partial(grads_kernel, plan), out_shape=[sds((2,...  28.3 us
    ppermute x12, starting transfers between devices, over_head(): return lax.ppermute(value, 'head', [(i, i ^ step) for i in range(count)])  23.5 us
    ppermute x22, waiting for transfers between devices, over_frame(): return lax.ppermute(value, 'frame', [(i, i ^ step) for i in range(count)])  21.8 us
    ppermute x22, starting transfers between devices, over_frame(): return lax.ppermute(value, 'frame', [(i, i ^ step) for i in range(count)])  18.4 us
    ppermute x12, waiting for transfers between devices, over_head(): return lax.ppermute(value, 'head', [(i, i ^ step) for i in range(count)])  14.9 us
    pallas_call x1, Pallas kernels, totals(): pl.pallas_call(functools.partial(totals_kernel, plan), out_shape=sds((pla...  7.58 us
    pallas_call x1, Pallas kernels, lists(): pl.pallas_call(functools.partial(lists_kernel, plan), out_shape=[sds((own...  6.63 us
    pallas_call x2, Pallas kernels, assemble(): pl.pallas_call(functools.partial(assemble_kernel, plan, n), out_shape=[sd...  3.11 us
  transfers between devices with their start and end apart: 34, of which 14 were waited for; matrix products, arithmetic and copies ran while one was open for 1% of the time, Pallas kernels for 14%

commit v1 on v0

v1 whole, which is shorter than its diff:
```python
import functools
import math

import jax
import jax.numpy as jnp
from jax import lax
from jax.experimental import pallas as pl
from jax.experimental.pallas import tpu as pltpu
from jax.sharding import PartitionSpec as P


HEADS = 16
HEAD_DIM = 128
NEG = -1e30
KEY_GROUP = 6
QUERY_GROUP = 4
TOGETHER = 2
EXTRA = 8


VMEM = pl.BlockSpec(memory_space=pltpu.VMEM)
SMEM = pl.BlockSpec(memory_space=pltpu.SMEM)
F32 = jnp.float32
BF16 = jnp.bfloat16
NT = (((1,), (1,)), ((), ()))
TN = (((0,), (0,)), ((), ()))
NN = (((1,), (0,)), ((), ()))


def dot(a, b, dims):
    return lax.dot_general(a, b, dims, preferred_element_type=F32)


def sds(shape, dtype):
    return jax.ShapeDtypeStruct(shape, dtype)


def lasts(microseconds):
    return pl.CostEstimate(flops=0, bytes_accessed=int(microseconds * 3.5e6), transcendentals=0)


def within(*shapes):
    held = sum(math.prod(s.shape) * s.dtype.itemsize for s in shapes)
    return pltpu.CompilerParams(vmem_limit_bytes=int(held * 5 // 4) + (6 << 20))


class Plan:
    def __init__(self, rows):
        self.nz = lax.axis_size("head")
        self.nf = lax.axis_size("frame")
        self.hh = HEADS // self.nz
        self.na = min(self.hh, self.nf)
        self.nb = self.nf // self.na
        self.rows = rows
        self.own = self.na * self.nz
        self.total = self.own * self.nb
        assert self.hh == self.na and rows == HEAD_DIM


def over_head(value, step):
    count = lax.axis_size("head")
    return lax.ppermute(value, "head", [(i, i ^ step) for i in range(count)])


def over_frame(value, step):
    count = lax.axis_size("frame")
    return lax.ppermute(value, "frame", [(i, i ^ step) for i in range(count)])


def prep_kernel(plan, head_first, ids, x_ref, *outs):
    hd = HEAD_DIM
    z, a = ids[0], ids[1]
    for p, out in enumerate(outs):
        for c in range(out.shape[0]):
            r, s = (p, c) if head_first else (c, p)
            head = (z ^ r) * plan.hh + (a ^ s)
            out[c] = x_ref[:, pl.ds(pl.multiple_of(head * hd, hd), hd)]


def prep(plan, ids, x, head_first):
    pieces, chunk = (plan.nz, plan.na) if head_first else (plan.na, plan.nz)
    return pl.pallas_call(
        functools.partial(prep_kernel, plan, head_first),
        out_shape=[sds((chunk, plan.rows, HEAD_DIM), BF16)] * pieces,
        in_specs=[SMEM, VMEM],
        out_specs=[VMEM] * pieces,
        cost_estimate=lasts(2),
        compiler_params=within(x, x),
    )(ids, x)


def prep_grad_kernel(plan, ids, g_ref, o_ref, *outs):
    hd, rows = HEAD_DIM, plan.rows
    z, a = ids[0], ids[1]
    ones = jnp.ones((EXTRA, hd), BF16)
    row = lax.broadcasted_iota(jnp.int32, (EXTRA, rows), 0)
    for s, out in enumerate(outs):
        for r in range(plan.nz):
            head = (z ^ r) * plan.hh + (a ^ s)
            cols = pl.ds(pl.multiple_of(head * hd, hd), hd)
            grad = g_ref[:, cols]
            out[r, :rows] = grad
            product = grad.astype(F32) * o_ref[:, cols].astype(F32)
            high = product.astype(BF16)
            low = (product - high.astype(F32)).astype(BF16)
            delta = dot(ones, high, NT) + dot(ones, low, NT)
            first = delta.astype(BF16)
            rest = delta - first.astype(F32)
            second = rest.astype(BF16)
            third = (rest - second.astype(F32)).astype(BF16)
            parts = jnp.where(
                row == 0,
                first.astype(F32),
                jnp.where(row == 1, second.astype(F32), jnp.where(row == 2, third.astype(F32), 0.0)),
            )
            out[r, rows:] = parts.astype(BF16)


def prep_grad(plan, ids, g, o):
    return pl.pallas_call(
        functools.partial(prep_grad_kernel, plan),
        out_shape=[sds((plan.nz, plan.rows + EXTRA, HEAD_DIM), BF16)] * plan.na,
        in_specs=[SMEM, VMEM, VMEM],
        out_specs=[VMEM] * plan.na,
        cost_estimate=lasts(2.5),
        compiler_params=within(g, o, g),
        name="prep_grad",
    )(ids, g, o)


def lists_kernel(plan, ids, order, live_ref, by_key, n_key, by_query, n_query, key_of, query_of, numbers):
    nz, na, nb, nf = plan.nz, plan.na, plan.nb, plan.nf
    z, a, b = ids[0], ids[1], ids[2]
    true = [z ^ r for r in range(nz)]

    def at_distance(d, carry):
        seen = [jnp.int32(0)] * nz
        for r in range(nz):
            count = jnp.int32(0)
            for rk in range(nz):
                live = (live_ref[d, true[r], true[rk]] > 0).astype(jnp.int32)
                key_of[d * nz + r, count] = jnp.int32(rk)
                query_of[d * nz + rk, seen[rk]] = jnp.int32(r)
                count = count + live
                seen[rk] = seen[rk] + live
            numbers[0, d * nz + r] = count
        for rk in range(nz):
            numbers[1, d * nz + rk] = seen[rk]
        return carry

    lax.fori_loop(0, nf, at_distance, 0)

    def clear(i, carry):
        n_query[i] = 0
        return carry

    lax.fori_loop(0, plan.total, clear, 0)

    def key_frame(s_key, carry):
        place_key = order[(a ^ s_key) * nb + b]

        def query_frame(ts, counts):
            t = ts // na
            place = order[(a ^ (ts - t * na)) * nb + (b ^ t)]
            d = jnp.abs(place - place_key)

            def found(counts):
                counts = list(counts)
                for r in range(nz):
                    i, row = ts * nz + r, d * nz + r
                    seen = n_query[i]
                    for u in range(nz):
                        by_query[i, seen + u] = s_key * nz + key_of[row, u]
                    n_query[i] = seen + numbers[0, row]
                for rk in range(nz):
                    row = d * nz + rk
                    for u in range(nz):
                        by_key[s_key * nz + rk, counts[rk] + u] = ts * nz + query_of[row, u]
                    counts[rk] = counts[rk] + numbers[1, row]
                return tuple(counts)

            return lax.cond(ts != s_key, found, lambda counts: counts, counts)

        counts = lax.fori_loop(0, na * nb, query_frame, (jnp.int32(0),) * nz)
        for rk in range(nz):
            n_key[s_key * nz + rk] = counts[rk]
        return carry

    lax.fori_loop(0, na, key_frame, 0)


def lists(plan, ids, order, live):
    own, total, nz, nf = plan.own, plan.total, plan.nz, plan.nf
    return pl.pallas_call(
        functools.partial(lists_kernel, plan),
        out_shape=[
            sds((own, total + KEY_GROUP + nz), jnp.int32),
            sds((own,), jnp.int32),
            sds((total, own + QUERY_GROUP + nz), jnp.int32),
            sds((total,), jnp.int32),
        ],
        in_specs=[SMEM] * 3,
        out_specs=[SMEM] * 4,
        scratch_shapes=[
            pltpu.SMEM((nf * nz, nz), jnp.int32),
            pltpu.SMEM((nf * nz, nz), jnp.int32),
            pltpu.SMEM((2, nf * nz), jnp.int32),
        ],
        cost_estimate=lasts(3),
        compiler_params=within(),
        name="lists",
    )(ids, order, live)


def picks(table, row, count, first, size):
    out = []
    for u in range(size):
        valid = first + u < count
        out.append((jnp.where(valid, table[row, first + u], 0), valid))
    return out


def totals_kernel(plan, by_query, n_query, k_ref, q_ref, out, peaks, sums):
    nz, na, nb, own, rows = plan.nz, plan.na, plan.nb, plan.own, plan.rows
    scale = HEAD_DIM**-0.5
    length = nz * rows

    def scores_of(i, first):
        chosen = picks(by_query, i, n_query[i], first, QUERY_GROUP)
        keys = jnp.concatenate([k_ref[j] for j, _ in chosen], axis=0)
        scores = scale * dot(keys, q_ref[i], NT)
        return [
            jnp.where(valid, scores[u * rows : (u + 1) * rows], NEG)
            for u, (_, valid) in enumerate(chosen)
        ]

    def near(s, carry):
        span = pl.ds(s * nz, nz)
        keys, q = k_ref[span].reshape(length, HEAD_DIM), q_ref[span].reshape(length, HEAD_DIM)
        scores = scale * dot(keys, q, NT)
        peak = jnp.max(scores, axis=0, keepdims=True)
        mass = jnp.sum(jnp.exp(scores - peak), axis=0, keepdims=True)
        for r in range(nz):
            peaks[pl.ds(s * nz + r, 1), :] = peak[:, r * rows : (r + 1) * rows]
            sums[pl.ds(s * nz + r, 1), :] = mass[:, r * rows : (r + 1) * rows]
        return carry

    lax.fori_loop(0, na, near, 0)
    if nb > 1:
        peaks[own:, :] = jnp.full((plan.total - own, rows), NEG, F32)
        sums[own:, :] = jnp.zeros((plan.total - own, rows), F32)

    def merged(i, parts):
        row = pl.ds(i, 1)
        old = peaks[row, :]
        peak = jnp.maximum(old, jnp.max(functools.reduce(jnp.maximum, parts), axis=0, keepdims=True))
        mass = functools.reduce(jnp.add, [jnp.exp(part - peak) for part in parts])
        fresh = sums[row, :] * jnp.exp(old - peak) + jnp.sum(mass, axis=0, keepdims=True)
        return peak, fresh

    def keep(i, found):
        peaks[pl.ds(i, 1), :], sums[pl.ds(i, 1), :] = found

    def away(m, carry):
        found = [(m * TOGETHER + u, merged(m * TOGETHER + u, scores_of(m * TOGETHER + u, 0))) for u in range(TOGETHER)]
        for i, each in found:
            keep(i, each)
        return carry

    lax.fori_loop(0, plan.total // TOGETHER, away, 0)

    def rest(i, carry):
        def group(step, carry):
            keep(i, merged(i, scores_of(i, step * QUERY_GROUP)))
            return carry

        return lax.fori_loop(1, lax.div(n_query[i] + (QUERY_GROUP - 1), QUERY_GROUP), group, carry)

    lax.fori_loop(0, plan.total, rest, 0)
    peak = peaks[...]
    out[...] = jnp.where(peak > 0.5 * NEG, peak + jnp.log(sums[...]), NEG)


def totals(plan, by_query, n_query, keys, queries):
    return pl.pallas_call(
        functools.partial(totals_kernel, plan),
        out_shape=sds((plan.total, plan.rows), F32),
        in_specs=[SMEM, SMEM, VMEM, VMEM],
        out_specs=VMEM,
        scratch_shapes=[pltpu.VMEM((plan.total, plan.rows), F32)] * 2,
        cost_estimate=lasts(7),
        compiler_params=within(keys, queries),
        name="totals",
    )(by_query, n_query, keys, queries)


def rows_kernel(plan, g_ref, *refs):
    nb, own, rows = plan.nb, plan.own, plan.rows
    parts, lse_all, delta_all = refs[:nb], refs[nb], refs[nb + 1]
    for t in range(nb):
        rivals = [parts[u][pl.ds((t ^ u) * own, own), :] for u in range(nb)]
        peak = functools.reduce(jnp.maximum, rivals)
        lse_all[pl.ds(t * own, own), :] = peak + jnp.log(sum(jnp.exp(x - peak) for x in rivals))

    def fill(i, carry):
        delta_all[pl.ds(i, 1), :] = jnp.sum(g_ref[i, rows:].astype(F32), axis=0, keepdims=True)
        return carry

    lax.fori_loop(0, plan.total, fill, 0)


def query_rows(plan, out_grads, parts):
    return pl.pallas_call(
        functools.partial(rows_kernel, plan),
        out_shape=[sds((plan.total, plan.rows), F32)] * 2,
        in_specs=[VMEM] * (1 + plan.nb),
        out_specs=[VMEM] * 2,
        cost_estimate=lasts(1),
        compiler_params=within(out_grads),
        name="query_rows",
    )(out_grads, *parts)


def grads_kernel(plan, span, first, last, by_key, n_key, q_ref, g_ref, lse_ref, delta_ref, k_ref, *refs):
    nz, na, nb, own, rows = plan.nz, plan.na, plan.nb, plan.own, plan.rows
    hd = HEAD_DIM
    scale = hd**-0.5
    length = nz * rows
    width = len(span)
    refs = list(refs)
    take = lambda n: [refs.pop(0) for _ in range(n)]
    v_refs = take(width)
    if not first:
        (dq_before,) = take(1)
    kv_outs = take(na)
    dq_outs = take(nb if last else 1)
    dk_all, dv_all = take(2)
    dq_all = refs.pop(0) if last else dq_outs[0]

    def begin(i, carry):
        dq_all[i] = jnp.zeros((rows, hd), F32) if first else dq_before[i]
        return carry

    lax.fori_loop(own if first else 0, plan.total, begin, 0)

    def wide_row(ref, start):
        return jnp.concatenate([ref[pl.ds(start + r, 1), :] for r in range(nz)], axis=1)

    def diagonal(s, carry):
        frame = pl.ds(s * nz, nz)
        k = jnp.concatenate([k_ref[s * nz + r] for r in span], axis=0)
        v = jnp.concatenate([v_ref[s] for v_ref in v_refs], axis=0)
        q, g = q_ref[frame].reshape(length, hd), g_ref[frame, :rows].reshape(length, hd)
        lse, delta = wide_row(lse_ref, s * nz), wide_row(delta_ref, s * nz)
        probs = jnp.exp(scale * dot(k, q, NT) - lse)
        dv = dot(probs.astype(BF16), g, NN)
        grad_scores = (probs * (dot(v, g, NT) - delta)).astype(BF16)
        dk = dot(grad_scores, q, NN)
        dq = dot(grad_scores, k, TN).reshape(nz, rows, hd)
        for x in range(width):
            dv_all[s * width + x] = dv[x * rows : (x + 1) * rows]
            dk_all[s * width + x] = dk[x * rows : (x + 1) * rows]
        if first:
            dq_all[frame] = dq
        else:
            dq_all[frame] += dq
        return carry

    lax.fori_loop(0, na, diagonal, 0)

    def add(s, x, j, start, size):
        k, v = k_ref[j], v_refs[x][s]
        chosen = picks(by_key, j, n_key[j], start, size)
        q = jnp.concatenate([q_ref[i] for i, _ in chosen], axis=0)
        g = jnp.concatenate([g_ref[i, :rows] for i, _ in chosen], axis=0)
        lse = jnp.concatenate([jnp.where(ok, lse_ref[pl.ds(i, 1), :], -NEG) for i, ok in chosen], axis=1)
        delta = jnp.concatenate([delta_ref[pl.ds(i, 1), :] for i, _ in chosen], axis=1)
        probs = jnp.exp(scale * dot(k, q, NT) - lse)
        dv_all[s * width + x] += dot(probs.astype(BF16), g, NN)
        grad_scores = (probs * (dot(v, g, NT) - delta)).astype(BF16)
        dk_all[s * width + x] += dot(grad_scores, q, NN)
        dq = dot(grad_scores, k, TN)
        for u, (i, _) in enumerate(chosen):
            dq_all[i] += dq[u * rows : (u + 1) * rows]

    def away(s, carry):
        for x, r in enumerate(span):
            j = s * nz + r
            count = n_key[j]
            full = lax.div(count, KEY_GROUP)

            def group(step, carry, x=x, j=j):
                add(s, x, j, step * KEY_GROUP, KEY_GROUP)
                return carry

            lax.fori_loop(0, full, group, 0)
            left = count - full * KEY_GROUP
            for size in range(2, KEY_GROUP + 1, 2):

                @pl.when((left > size - 2) & (left <= size))
                def _(x=x, j=j, full=full, size=size):
                    add(s, x, j, full * KEY_GROUP, size)

        return carry

    lax.fori_loop(0, na, away, 0)

    for s, out in enumerate(kv_outs):
        for x in range(width):
            out[0, x] = (scale * dk_all[s * width + x]).astype(BF16)
            out[1, x] = dv_all[s * width + x].astype(BF16)
    if last:
        for t in range(nb):

            def drain(m, carry, t=t):
                dq_outs[t][m] = scale * dq_all[t * own + m]
                return carry

            lax.fori_loop(0, own, drain, 0)


def grads(plan, span, tables, queries, out_grads, lse, delta, keys, values, dq_before, last):
    nb, na, own, rows, total = plan.nb, plan.na, plan.own, plan.rows, plan.total
    hd, width, first = HEAD_DIM, len(span), dq_before is None
    kv = [sds((2, width, rows, hd), BF16)] * na
    dq = [sds((own, rows, hd), F32)] * nb if last else [sds((total, rows, hd), F32)]
    before = [] if first else [dq_before]
    partial = sds((own, rows, hd), F32)
    outs = pl.pallas_call(
        functools.partial(grads_kernel, plan, span, first, last),
        out_shape=kv + dq,
        in_specs=[SMEM] * 2 + [VMEM] * (5 + width + len(before)),
        out_specs=[VMEM] * (na + len(dq)),
        scratch_shapes=[pltpu.VMEM((na * width, rows, hd), F32)] * 2
        + ([pltpu.VMEM((total, rows, hd), F32)] if last else []),
        cost_estimate=lasts(7),
        compiler_params=within(queries, out_grads, keys, keys, *[partial] * (4 + 3 * nb)),
    )(*tables, queries, out_grads, lse, delta, keys, *values, *before)
    return outs[:na], outs[na:]


def pack_kernel(plan, *refs):
    nb, nz = plan.nb, plan.nz
    for s, out in enumerate(refs[nb:]):
        for r in range(nz):
            out[0, r] = sum(ref[s * nz + r] for ref in refs[:nb]).astype(BF16)


def pack(plan, partials):
    return pl.pallas_call(
        functools.partial(pack_kernel, plan),
        out_shape=[sds((1, plan.nz, plan.rows, HEAD_DIM), BF16)] * plan.na,
        in_specs=[VMEM] * plan.nb,
        out_specs=[VMEM] * plan.na,
        cost_estimate=lasts(1),
        compiler_params=within(*partials, *partials),
        name="pack",
    )(*partials)


def assemble_kernel(plan, spans, n, ids, *refs):
    na, rows, hd = plan.na, plan.rows, HEAD_DIM
    refs = list(refs)
    outs = refs[na * len(spans) :]
    for span in spans:
        for s in range(na):
            piece = refs.pop(0)
            cols = pl.ds(pl.multiple_of((ids[1] ^ s) * hd, hd), hd)
            for w in range(n):
                for x, r in enumerate(span):
                    place = pl.ds(pl.multiple_of((ids[0] ^ r) * rows, rows), rows)
                    outs[w][place, cols] = piece[w, x]


def assemble(plan, ids, spans, groups):
    n = groups[0][0].shape[0]
    pieces = [piece for group in groups for piece in group]
    return pl.pallas_call(
        functools.partial(assemble_kernel, plan, spans, n),
        out_shape=[sds((plan.nz * plan.rows, plan.na * HEAD_DIM), BF16)] * n,
        in_specs=[SMEM] + [VMEM] * len(pieces),
        out_specs=[VMEM] * n,
        cost_estimate=lasts(1.5),
        compiler_params=within(*pieces, *pieces),
    )(ids, *pieces)


def local(queries, key_states, value_states, attn_out, grad_out, frame_order, block_live):
    plan = Plan(queries.shape[0])
    nz, na, nb = plan.nz, plan.na, plan.nb
    slot = lax.axis_index("frame")
    ids = jnp.stack([lax.axis_index("head"), slot // nb, slot % nb]).astype(jnp.int32)

    def staged(order, pieces, send):
        moved = {}
        for step in order:
            moved[step] = send(pieces[step], step)
        return [pieces[0]] + [moved[step] for step in range(1, len(pieces))]

    def head_stage(pieces):
        return staged([*range(2, nz), 1], pieces, over_head)

    def frame_stage(pieces):
        return staged(range(na - 1, 0, -1), pieces, lambda x, s: over_frame(x, s * nb))

    def swapped(parts):
        return staged(range(1, nb), parts, over_frame)

    def regroup(pieces):
        return [jnp.concatenate([p[i : i + 1] for p in pieces]) for i in range(pieces[0].shape[0])]

    def flat_frames_first(by_frame):
        return jnp.concatenate(by_frame)

    def flat_heads_first(by_head):
        return jnp.concatenate([p[s : s + 1] for s in range(na) for p in by_head])

    q_sent = head_stage(prep(plan, ids, queries, True))
    k_near = frame_stage(prep(plan, ids, key_states, False))
    g_near = frame_stage(prep_grad(plan, ids, grad_out, attn_out))
    v_near = frame_stage(prep(plan, ids, value_states, False))
    by_key, n_key, by_query, n_query = lists(plan, ids, frame_order, block_live)
    keys = flat_heads_first(head_stage(regroup(k_near)))
    q_own = flat_frames_first(frame_stage(regroup(q_sent)))
    q_all = jnp.concatenate(swapped([q_own] * nb))
    g_own = flat_heads_first(head_stage(regroup(g_near)))
    g_all = jnp.concatenate(swapped([g_own] * nb))
    values = head_stage(regroup(v_near))

    lse_part = totals(plan, by_query, n_query, keys, q_all)
    lse, delta = query_rows(plan, g_all, swapped([lse_part] * nb))
    spans = [range(0, 2), range(2, nz)]
    kv_home, dq = [], None
    for place, span in enumerate(spans):
        last = place == len(spans) - 1
        kv, dq_parts = grads(
            plan, span, (by_key, n_key), q_all, g_all, lse, delta, keys,
            [values[r] for r in span], dq, last,
        )
        dq = dq_parts[0]
        kv_home.append(frame_stage(kv))
    dq_home = frame_stage(pack(plan, swapped(dq_parts)))
    grad_key, grad_value = assemble(plan, ids, spans, kv_home)
    (grad_query,) = assemble(plan, ids, [range(nz)], [dq_home])
    return grad_query, grad_key, grad_value


def solution(mesh):
    rows = P(("frame", "head"), None)
    in_specs = (rows,) * 5 + (P(), P())
    out_specs = (P("frame", "head"),) * 3
    return jax.shard_map(local, mesh=mesh, in_specs=in_specs, out_specs=out_specs, check_vma=False)
```

time: 135 us -> 131 us (0.970)
  Pallas kernels: 49.6 us -> 40.8 us
  waiting for transfers between devices: 36.7 us -> 43.1 us
  starting transfers between devices: 41.9 us -> 40 us
    pallas_call x4 -> x6, Pallas kernels: 32.1 us -> 21.4 us  [the longest x2 17.8 us: grads(): pl.pallas_call(functools.partial(grads_kernel, plan, span, first, last),...]
    ppermute x22 -> x25, waiting for transfers between devices: 21.8 us -> 30.1 us  [over_frame(): return lax.ppermute(value, 'frame', [(i, i ^ step) for i in range(count)])]
    ppermute x12, starting transfers between devices: 23.5 us -> 16.6 us  [over_head(): return lax.ppermute(value, 'head', [(i, i ^ step) for i in range(count)])]
    ppermute x22 -> x25, starting transfers between devices: 18.4 us -> 23.4 us  [over_frame(): return lax.ppermute(value, 'frame', [(i, i ^ step) for i in range(count)])]
    ppermute x12, waiting for transfers between devices: 14.9 us -> 13 us  [over_head(): return lax.ppermute(value, 'head', [(i, i ^ step) for i in range(count)])]
    unnamed x59 -> x62, local copies, waits for them, and re-layouts: 2.73 us -> 2.86 us
  transfers between devices with their start and end apart: 34 -> 37, of which waited for: 14 -> 16; matrix products, arithmetic and copies ran while one was open for 1% -> 1% of each run, Pallas kernels for 14% -> 23%
where the time goes in v1:
time: 131 us; the launch traced here: 129 us
  waiting for transfers between devices  43.1 us (33%)
  Pallas kernels  40.8 us (31%)
  starting transfers between devices  40 us (31%)
  local copies, waits for them, and re-layouts  3.19 us (2%)
    ppermute x25, waiting for transfers between devices, over_frame(): return lax.ppermute(value, 'frame', [(i, i ^ step) for i in range(count)])  30.1 us
    ppermute x25, starting transfers between devices, over_frame(): return lax.ppermute(value, 'frame', [(i, i ^ step) for i in range(count)])  23.4 us
    pallas_call x2, Pallas kernels, grads(): pl.pallas_call(functools.partial(grads_kernel, plan, span, first, last),...  17.8 us
    ppermute x12, starting transfers between devices, over_head(): return lax.ppermute(value, 'head', [(i, i ^ step) for i in range(count)])  16.6 us
    ppermute x12, waiting for transfers between devices, over_head(): return lax.ppermute(value, 'head', [(i, i ^ step) for i in range(count)])  13 us
    pallas_call x1, Pallas kernels, totals(): pl.pallas_call(functools.partial(totals_kernel, plan), out_shape=sds((pla...  8.75 us
    pallas_call x1, Pallas kernels, lists(): pl.pallas_call(functools.partial(lists_kernel, plan), out_shape=[sds((own...  7.35 us
    pallas_call x2, Pallas kernels, assemble(): pl.pallas_call(functools.partial(assemble_kernel, plan, spans, n), out_sh...  3.12 us
  transfers between devices with their start and end apart: 37, of which 16 were waited for; matrix products, arithmetic and copies ran while one was open for 1% of the time, Pallas kernels for 23%

profile of v1, /device:TPU:4, one launch (start us, length us, event | category | flops | bytes accessed | tf_op | source)
XLA Modules:
  0.0 128.7 jit_solution(11183604980328646492)
XLA Ops:
  0.7 0.1 pad_add_fusion.ids
  0.7 1.0 copy-done
  1.8 0.7 shard_map.94
  2.5 1.6 %collective-permute-start = (bf16[4,128,128]{2,1,0:T(8,128)(2,1)S(1)}, bf16[4,128,128]{2,1,0:T(8,128)(2,1)S(1)}, u32[]{:S(2)}, u32[]{:S(2)}) collective-permute-start(bf16[4,128,128]{2,1,0:T(8,128)(2,1)S(1)} %get-tuple-element.45), channel_id=1, source_target_pairs={{0,8},{8,0},{16,24},{24,16},{1,9},{9,1},{17,25},{25,17},{2,10},{10... | collective-permute-start | bytes 393224 | tf_op jit(solution)/shard_map/ppermute | solution.py:62
  4.1 2.6 %collective-permute-start.1 = (bf16[4,128,128]{2,1,0:T(8,128)(2,1)S(1)}, bf16[4,128,128]{2,1,0:T(8,128)(2,1)S(1)}, u32[]{:S(2)}, u32[]{:S(2)}) collective-permute-start(bf16[4,128,128]{2,1,0:T(8,128)(2,1)S(1)} %get-tuple-element.46), channel_id=1, source_target_pairs={{0,16},{8,24},{16,0},{24,8},{1,17},{9,25},{17,1},{25,9},{2,18},{10... | collective-permute-start | bytes 393224 | tf_op jit(solution)/shard_map/ppermute | solution.py:62
  6.7 0.2 collective-permute-start.2
  6.9 1.0 copy-done.1
  8.0 0.7 shard_map.95
  8.7 1.6 %collective-permute-start.14 = (bf16[4,128,128]{2,1,0:T(8,128)(2,1)S(1)}, bf16[4,128,128]{2,1,0:T(8,128)(2,1)S(1)}, u32[]{:S(2)}, u32[]{:S(2)}) collective-permute-start(bf16[4,128,128]{2,1,0:T(8,128)(2,1)S(1)} %get-tuple-element.55), channel_id=1, source_target_pairs={{0,2},{1,3},{2,0},{3,1},{4,6},{5,7},{6,4},{7,5},{8,10},{9,11},{10,... | collective-permute-start | bytes 393224 | tf_op jit(solution)/shard_map/ppermute | solution.py:67
  10.2 0.7 shard_map.96
  10.9 0.6 collective-permute-start.21
  11.5 0.1 copy.10.live_ref
  11.7 1.2 prep_grad.1
  13.0 7.4 %lists.1 = (s32[16,42]{1,0:T(8,128)S(1)}, s32[16]{0:T(128)S(1)}, s32[32,24]{1,0:T(8,128)S(1)}, s32[32]{0:T(128)S(1)}) custom-call(s32[3]{0:T(128)S(1)} %pad_add_fusion.ids, s32[8]{0:T(128)S(1)} %copy-done.5, s32[8,4,4]{2,1,0:T(4,128)S(1)} %copy.10.live_ref), custom_call_target="tpu_custom_call" | custom-call | bytes 10500000 | tf_op jit(solution)/shard_map/lists/pallas_call | solution.py:194
  20.4 0.4 collective-permute-start.22
  20.7 4.7 %collective-permute-done.22 = bf16[4,128,128]{2,1,0:T(8,128)(2,1)S(1)} collective-permute-done((bf16[4,128,128]{2,1,0:T(8,128)(2,1)S(1)}, bf16[4,128,128]{2,1,0:T(8,128)(2,1)S(1)}, u32[]{:S(2)}, u32[]{:S(2)}) %collective-permute-start.22) | collective-permute-done | bytes 131104 | tf_op jit(solution)/shard_map/ppermute | solution.py:67
  25.5 0.2 collective-permute-start.15
  25.7 2.8 %collective-permute-start.16 = (bf16[4,128,128]{2,1,0:T(8,128)(2,1)S(1)}, bf16[4,128,128]{2,1,0:T(8,128)(2,1)S(1)}, u32[]{:S(2)}, u32[]{:S(2)}) collective-permute-start(bf16[4,128,128]{2,1,0:T(8,128)(2,1)S(1)} %get-tuple-element.57), channel_id=1, source_target_pairs={{0,6},{1,7},{2,4},{3,5},{4,2},{5,3},{6,0},{7,1},{8,14},{9,15},{10,... | collective-permute-start | bytes 393224 | tf_op jit(solution)/shard_map/ppermute | solution.py:67
  28.5 4.7 %collective-permute-done.15 = bf16[4,128,128]{2,1,0:T(8,128)(2,1)S(1)} collective-permute-done((bf16[4,128,128]{2,1,0:T(8,128)(2,1)S(1)}, bf16[4,128,128]{2,1,0:T(8,128)(2,1)S(1)}, u32[]{:S(2)}, u32[]{:S(2)}) %collective-permute-start.15) | collective-permute-done | bytes 131104 | tf_op jit(solution)/shard_map/ppermute | solution.py:67
  33.3 0.5 collective-permute-start.7
  33.8 6.4 %collective-permute-done.23 = bf16[4,128,128]{2,1,0:T(8,128)(2,1)S(1)} collective-permute-done((bf16[4,128,128]{2,1,0:T(8,128)(2,1)S(1)}, bf16[4,128,128]{2,1,0:T(8,128)(2,1)S(1)}, u32[]{:S(2)}, u32[]{:S(2)}) %collective-permute-start.23) | collective-permute-done | bytes 131104 | tf_op jit(solution)/shard_map/ppermute | solution.py:67
  40.4 0.1 collective-permute-start.9
  40.7 3.5 %collective-permute-start.18 = (bf16[4,128,128]{2,1,0:T(8,128)(2,1)S(1)}, bf16[4,128,128]{2,1,0:T(8,128)(2,1)S(1)}, u32[]{:S(2)}, u32[]{:S(2)}) collective-permute-start(bf16[4,128,128]{2,1,0:T(8,128)(2,1)S(1)} %pad_maximum_fusion.7), channel_id=1, source_target_pairs={{0,16},{8,24},{16,0},{24,8},{1,17},{9,25},{17,1},{25,9},{2,18},{10... | collective-permute-start | bytes 393224 | tf_op jit(solution)/shard_map/ppermute | solution.py:62
  44.3 1.0 collective-permute-start.19
  45.4 1.5 %collective-permute-done.8 = bf16[4,136,128]{2,1,0:T(8,128)(2,1)S(1)} collective-permute-done((bf16[4,136,128]{2,1,0:T(8,128)(2,1)S(1)}, bf16[4,136,128]{2,1,0:T(8,128)(2,1)S(1)}, u32[]{:S(2)}, u32[]{:S(2)}) %collective-permute-start.8) | collective-permute-done | bytes 139296 | tf_op jit(solution)/shard_map/ppermute | solution.py:67
  46.9 1.6 %collective-permute-start.25 = (bf16[4,128,128]{2,1,0:T(8,128)(2,1)S(1)}, bf16[4,128,128]{2,1,0:T(8,128)(2,1)S(1)}, u32[]{:S(2)}, u32[]{:S(2)}) collective-permute-start(bf16[4,128,128]{2,1,0:T(8,128)(2,1)S(1)} %pad_maximum_fusion.10), channel_id=1, source_target_pairs={{0,24},{8,16},{16,8},{24,0},{1,25},{9,17},{17,9},{25,1},{2,26},{10... | collective-permute-start | bytes 393224 | tf_op jit(solution)/shard_map/ppermute | solution.py:62
  48.5 2.0 %collective-permute-start.26 = (bf16[4,128,128]{2,1,0:T(8,128)(2,1)S(1)}, bf16[4,128,128]{2,1,0:T(8,128)(2,1)S(1)}, u32[]{:S(2)}, u32[]{:S(2)}) collective-permute-start(bf16[4,128,128]{2,1,0:T(8,128)(2,1)S(1)} %pad_maximum_fusion.12), channel_id=1, source_target_pairs={{0,8},{8,0},{16,24},{24,16},{1,9},{9,1},{17,25},{25,17},{2,10},{10... | collective-permute-start | bytes 393224 | tf_op jit(solution)/shard_map/ppermute | solution.py:62
  50.6 6.6 %collective-permute-done.18 = bf16[4,128,128]{2,1,0:T(8,128)(2,1)S(1)} collective-permute-done((bf16[4,128,128]{2,1,0:T(8,128)(2,1)S(1)}, bf16[4,128,128]{2,1,0:T(8,128)(2,1)S(1)}, u32[]{:S(2)}, u32[]{:S(2)}) %collective-permute-start.18) | collective-permute-done | bytes 131104 | tf_op jit(solution)/shard_map/ppermute | solution.py:62
  57.2 1.6 %collective-permute-start.3 = (bf16[4,128,128]{2,1,0:T(8,128)(2,1)S(1)}, bf16[4,128,128]{2,1,0:T(8,128)(2,1)S(1)}, u32[]{:S(2)}, u32[]{:S(2)}) collective-permute-start(bf16[4,128,128]{2,1,0:T(8,128)(2,1)S(1)} %pad_maximum_fusion.3), channel_id=1, source_target_pairs={{0,2},{1,3},{2,0},{3,1},{4,6},{5,7},{6,4},{7,5},{8,10},{9,11},{10,... | collective-permute-start | bytes 393224 | tf_op jit(solution)/shard_map/ppermute | solution.py:67
  58.9 1.0 collective-permute-start.4
  60.1 2.2 %collective-permute-done.3 = bf16[4,128,128]{2,1,0:T(8,128)(2,1)S(1)} collective-permute-done((bf16[4,128,128]{2,1,0:T(8,128)(2,1)S(1)}, bf16[4,128,128]{2,1,0:T(8,128)(2,1)S(1)}, u32[]{:S(2)}, u32[]{:S(2)}) %collective-permute-start.3) | collective-permute-done | bytes 131104 | tf_op jit(solution)/shard_map/ppermute | solution.py:67
  62.2 2.0 %collective-permute-start.5 = (bf16[4,128,128]{2,1,0:T(8,128)(2,1)S(1)}, bf16[4,128,128]{2,1,0:T(8,128)(2,1)S(1)}, u32[]{:S(2)}, u32[]{:S(2)}) collective-permute-start(bf16[4,128,128]{2,1,0:T(8,128)(2,1)S(1)} %pad_maximum_fusion.5), channel_id=1, source_target_pairs={{0,6},{1,7},{2,4},{3,5},{4,2},{5,3},{6,0},{7,1},{8,14},{9,15},{10,... | collective-permute-start | bytes 393224 | tf_op jit(solution)/shard_map/ppermute | solution.py:67
  64.3 1.3 %collective-permute-start.10 = (bf16[4,136,128]{2,1,0:T(8,128)(2,1)S(1)}, bf16[4,136,128]{2,1,0:T(8,128)(2,1)S(1)}, u32[]{:S(2)}, u32[]{:S(2)}) collective-permute-start(bf16[4,136,128]{2,1,0:T(8,128)(2,1)S(1)} %pad_maximum_fusion), channel_id=1, source_target_pairs={{0,8},{8,0},{16,24},{24,16},{1,9},{9,1},{17,25},{25,17},{2,10},{10... | collective-permute-start | bytes 417800 | tf_op jit(solution)/shard_map/ppermute | solution.py:62
  65.6 2.4 %collective-permute-done.5 = bf16[4,128,128]{2,1,0:T(8,128)(2,1)S(1)} collective-permute-done((bf16[4,128,128]{2,1,0:T(8,128)(2,1)S(1)}, bf16[4,128,128]{2,1,0:T(8,128)(2,1)S(1)}, u32[]{:S(2)}, u32[]{:S(2)}) %collective-permute-start.5) | collective-permute-done | bytes 131104 | tf_op jit(solution)/shard_map/ppermute | solution.py:67
  68.1 0.6 collective-permute-start.11
  68.7 1.5 %collective-permute-done.10 = bf16[4,136,128]{2,1,0:T(8,128)(2,1)S(1)} collective-permute-done((bf16[4,136,128]{2,1,0:T(8,128)(2,1)S(1)}, bf16[4,136,128]{2,1,0:T(8,128)(2,1)S(1)}, u32[]{:S(2)}, u32[]{:S(2)}) %collective-permute-start.10) | collective-permute-done | bytes 139296 | tf_op jit(solution)/shard_map/ppermute | solution.py:62
  70.3 2.1 %collective-permute-start.12 = (bf16[4,136,128]{2,1,0:T(8,128)(2,1)S(1)}, bf16[4,136,128]{2,1,0:T(8,128)(2,1)S(1)}, u32[]{:S(2)}, u32[]{:S(2)}) collective-permute-start(bf16[4,136,128]{2,1,0:T(8,128)(2,1)S(1)} %pad_maximum_fusion.2), channel_id=1, source_target_pairs={{0,24},{8,16},{16,8},{24,0},{1,25},{9,17},{17,9},{25,1},{2,26},{10... | collective-permute-start | bytes 417800 | tf_op jit(solution)/shard_map/ppermute | solution.py:62
  72.4 2.5 %collective-permute-done.11 = bf16[4,136,128]{2,1,0:T(8,128)(2,1)S(1)} collective-permute-done((bf16[4,136,128]{2,1,0:T(8,128)(2,1)S(1)}, bf16[4,136,128]{2,1,0:T(8,128)(2,1)S(1)}, u32[]{:S(2)}, u32[]{:S(2)}) %collective-permute-start.11) | collective-permute-done | bytes 139296 | tf_op jit(solution)/shard_map/ppermute | solution.py:62
  74.9 2.3 %collective-permute-done.12 = bf16[4,136,128]{2,1,0:T(8,128)(2,1)S(1)} collective-permute-done((bf16[4,136,128]{2,1,0:T(8,128)(2,1)S(1)}, bf16[4,136,128]{2,1,0:T(8,128)(2,1)S(1)}, u32[]{:S(2)}, u32[]{:S(2)}) %collective-permute-start.12) | collective-permute-done | bytes 139296 | tf_op jit(solution)/shard_map/ppermute | solution.py:62
  77.7 0.1 constant_dynamic-update-slice_fusion.7.q_ref
  77.8 8.7 %totals.1.refs_0_ = f32[32,128]{1,0:T(8,128)S(1)} custom-call(s32[32,24]{1,0:T(8,128)S(1)} %get-tuple-element.52.by_query, s32[32]{0:T(128)S(1)} %get-tuple-element.53.n_query, bf16[16,128,128]{2,1,0:T(8,128)(2,1)S(1)} %constant_dynamic-update-slice_fusion.48.k_ref, bf16[32,128,128]{2,1,0:T(8,128)(2,1)S(1)} %constant_dynamic-update-slice_fusion.7.q_ref), custom_call_target="tpu_custom_call" | custom-call | bytes 24500000 | tf_op jit(solution)/shard_map/totals/pallas_call | solution.py:285
  86.6 0.6 collective-permute-start.20
  87.1 0.1 constant_dynamic-update-slice_fusion.31.g_ref
  87.2 0.8 collective-permute-done.20.refs_1_
  88.0 0.3 query_rows.1
  88.3 8.7 %shard_map.97 = (bf16[2,2,128,128]{3,2,1,0:T(8,128)(2,1)S(1)}, bf16[2,2,128,128]{3,2,1,0:T(8,128)(2,1)S(1)}, bf16[2,2,128,128]{3,2,1,0:T(8,128)(2,1)S(1)}, bf16[...) custom-call(s32[16,42]{1,0:T(8,128)S(1)} %get-tuple-element.42.by_key, s32[16]{0:T(128)S(1)} %get-tuple-element.43.n_key, ...), custom_call_target="tpu_custom_call" | custom-call | bytes 24500000 | tf_op jit(solution)/shard_map/pallas_call | solution.py:429
  97.0 9.1 %shard_map.98 = (bf16[2,2,128,128]{3,2,1,0:T(8,128)(2,1)S(1)}, bf16[2,2,128,128]{3,2,1,0:T(8,128)(2,1)S(1)}, bf16[2,2,128,128]{3,2,1,0:T(8,128)(2,1)S(1)}, bf16[...) custom-call(s32[16,42]{1,0:T(8,128)S(1)} %get-tuple-element.42.by_key, ...), custom_call_target="tpu_custom_call" | custom-call | bytes 24500000 | tf_op jit(solution)/shard_map/pallas_call | solution.py:429
  106.1 0.4 collective-permute-start.27
  106.5 1.4 %collective-permute-start.34 = (bf16[2,2,128,128]{3,2,1,0:T(8,128)(2,1)S(1)}, bf16[2,2,128,128]{3,2,1,0:T(8,128)(2,1)S(1)}, u32[]{:S(2)}, u32[]{:S(2)}) collective-permute-start(bf16[2,2,128,128]{3,2,1,0:T(8,128)(2,1)S(1)} %get-tuple-element.76), channel_id=1, source_target_pairs={{0,2},{1,3},{2,0},{3,1},{4,6},{5,7},{6,4},{7,5},{8,10},{9,11},{10,... | collective-permute-start | bytes 393224 | tf_op jit(solution)/shard_map/ppermute | solution.py:67
  107.9 1.0 collective-permute-start.35
  108.9 1.1 collective-permute-start.36
  110.0 1.4 %collective-permute-start.31 = (bf16[2,2,128,128]{3,2,1,0:T(8,128)(2,1)S(1)}, bf16[2,2,128,128]{3,2,1,0:T(8,128)(2,1)S(1)}, u32[]{:S(2)}, u32[]{:S(2)}) collective-permute-start(bf16[2,2,128,128]{3,2,1,0:T(8,128)(2,1)S(1)} %get-tuple-element.72), channel_id=1, source_target_pairs={{0,2},{1,3},{2,0},{3,1},{4,6},{5,7},{6,4},{7,5},{8,10},{9,11},{10,... | collective-permute-start | bytes 393224 | tf_op jit(solution)/shard_map/ppermute | solution.py:67
  111.4 1.0 collective-permute-start.32
  112.4 0.2 pack.1
  112.6 2.1 %collective-permute-start.33 = (bf16[2,2,128,128]{3,2,1,0:T(8,128)(2,1)S(1)}, bf16[2,2,128,128]{3,2,1,0:T(8,128)(2,1)S(1)}, u32[]{:S(2)}, u32[]{:S(2)}) collective-permute-start(bf16[2,2,128,128]{3,2,1,0:T(8,128)(2,1)S(1)} %get-tuple-element.74), channel_id=1, source_target_pairs={{0,6},{1,7},{2,4},{3,5},{4,2},{5,3},{6,0},{7,1},{8,14},{9,15},{10,... | collective-permute-start | bytes 393224 | tf_op jit(solution)/shard_map/ppermute | solution.py:67
  114.7 1.9 %collective-permute-done.35.refs_6_ = bf16[2,2,128,128]{3,2,1,0:T(8,128)(2,1)S(1)} collective-permute-done((bf16[2,2,128,128]{3,2,1,0:T(8,128)(2,1)S(1)}, bf16[2,2,128,128]{3,2,1,0:T(8,128)(2,1)S(1)}, u32[]{:S(2)}, u32[]{:S(2)}) %collective-permute-start.35) | collective-permute-done | bytes 131104 | tf_op jit(solution)/shard_map/ppermute | solution.py:67
  116.7 1.7 %collective-permute-start.29 = (bf16[1,4,128,128]{3,2,1,0:T(8,128)(2,1)S(1)}, bf16[1,4,128,128]{3,2,1,0:T(8,128)(2,1)S(1)}, u32[]{:S(2)}, u32[]{:S(2)}) collective-permute-start(bf16[1,4,128,128]{3,2,1,0:T(8,128)(2,1)S(1)} %get-tuple-element.69), channel_id=1, source_target_pairs={{0,4},{1,5},{2,6},{3,7},{4,0},{5,1},{6,2},{7,3},{8,12},{9,13},{10,... | collective-permute-start | bytes 393224 | tf_op jit(solution)/shard_map/ppermute | solution.py:67
  118.4 0.2 collective-permute-done.31.refs_1_
  118.6 1.8 %collective-permute-start.30 = (bf16[1,4,128,128]{3,2,1,0:T(8,128)(2,1)S(1)}, bf16[1,4,128,128]{3,2,1,0:T(8,128)(2,1)S(1)}, u32[]{:S(2)}, u32[]{:S(2)}) collective-permute-start(bf16[1,4,128,128]{3,2,1,0:T(8,128)(2,1)S(1)} %get-tuple-element.70), channel_id=1, source_target_pairs={{0,6},{1,7},{2,4},{3,5},{4,2},{5,3},{6,0},{7,1},{8,14},{9,15},{10,... | collective-permute-start | bytes 393224 | tf_op jit(solution)/shard_map/ppermute | solution.py:67
  120.4 1.9 %collective-permute-done.32.refs_2_ = bf16[2,2,128,128]{3,2,1,0:T(8,128)(2,1)S(1)} collective-permute-done((bf16[2,2,128,128]{3,2,1,0:T(8,128)(2,1)S(1)}, bf16[2,2,128,128]{3,2,1,0:T(8,128)(2,1)S(1)}, u32[]{:S(2)}, u32[]{:S(2)}) %collective-permute-start.32) | collective-permute-done | bytes 131104 | tf_op jit(solution)/shard_map/ppermute | solution.py:67
  122.3 1.7 %shard_map.100 = (bf16[512,512]{1,0:T(8,128)(2,1)}, bf16[512,512]{1,0:T(8,128)(2,1)}) custom-call(s32[3]{0:T(128)S(1)} %pad_add_fusion.ids, bf16[2,2,128,128]{3,2,1,0:T(8,128)(2,1)S(1)} %get-tuple-element.71.refs_0_, bf16[2,2,128,128]{3,2,1,0:T(8,128)(2,1)S(1)} %collective-permute-done.31.refs_1_, ...), custom_call_target="tpu_custom_call" | custom-call | bytes 5250000 | tf_op jit(solution)/shard_map/pallas_call | solution.py:478
  124.0 0.3 collective-permute-done.28.refs_1_
  124.3 3.0 %collective-permute-done.29.refs_2_ = bf16[1,4,128,128]{3,2,1,0:T(8,128)(2,1)S(1)} collective-permute-done((bf16[1,4,128,128]{3,2,1,0:T(8,128)(2,1)S(1)}, bf16[1,4,128,128]{3,2,1,0:T(8,128)(2,1)S(1)}, u32[]{:S(2)}, u32[]{:S(2)}) %collective-permute-start.29) | collective-permute-done | bytes 131104 | tf_op jit(solution)/shard_map/ppermute | solution.py:67
  127.2 1.4 %shard_map.99 = bf16[512,512]{1,0:T(8,128)(2,1)} custom-call(s32[3]{0:T(128)S(1)} %pad_add_fusion.ids, bf16[1,4,128,128]{3,2,1,0:T(8,128)(2,1)S(1)} %get-tuple-element.67.refs_0_, bf16[1,4,128,128]{3,2,1,0:T(8,128)(2,1)S(1)} %collective-permute-done.28.refs_1_, bf16[1,4,128,128]{3,2,1,0:T(8,128)(2,1)S(1)} %collective-permute-done.29.refs_2_, ...), custom_call_target="tpu_custom_call" | custom-call | bytes 5250000 | tf_op jit(solution)/shard_map/pallas_call | solution.py:478
  (114 shorter events, 1.3 us)
Async XLA Ops:
  0.6 10.9 %copy-start.6 = (s32[8,4,4]{0,2,1:T(4,128)S(1)}, s32[8,4,4]{0,2,1:T(4,128)}, u32[]{:S(2)}) copy-start(s32[8,4,4]{0,2,1:T(4,128)} %param.13) | copy-start | bytes 1540
  0.7 1.0 copy-start
  1.8 8.5 %copy-start.2 = (bf16[128,2048]{1,0:T(8,128)(2,1)S(1)}, bf16[128,2048]{1,0:T(8,128)(2,1)}, u32[]{:S(2)}) copy-start(bf16[128,2048]{1,0:T(8,128)(2,1)} %x_ref.5) | copy-start | bytes 1572868
  2.5 37.9 %collective-permute-start = (bf16[4,128,128]{2,1,0:T(8,128)(2,1)S(1)}, bf16[4,128,128]{2,1,0:T(8,128)(2,1)S(1)}, u32[]{:S(2)}, u32[]{:S(2)}) collective-permute-start(bf16[4,128,128]{2,1,0:T(8,128)(2,1)S(1)} %get-tuple-element.45), channel_id=1, source_target_pairs={{0,8},{8,0},{16,24},{24,16},{1,9},{9,1},{17,25},{25,17},{2,10},{10... | collective-permute-start | bytes 393224 | tf_op jit(solution)/shard_map/ppermute | solution.py:62
  4.1 36.4 %collective-permute-start.1 = (bf16[4,128,128]{2,1,0:T(8,128)(2,1)S(1)}, bf16[4,128,128]{2,1,0:T(8,128)(2,1)S(1)}, u32[]{:S(2)}, u32[]{:S(2)}) collective-permute-start(bf16[4,128,128]{2,1,0:T(8,128)(2,1)S(1)} %get-tuple-element.46), channel_id=1, source_target_pairs={{0,16},{8,24},{16,0},{24,8},{1,17},{9,25},{17,1},{25,9},{2,18},{10... | collective-permute-start | bytes 393224 | tf_op jit(solution)/shard_map/ppermute | solution.py:62
  6.7 34.0 %collective-permute-start.2 = (bf16[4,128,128]{2,1,0:T(8,128)(2,1)S(1)}, bf16[4,128,128]{2,1,0:T(8,128)(2,1)S(1)}, u32[]{:S(2)}, u32[]{:S(2)}) collective-permute-start(bf16[4,128,128]{2,1,0:T(8,128)(2,1)S(1)} %get-tuple-element.47), channel_id=1, source_target_pairs={{0,24},{8,16},{16,8},{24,0},{1,25},{9,17},{17,9},{25,1},{2,26},{10... | collective-permute-start | bytes 393224 | tf_op jit(solution)/shard_map/ppermute | solution.py:62
  6.9 1.0 copy-start.1
  8.0 3.7 %copy-start.3 = (bf16[128,2048]{1,0:T(8,128)(2,1)S(1)}, bf16[128,2048]{1,0:T(8,128)(2,1)}, u32[]{:S(2)}) copy-start(bf16[128,2048]{1,0:T(8,128)(2,1)} %g_ref.1) | copy-start | bytes 1572868
  8.0 3.7 %copy-start.4 = (bf16[128,2048]{1,0:T(8,128)(2,1)S(1)}, bf16[128,2048]{1,0:T(8,128)(2,1)}, u32[]{:S(2)}) copy-start(bf16[128,2048]{1,0:T(8,128)(2,1)} %o_ref.1) | copy-start | bytes 1572868
  8.7 4.3 %copy-start.5 = (s32[8]{0:T(128)S(1)}, s32[8]{0:T(128)}, u32[]{:S(2)}) copy-start(s32[8]{0:T(128)} %order.1) | copy-start | bytes 100
  8.7 17.0 %collective-permute-start.14 = (bf16[4,128,128]{2,1,0:T(8,128)(2,1)S(1)}, bf16[4,128,128]{2,1,0:T(8,128)(2,1)S(1)}, u32[]{:S(2)}, u32[]{:S(2)}) collective-permute-start(bf16[4,128,128]{2,1,0:T(8,128)(2,1)S(1)} %get-tuple-element.55), channel_id=1, source_target_pairs={{0,2},{1,3},{2,0},{3,1},{4,6},{5,7},{6,4},{7,5},{8,10},{9,11},{10,... | collective-permute-start | bytes 393224 | tf_op jit(solution)/shard_map/ppermute | solution.py:67
  10.9 9.4 %collective-permute-start.21 = (bf16[4,128,128]{2,1,0:T(8,128)(2,1)S(1)}, bf16[4,128,128]{2,1,0:T(8,128)(2,1)S(1)}, u32[]{:S(2)}, u32[]{:S(2)}) collective-permute-start(bf16[4,128,128]{2,1,0:T(8,128)(2,1)S(1)} %get-tuple-element.61), channel_id=1, source_target_pairs={{0,2},{1,3},{2,0},{3,1},{4,6},{5,7},{6,4},{7,5},{8,10},{9,11},{10,... | collective-permute-start | bytes 393224 | tf_op jit(solution)/shard_map/ppermute | solution.py:67
  20.4 5.1 %collective-permute-start.22 = (bf16[4,128,128]{2,1,0:T(8,128)(2,1)S(1)}, bf16[4,128,128]{2,1,0:T(8,128)(2,1)S(1)}, u32[]{:S(2)}, u32[]{:S(2)}) collective-permute-start(bf16[4,128,128]{2,1,0:T(8,128)(2,1)S(1)} %get-tuple-element.62), channel_id=1, source_target_pairs={{0,4},{1,5},{2,6},{3,7},{4,0},{5,1},{6,2},{7,3},{8,12},{9,13},{10,... | collective-permute-start | bytes 393224 | tf_op jit(solution)/shard_map/ppermute | solution.py:67
  25.5 7.8 %collective-permute-start.15 = (bf16[4,128,128]{2,1,0:T(8,128)(2,1)S(1)}, bf16[4,128,128]{2,1,0:T(8,128)(2,1)S(1)}, u32[]{:S(2)}, u32[]{:S(2)}) collective-permute-start(bf16[4,128,128]{2,1,0:T(8,128)(2,1)S(1)} %get-tuple-element.56), channel_id=1, source_target_pairs={{0,4},{1,5},{2,6},{3,7},{4,0},{5,1},{6,2},{7,3},{8,12},{9,13},{10,... | collective-permute-start | bytes 393224 | tf_op jit(solution)/shard_map/ppermute | solution.py:67
  25.7 7.5 %collective-permute-start.16 = (bf16[4,128,128]{2,1,0:T(8,128)(2,1)S(1)}, bf16[4,128,128]{2,1,0:T(8,128)(2,1)S(1)}, u32[]{:S(2)}, u32[]{:S(2)}) collective-permute-start(bf16[4,128,128]{2,1,0:T(8,128)(2,1)S(1)} %get-tuple-element.57), channel_id=1, source_target_pairs={{0,6},{1,7},{2,4},{3,5},{4,2},{5,3},{6,0},{7,1},{8,14},{9,15},{10,... | collective-permute-start | bytes 393224 | tf_op jit(solution)/shard_map/ppermute | solution.py:67
  33.2 7.1 %collective-permute-start.23 = (bf16[4,128,128]{2,1,0:T(8,128)(2,1)S(1)}, bf16[4,128,128]{2,1,0:T(8,128)(2,1)S(1)}, u32[]{:S(2)}, u32[]{:S(2)}) collective-permute-start(bf16[4,128,128]{2,1,0:T(8,128)(2,1)S(1)} %get-tuple-element.63), channel_id=1, source_target_pairs={{0,6},{1,7},{2,4},{3,5},{4,2},{5,3},{6,0},{7,1},{8,14},{9,15},{10,... | collective-permute-start | bytes 393224 | tf_op jit(solution)/shard_map/ppermute | solution.py:67
  33.3 11.1 %collective-permute-start.7 = (bf16[4,136,128]{2,1,0:T(8,128)(2,1)S(1)}, bf16[4,136,128]{2,1,0:T(8,128)(2,1)S(1)}, u32[]{:S(2)}, u32[]{:S(2)}) collective-permute-start(bf16[4,136,128]{2,1,0:T(8,128)(2,1)S(1)} %get-tuple-element.49), channel_id=1, source_target_pairs={{0,2},{1,3},{2,0},{3,1},{4,6},{5,7},{6,4},{7,5},{8,10},{9,11},{10,... | collective-permute-start | bytes 417800 | tf_op jit(solution)/shard_map/ppermute | solution.py:67
  40.3 6.5 %collective-permute-start.8 = (bf16[4,136,128]{2,1,0:T(8,128)(2,1)S(1)}, bf16[4,136,128]{2,1,0:T(8,128)(2,1)S(1)}, u32[]{:S(2)}, u32[]{:S(2)}) collective-permute-start(bf16[4,136,128]{2,1,0:T(8,128)(2,1)S(1)} %get-tuple-element.50), channel_id=1, source_target_pairs={{0,4},{1,5},{2,6},{3,7},{4,0},{5,1},{6,2},{7,3},{8,12},{9,13},{10,... | collective-permute-start | bytes 417800 | tf_op jit(solution)/shard_map/ppermute | solution.py:67
  40.4 6.5 %collective-permute-start.9 = (bf16[4,136,128]{2,1,0:T(8,128)(2,1)S(1)}, bf16[4,136,128]{2,1,0:T(8,128)(2,1)S(1)}, u32[]{:S(2)}, u32[]{:S(2)}) collective-permute-start(bf16[4,136,128]{2,1,0:T(8,128)(2,1)S(1)} %get-tuple-element.51), channel_id=1, source_target_pairs={{0,6},{1,7},{2,4},{3,5},{4,2},{5,3},{6,0},{7,1},{8,14},{9,15},{10,... | collective-permute-start | bytes 417800 | tf_op jit(solution)/shard_map/ppermute | solution.py:67
  40.5 8.0 %collective-permute-start.17 = (bf16[4,128,128]{2,1,0:T(8,128)(2,1)S(1)}, bf16[4,128,128]{2,1,0:T(8,128)(2,1)S(1)}, u32[]{:S(2)}, u32[]{:S(2)}) collective-permute-start(bf16[4,128,128]{2,1,0:T(8,128)(2,1)S(1)} %pad_maximum_fusion.6), channel_id=1, source_target_pairs={{0,8},{8,0},{16,24},{24,16},{1,9},{9,1},{17,25},{25,17},{2,10},{10... | collective-permute-start | bytes 393224 | tf_op jit(solution)/shard_map/ppermute | solution.py:62
  40.7 16.5 %collective-permute-start.18 = (bf16[4,128,128]{2,1,0:T(8,128)(2,1)S(1)}, bf16[4,128,128]{2,1,0:T(8,128)(2,1)S(1)}, u32[]{:S(2)}, u32[]{:S(2)}) collective-permute-start(bf16[4,128,128]{2,1,0:T(8,128)(2,1)S(1)} %pad_maximum_fusion.7), channel_id=1, source_target_pairs={{0,16},{8,24},{16,0},{24,8},{1,17},{9,25},{17,1},{25,9},{2,18},{10... | collective-permute-start | bytes 393224 | tf_op jit(solution)/shard_map/ppermute | solution.py:62
  44.3 14.5 %collective-permute-start.19 = (bf16[4,128,128]{2,1,0:T(8,128)(2,1)S(1)}, bf16[4,128,128]{2,1,0:T(8,128)(2,1)S(1)}, u32[]{:S(2)}, u32[]{:S(2)}) collective-permute-start(bf16[4,128,128]{2,1,0:T(8,128)(2,1)S(1)} %pad_maximum_fusion.8), channel_id=1, source_target_pairs={{0,24},{8,16},{16,8},{24,0},{1,25},{9,17},{17,9},{25,1},{2,26},{10... | collective-permute-start | bytes 393224 | tf_op jit(solution)/shard_map/ppermute | solution.py:62
  46.8 50.1 %collective-permute-start.24 = (bf16[4,128,128]{2,1,0:T(8,128)(2,1)S(1)}, bf16[4,128,128]{2,1,0:T(8,128)(2,1)S(1)}, u32[]{:S(2)}, u32[]{:S(2)}) collective-permute-start(bf16[4,128,128]{2,1,0:T(8,128)(2,1)S(1)} %pad_maximum_fusion.9), channel_id=1, source_target_pairs={{0,16},{8,24},{16,0},{24,8},{1,17},{9,25},{17,1},{25,9},{2,18},{10... | collective-permute-start | bytes 393224 | tf_op jit(solution)/shard_map/ppermute | solution.py:62
  46.9 50.1 %collective-permute-start.25 = (bf16[4,128,128]{2,1,0:T(8,128)(2,1)S(1)}, bf16[4,128,128]{2,1,0:T(8,128)(2,1)S(1)}, u32[]{:S(2)}, u32[]{:S(2)}) collective-permute-start(bf16[4,128,128]{2,1,0:T(8,128)(2,1)S(1)} %pad_maximum_fusion.10), channel_id=1, source_target_pairs={{0,24},{8,16},{16,8},{24,0},{1,25},{9,17},{17,9},{25,1},{2,26},{10... | collective-permute-start | bytes 393224 | tf_op jit(solution)/shard_map/ppermute | solution.py:62
  48.5 39.7 %collective-permute-start.26 = (bf16[4,128,128]{2,1,0:T(8,128)(2,1)S(1)}, bf16[4,128,128]{2,1,0:T(8,128)(2,1)S(1)}, u32[]{:S(2)}, u32[]{:S(2)}) collective-permute-start(bf16[4,128,128]{2,1,0:T(8,128)(2,1)S(1)} %pad_maximum_fusion.12), channel_id=1, source_target_pairs={{0,8},{8,0},{16,24},{24,16},{1,9},{9,1},{17,25},{25,17},{2,10},{10... | collective-permute-start | bytes 393224 | tf_op jit(solution)/shard_map/ppermute | solution.py:62
  57.2 5.0 %collective-permute-start.3 = (bf16[4,128,128]{2,1,0:T(8,128)(2,1)S(1)}, bf16[4,128,128]{2,1,0:T(8,128)(2,1)S(1)}, u32[]{:S(2)}, u32[]{:S(2)}) collective-permute-start(bf16[4,128,128]{2,1,0:T(8,128)(2,1)S(1)} %pad_maximum_fusion.3), channel_id=1, source_target_pairs={{0,2},{1,3},{2,0},{3,1},{4,6},{5,7},{6,4},{7,5},{8,10},{9,11},{10,... | collective-permute-start | bytes 393224 | tf_op jit(solution)/shard_map/ppermute | solution.py:67
  58.9 5.4 %collective-permute-start.4 = (bf16[4,128,128]{2,1,0:T(8,128)(2,1)S(1)}, bf16[4,128,128]{2,1,0:T(8,128)(2,1)S(1)}, u32[]{:S(2)}, u32[]{:S(2)}) collective-permute-start(bf16[4,128,128]{2,1,0:T(8,128)(2,1)S(1)} %pad_maximum_fusion.4), channel_id=1, source_target_pairs={{0,4},{1,5},{2,6},{3,7},{4,0},{5,1},{6,2},{7,3},{8,12},{9,13},{10,... | collective-permute-start | bytes 393224 | tf_op jit(solution)/shard_map/ppermute | solution.py:67
  62.2 5.9 %collective-permute-start.5 = (bf16[4,128,128]{2,1,0:T(8,128)(2,1)S(1)}, bf16[4,128,128]{2,1,0:T(8,128)(2,1)S(1)}, u32[]{:S(2)}, u32[]{:S(2)}) collective-permute-start(bf16[4,128,128]{2,1,0:T(8,128)(2,1)S(1)} %pad_maximum_fusion.5), channel_id=1, source_target_pairs={{0,6},{1,7},{2,4},{3,5},{4,2},{5,3},{6,0},{7,1},{8,14},{9,15},{10,... | collective-permute-start | bytes 393224 | tf_op jit(solution)/shard_map/ppermute | solution.py:67
  64.3 6.0 %collective-permute-start.10 = (bf16[4,136,128]{2,1,0:T(8,128)(2,1)S(1)}, bf16[4,136,128]{2,1,0:T(8,128)(2,1)S(1)}, u32[]{:S(2)}, u32[]{:S(2)}) collective-permute-start(bf16[4,136,128]{2,1,0:T(8,128)(2,1)S(1)} %pad_maximum_fusion), channel_id=1, source_target_pairs={{0,8},{8,0},{16,24},{24,16},{1,9},{9,1},{17,25},{25,17},{2,10},{10... | collective-permute-start | bytes 417800 | tf_op jit(solution)/shard_map/ppermute | solution.py:62
  68.1 6.8 %collective-permute-start.11 = (bf16[4,136,128]{2,1,0:T(8,128)(2,1)S(1)}, bf16[4,136,128]{2,1,0:T(8,128)(2,1)S(1)}, u32[]{:S(2)}, u32[]{:S(2)}) collective-permute-start(bf16[4,136,128]{2,1,0:T(8,128)(2,1)S(1)} %pad_maximum_fusion.1), channel_id=1, source_target_pairs={{0,16},{8,24},{16,0},{24,8},{1,17},{9,25},{17,1},{25,9},{2,18},{10... | collective-permute-start | bytes 417800 | tf_op jit(solution)/shard_map/ppermute | solution.py:62
  70.3 7.0 %collective-permute-start.12 = (bf16[4,136,128]{2,1,0:T(8,128)(2,1)S(1)}, bf16[4,136,128]{2,1,0:T(8,128)(2,1)S(1)}, u32[]{:S(2)}, u32[]{:S(2)}) collective-permute-start(bf16[4,136,128]{2,1,0:T(8,128)(2,1)S(1)} %pad_maximum_fusion.2), channel_id=1, source_target_pairs={{0,24},{8,16},{16,8},{24,0},{1,25},{9,17},{17,9},{25,1},{2,26},{10... | collective-permute-start | bytes 417800 | tf_op jit(solution)/shard_map/ppermute | solution.py:62
  74.9 2.8 %collective-permute-start.6 = (bf16[16,128,128]{2,1,0:T(8,128)(2,1)S(1)}, bf16[16,128,128]{2,1,0:T(8,128)(2,1)S(1)}, u32[]{:S(2)}, u32[]{:S(2)}) collective-permute-start(bf16[16,128,128]{2,1,0:T(8,128)(2,1)S(1)} %get-tuple-element.130), channel_id=1, source_target_pairs={{0,1},{1,0},{2,3},{3,2},{4,5},{5,4},{6,7},{7,6},{8,9},{9,8},{10,11... | collective-permute-start | bytes 1572872 | tf_op jit(solution)/shard_map/ppermute | solution.py:67
  77.4 9.7 %collective-permute-start.13 = (bf16[16,136,128]{2,1,0:T(8,128)(2,1)S(1)}, bf16[16,136,128]{2,1,0:T(8,128)(2,1)S(1)}, u32[]{:S(2)}, u32[]{:S(2)}) collective-permute-start(bf16[16,136,128]{2,1,0:T(8,128)(2,1)S(1)} %get-tuple-element.81), channel_id=1, source_target_pairs={{0,1},{1,0},{2,3},{3,2},{4,5},{5,4},{6,7},{7,6},{8,9},{9,8},{10,11... | collective-permute-start | bytes 1671176 | tf_op jit(solution)/shard_map/ppermute | solution.py:67
  86.6 1.4 %collective-permute-start.20 = (f32[32,128]{1,0:T(8,128)S(1)}, f32[32,128]{1,0:T(8,128)S(1)}, u32[]{:S(2)}, u32[]{:S(2)}) collective-permute-start(f32[32,128]{1,0:T(8,128)S(1)} %totals.1.refs_0_), channel_id=1, source_target_pairs={{0,1},{1,0},{2,3},{3,2},{4,5},{5,4},{6,7},{7,6},{8,9},{9,8},{10,11... | collective-permute-start | bytes 49160 | tf_op jit(solution)/shard_map/ppermute | solution.py:67
  106.1 5.4 %collective-permute-start.27 = (f32[16,128,128]{2,1,0:T(8,128)S(1)}, f32[16,128,128]{2,1,0:T(8,128)S(1)}, u32[]{:S(2)}, u32[]{:S(2)}) collective-permute-start(f32[16,128,128]{2,1,0:T(8,128)S(1)} %get-tuple-element.66), channel_id=1, source_target_pairs={{0,1},{1,0},{2,3},{3,2},{4,5},{5,4},{6,7},{7,6},{8,9},{9,8},{10,11... | collective-permute-start | bytes 3145736 | tf_op jit(solution)/shard_map/ppermute | solution.py:67
  106.5 6.1 %collective-permute-start.34 = (bf16[2,2,128,128]{3,2,1,0:T(8,128)(2,1)S(1)}, bf16[2,2,128,128]{3,2,1,0:T(8,128)(2,1)S(1)}, u32[]{:S(2)}, u32[]{:S(2)}) collective-permute-start(bf16[2,2,128,128]{3,2,1,0:T(8,128)(2,1)S(1)} %get-tuple-element.76), channel_id=1, source_target_pairs={{0,2},{1,3},{2,0},{3,1},{4,6},{5,7},{6,4},{7,5},{8,10},{9,11},{10,... | collective-permute-start | bytes 393224 | tf_op jit(solution)/shard_map/ppermute | solution.py:67
  107.9 8.7 %collective-permute-start.35 = (bf16[2,2,128,128]{3,2,1,0:T(8,128)(2,1)S(1)}, bf16[2,2,128,128]{3,2,1,0:T(8,128)(2,1)S(1)}, u32[]{:S(2)}, u32[]{:S(2)}) collective-permute-start(bf16[2,2,128,128]{3,2,1,0:T(8,128)(2,1)S(1)} %get-tuple-element.77), channel_id=1, source_target_pairs={{0,4},{1,5},{2,6},{3,7},{4,0},{5,1},{6,2},{7,3},{8,12},{9,13},{10,... | collective-permute-start | bytes 393224 | tf_op jit(solution)/shard_map/ppermute | solution.py:67
  108.9 7.8 %collective-permute-start.36 = (bf16[2,2,128,128]{3,2,1,0:T(8,128)(2,1)S(1)}, bf16[2,2,128,128]{3,2,1,0:T(8,128)(2,1)S(1)}, u32[]{:S(2)}, u32[]{:S(2)}) collective-permute-start(bf16[2,2,128,128]{3,2,1,0:T(8,128)(2,1)S(1)} %get-tuple-element.78), channel_id=1, source_target_pairs={{0,6},{1,7},{2,4},{3,5},{4,2},{5,3},{6,0},{7,1},{8,14},{9,15},{10,... | collective-permute-start | bytes 393224 | tf_op jit(solution)/shard_map/ppermute | solution.py:67
  110.0 8.6 %collective-permute-start.31 = (bf16[2,2,128,128]{3,2,1,0:T(8,128)(2,1)S(1)}, bf16[2,2,128,128]{3,2,1,0:T(8,128)(2,1)S(1)}, u32[]{:S(2)}, u32[]{:S(2)}) collective-permute-start(bf16[2,2,128,128]{3,2,1,0:T(8,128)(2,1)S(1)} %get-tuple-element.72), channel_id=1, source_target_pairs={{0,2},{1,3},{2,0},{3,1},{4,6},{5,7},{6,4},{7,5},{8,10},{9,11},{10,... | collective-permute-start | bytes 393224 | tf_op jit(solution)/shard_map/ppermute | solution.py:67
  111.4 10.9 %collective-permute-start.32 = (bf16[2,2,128,128]{3,2,1,0:T(8,128)(2,1)S(1)}, bf16[2,2,128,128]{3,2,1,0:T(8,128)(2,1)S(1)}, u32[]{:S(2)}, u32[]{:S(2)}) collective-permute-start(bf16[2,2,128,128]{3,2,1,0:T(8,128)(2,1)S(1)} %get-tuple-element.73), channel_id=1, source_target_pairs={{0,4},{1,5},{2,6},{3,7},{4,0},{5,1},{6,2},{7,3},{8,12},{9,13},{10,... | collective-permute-start | bytes 393224 | tf_op jit(solution)/shard_map/ppermute | solution.py:67
  112.6 9.7 %collective-permute-start.33 = (bf16[2,2,128,128]{3,2,1,0:T(8,128)(2,1)S(1)}, bf16[2,2,128,128]{3,2,1,0:T(8,128)(2,1)S(1)}, u32[]{:S(2)}, u32[]{:S(2)}) collective-permute-start(bf16[2,2,128,128]{3,2,1,0:T(8,128)(2,1)S(1)} %get-tuple-element.74), channel_id=1, source_target_pairs={{0,6},{1,7},{2,4},{3,5},{4,2},{5,3},{6,0},{7,1},{8,14},{9,15},{10,... | collective-permute-start | bytes 393224 | tf_op jit(solution)/shard_map/ppermute | solution.py:67
  116.7 7.6 %collective-permute-start.28 = (bf16[1,4,128,128]{3,2,1,0:T(8,128)(2,1)S(1)}, bf16[1,4,128,128]{3,2,1,0:T(8,128)(2,1)S(1)}, u32[]{:S(2)}, u32[]{:S(2)}) collective-permute-start(bf16[1,4,128,128]{3,2,1,0:T(8,128)(2,1)S(1)} %get-tuple-element.68), channel_id=1, source_target_pairs={{0,2},{1,3},{2,0},{3,1},{4,6},{5,7},{6,4},{7,5},{8,10},{9,11},{10,... | collective-permute-start | bytes 393224 | tf_op jit(solution)/shard_map/ppermute | solution.py:67
  116.7 10.6 %collective-permute-start.29 = (bf16[1,4,128,128]{3,2,1,0:T(8,128)(2,1)S(1)}, bf16[1,4,128,128]{3,2,1,0:T(8,128)(2,1)S(1)}, u32[]{:S(2)}, u32[]{:S(2)}) collective-permute-start(bf16[1,4,128,128]{3,2,1,0:T(8,128)(2,1)S(1)} %get-tuple-element.69), channel_id=1, source_target_pairs={{0,4},{1,5},{2,6},{3,7},{4,0},{5,1},{6,2},{7,3},{8,12},{9,13},{10,... | collective-permute-start | bytes 393224 | tf_op jit(solution)/shard_map/ppermute | solution.py:67
  118.6 8.6 %collective-permute-start.30 = (bf16[1,4,128,128]{3,2,1,0:T(8,128)(2,1)S(1)}, bf16[1,4,128,128]{3,2,1,0:T(8,128)(2,1)S(1)}, u32[]{:S(2)}, u32[]{:S(2)}) collective-permute-start(bf16[1,4,128,128]{3,2,1,0:T(8,128)(2,1)S(1)} %get-tuple-element.70), channel_id=1, source_target_pairs={{0,6},{1,7},{2,4},{3,5},{4,2},{5,3},{6,0},{7,1},{8,14},{9,15},{10,... | collective-permute-start | bytes 393224 | tf_op jit(solution)/shard_map/ppermute | solution.py:67

commit v2 on v1

--- a/solution.py
+++ b/solution.py
@@ -13,8 +13,7 @@
 HEAD_DIM = 128
 NEG = -1e30
 KEY_GROUP = 6
-QUERY_GROUP = 4
-TOGETHER = 2
+REACH = 4
 EXTRA = 8
 
 
@@ -67,94 +66,111 @@
     return lax.ppermute(value, "frame", [(i, i ^ step) for i in range(count)])
 
 
-def prep_kernel(plan, head_first, ids, x_ref, *outs):
-    hd = HEAD_DIM
-    z, a = ids[0], ids[1]
-    for p, out in enumerate(outs):
-        for c in range(out.shape[0]):
-            r, s = (p, c) if head_first else (c, p)
-            head = (z ^ r) * plan.hh + (a ^ s)
-            out[c] = x_ref[:, pl.ds(pl.multiple_of(head * hd, hd), hd)]
-
-
-def prep(plan, ids, x, head_first):
-    pieces, chunk = (plan.nz, plan.na) if head_first else (plan.na, plan.nz)
+def columns(plan, ids, r, s):
+    head = (ids[0] ^ r) * plan.hh + (ids[1] ^ s)
+    return pl.ds(pl.multiple_of(head * HEAD_DIM, HEAD_DIM), HEAD_DIM)
+
+
+def prep_query_kernel(plan, ids, x_ref, *refs):
+    outs, sems = refs[:-1], refs[-1]
+    copies = [
+        pltpu.make_async_copy(x_ref.at[:, columns(plan, ids, r, s)], outs[r].at[s], sems.at[r, s])
+        for r in range(plan.nz)
+        for s in range(plan.na)
+    ]
+    for copy in copies:
+        copy.start()
+    for copy in copies:
+        copy.wait()
+
+
+def prep_query(plan, ids, x):
     return pl.pallas_call(
-        functools.partial(prep_kernel, plan, head_first),
-        out_shape=[sds((chunk, plan.rows, HEAD_DIM), BF16)] * pieces,
-        in_specs=[SMEM, VMEM],
-        out_specs=[VMEM] * pieces,
-        cost_estimate=lasts(2),
+        functools.partial(prep_query_kernel, plan),
+        out_shape=[sds((plan.na, plan.rows, HEAD_DIM), BF16)] * plan.nz,
+        in_specs=[SMEM, pl.BlockSpec(memory_space=pl.ANY)],
+        out_specs=[VMEM] * plan.nz,
+        scratch_shapes=[pltpu.SemaphoreType.DMA((plan.nz, plan.na))],
+        cost_estimate=lasts(1),
         compiler_params=within(x, x),
+        name="prep_q",
     )(ids, x)
 
 
-def prep_grad_kernel(plan, ids, g_ref, o_ref, *outs):
-    hd, rows = HEAD_DIM, plan.rows
-    z, a = ids[0], ids[1]
-    ones = jnp.ones((EXTRA, hd), BF16)
+def prep_rest_kernel(plan, ids, k_ref, g_ref, o_ref, v_ref, *refs):
+    nz, na, rows = plan.nz, plan.na, plan.rows
+    k_outs, gv_outs, (o_all, sems, o_sem) = refs[:na], refs[na : 2 * na], refs[2 * na :]
+    spots = [(s, r) for s in range(na) for r in range(nz)]
+    behind = pl.ds(rows + EXTRA, rows)
+
+    def copy(which, ref, out, s, r):
+        return pltpu.make_async_copy(ref.at[:, columns(plan, ids, r, s)], out, sems.at[which, s, r])
+
+    k_copies = [copy(0, k_ref, k_outs[s].at[r], s, r) for s, r in spots]
+    g_copies = [copy(1, g_ref, gv_outs[s].at[r, pl.ds(0, rows)], s, r) for s, r in spots]
+    v_copies = [copy(2, v_ref, gv_outs[s].at[r, behind], s, r) for s, r in spots]
+    o_copy = pltpu.make_async_copy(o_ref, o_all, o_sem)
+    for each in k_copies:
+        each.start()
+    o_copy.start()
+    for each in g_copies + v_copies:
+        each.start()
+    ones = jnp.ones((EXTRA, HEAD_DIM), BF16)
     row = lax.broadcasted_iota(jnp.int32, (EXTRA, rows), 0)
-    for s, out in enumerate(outs):
-        for r in range(plan.nz):
-            head = (z ^ r) * plan.hh + (a ^ s)
-            cols = pl.ds(pl.multiple_of(head * hd, hd), hd)
-            grad = g_ref[:, cols]
-            out[r, :rows] = grad
-            product = grad.astype(F32) * o_ref[:, cols].astype(F32)
-            high = product.astype(BF16)
-            low = (product - high.astype(F32)).astype(BF16)
-            delta = dot(ones, high, NT) + dot(ones, low, NT)
-            first = delta.astype(BF16)
-            rest = delta - first.astype(F32)
-            second = rest.astype(BF16)
-            third = (rest - second.astype(F32)).astype(BF16)
-            parts = jnp.where(
-                row == 0,
-                first.astype(F32),
-                jnp.where(row == 1, second.astype(F32), jnp.where(row == 2, third.astype(F32), 0.0)),
-            )
-            out[r, rows:] = parts.astype(BF16)
-
-
-def prep_grad(plan, ids, g, o):
-    return pl.pallas_call(
-        functools.partial(prep_grad_kernel, plan),
-        out_shape=[sds((plan.nz, plan.rows + EXTRA, HEAD_DIM), BF16)] * plan.na,
-        in_specs=[SMEM, VMEM, VMEM],
-        out_specs=[VMEM] * plan.na,
+    for each in k_copies:
+        each.wait()
+    o_copy.wait()
+    for (s, r), each in zip(spots, g_copies):
+        each.wait()
+        grad = gv_outs[s][r, :rows]
+        product = grad.astype(F32) * o_all[:, columns(plan, ids, r, s)].astype(F32)
+        high = product.astype(BF16)
+        low = (product - high.astype(F32)).astype(BF16)
+        delta = dot(ones, high, NT) + dot(ones, low, NT)
+        first = delta.astype(BF16).astype(F32)
+        rest = delta - first
+        second = rest.astype(BF16).astype(F32)
+        parts = jnp.where(row == 2, rest - second, 0.0)
+        parts = jnp.where(row == 0, first, jnp.where(row == 1, second, parts))
+        gv_outs[s][r, rows : rows + EXTRA] = parts.astype(BF16)
+    for each in v_copies:
+        each.wait()
+
+
+def prep_rest(plan, ids, k, g, o, v):
+    outs = pl.pallas_call(
+        functools.partial(prep_rest_kernel, plan),
+        out_shape=[sds((plan.nz, plan.rows, HEAD_DIM), BF16)] * plan.na
+        + [sds((plan.nz, 2 * plan.rows + EXTRA, HEAD_DIM), BF16)] * plan.na,
+        in_specs=[SMEM] + [pl.BlockSpec(memory_space=pl.ANY)] * 4,
+        out_specs=[VMEM] * (2 * plan.na),
+        scratch_shapes=[
+            pltpu.VMEM(o.shape, BF16),
+            pltpu.SemaphoreType.DMA((3, plan.na, plan.nz)),
+            pltpu.SemaphoreType.DMA,
+        ],
         cost_estimate=lasts(2.5),
-        compiler_params=within(g, o, g),
-        name="prep_grad",
-    )(ids, g, o)
-
-
-def lists_kernel(plan, ids, order, live_ref, by_key, n_key, by_query, n_query, key_of, query_of, numbers):
-    nz, na, nb, nf = plan.nz, plan.na, plan.nb, plan.nf
+        compiler_params=within(k, g, o, v),
+        name="prep_rest",
+    )(ids, k, g, o, v)
+    return outs[: plan.na], outs[plan.na :]
+
+
+def lists_kernel(plan, ids, order, live_ref, by_key, n_key, query_of, numbers):
+    nz, na, nb = plan.nz, plan.na, plan.nb
     z, a, b = ids[0], ids[1], ids[2]
     true = [z ^ r for r in range(nz)]
 
     def at_distance(d, carry):
-        seen = [jnp.int32(0)] * nz
-        for r in range(nz):
+        for rk in range(nz):
             count = jnp.int32(0)
-            for rk in range(nz):
-                live = (live_ref[d, true[r], true[rk]] > 0).astype(jnp.int32)
-                key_of[d * nz + r, count] = jnp.int32(rk)
-                query_of[d * nz + rk, seen[rk]] = jnp.int32(r)
-                count = count + live
-                seen[rk] = seen[rk] + live
-            numbers[0, d * nz + r] = count
-        for rk in range(nz):
-            numbers[1, d * nz + rk] = seen[rk]
-        return carry
-
-    lax.fori_loop(0, nf, at_distance, 0)
-
-    def clear(i, carry):
-        n_query[i] = 0
-        return carry
-
-    lax.fori_loop(0, plan.total, clear, 0)
+            for r in range(nz):
+                query_of[d * nz + rk, count] = jnp.int32(r)
+                count = count + (live_ref[d, true[r], true[rk]] > 0).astype(jnp.int32)
+            numbers[d * nz + rk] = count
+        return carry
+
+    lax.fori_loop(1, REACH, at_distance, 0)
 
     def key_frame(s_key, carry):
         place_key = order[(a ^ s_key) * nb + b]
@@ -166,20 +182,14 @@
 
             def found(counts):
                 counts = list(counts)
-                for r in range(nz):
-                    i, row = ts * nz + r, d * nz + r
-                    seen = n_query[i]
-                    for u in range(nz):
-                        by_query[i, seen + u] = s_key * nz + key_of[row, u]
-                    n_query[i] = seen + numbers[0, row]
                 for rk in range(nz):
                     row = d * nz + rk
                     for u in range(nz):
                         by_key[s_key * nz + rk, counts[rk] + u] = ts * nz + query_of[row, u]
-                    counts[rk] = counts[rk] + numbers[1, row]
+                    counts[rk] = counts[rk] + numbers[row]
                 return tuple(counts)
 
-            return lax.cond(ts != s_key, found, lambda counts: counts, counts)
+            return lax.cond((d > 0) & (d < REACH), found, lambda counts: counts, counts)
 
         counts = lax.fori_loop(0, na * nb, query_frame, (jnp.int32(0),) * nz)
         for rk in range(nz):
@@ -190,21 +200,15 @@
 
 
 def lists(plan, ids, order, live):
-    own, total, nz, nf = plan.own, plan.total, plan.nz, plan.nf
+    own, total, nz = plan.own, plan.total, plan.nz
     return pl.pallas_call(
         functools.partial(lists_kernel, plan),
-        out_shape=[
-            sds((own, total + KEY_GROUP + nz), jnp.int32),
-            sds((own,), jnp.int32),
-            sds((total, own + QUERY_GROUP + nz), jnp.int32),
-            sds((total,), jnp.int32),
-        ],
+        out_shape=[sds((own, total + KEY_GROUP + nz), jnp.int32), sds((own,), jnp.int32)],
         in_specs=[SMEM] * 3,
-        out_specs=[SMEM] * 4,
+        out_specs=[SMEM] * 2,
         scratch_shapes=[
-            pltpu.SMEM((nf * nz, nz), jnp.int32),
-            pltpu.SMEM((nf * nz, nz), jnp.int32),
-            pltpu.SMEM((2, nf * nz), jnp.int32),
+            pltpu.SMEM((REACH * nz, nz), jnp.int32),
+            pltpu.SMEM((REACH * nz,), jnp.int32),
         ],
         cost_estimate=lasts(3),
         compiler_params=within(),
@@ -220,19 +224,28 @@
     return out
 
 
-def totals_kernel(plan, by_query, n_query, k_ref, q_ref, out, peaks, sums):
-    nz, na, nb, own, rows = plan.nz, plan.na, plan.nb, plan.own, plan.rows
+def in_groups(count, visit):
+    full = lax.div(count, KEY_GROUP)
+
+    def group(step, carry):
+        visit(step * KEY_GROUP, KEY_GROUP)
+        return carry
+
+    lax.fori_loop(0, full, group, 0)
+    left = count - full * KEY_GROUP
+    for size in range(2, KEY_GROUP + 1, 2):
+
+        @pl.when((left > size - 2) & (left <= size))
+        def _(size=size):
+            visit(full * KEY_GROUP, size)
+
+
+def totals_kernel(plan, by_key, n_key, k_ref, q_ref, out, peaks, sums):
+    nz, na, own, rows, total = plan.nz, plan.na, plan.own, plan.rows, plan.total
     scale = HEAD_DIM**-0.5
     length = nz * rows
-
-    def scores_of(i, first):
-        chosen = picks(by_query, i, n_query[i], first, QUERY_GROUP)
-        keys = jnp.concatenate([k_ref[j] for j, _ in chosen], axis=0)
-        scores = scale * dot(keys, q_ref[i], NT)
-        return [
-            jnp.where(valid, scores[u * rows : (u + 1) * rows], NEG)
-            for u, (_, valid) in enumerate(chosen)
-        ]
+    peaks[own:, :] = jnp.full((peaks.shape[0] - own, rows), NEG, F32)
+    sums[own:, :] = jnp.zeros((peaks.shape[0] - own, rows), F32)
 
     def near(s, carry):
         span = pl.ds(s * nz, nz)
@@ -246,52 +259,42 @@
         return carry
 
     lax.fori_loop(0, na, near, 0)
-    if nb > 1:
-        peaks[own:, :] = jnp.full((plan.total - own, rows), NEG, F32)
-        sums[own:, :] = jnp.zeros((plan.total - own, rows), F32)
-
-    def merged(i, parts):
-        row = pl.ds(i, 1)
-        old = peaks[row, :]
-        peak = jnp.maximum(old, jnp.max(functools.reduce(jnp.maximum, parts), axis=0, keepdims=True))
-        mass = functools.reduce(jnp.add, [jnp.exp(part - peak) for part in parts])
-        fresh = sums[row, :] * jnp.exp(old - peak) + jnp.sum(mass, axis=0, keepdims=True)
-        return peak, fresh
-
-    def keep(i, found):
-        peaks[pl.ds(i, 1), :], sums[pl.ds(i, 1), :] = found
-
-    def away(m, carry):
-        found = [(m * TOGETHER + u, merged(m * TOGETHER + u, scores_of(m * TOGETHER + u, 0))) for u in range(TOGETHER)]
-        for i, each in found:
-            keep(i, each)
-        return carry
-
-    lax.fori_loop(0, plan.total // TOGETHER, away, 0)
-
-    def rest(i, carry):
-        def group(step, carry):
-            keep(i, merged(i, scores_of(i, step * QUERY_GROUP)))
-            return carry
-
-        return lax.fori_loop(1, lax.div(n_query[i] + (QUERY_GROUP - 1), QUERY_GROUP), group, carry)
-
-    lax.fori_loop(0, plan.total, rest, 0)
-    peak = peaks[...]
-    out[...] = jnp.where(peak > 0.5 * NEG, peak + jnp.log(sums[...]), NEG)
-
-
-def totals(plan, by_query, n_query, keys, queries):
+
+    def away(j, carry):
+        def visit(start, size):
+            chosen = picks(by_key, j, n_key[j], start, size)
+            places = [pl.ds(jnp.where(ok, i, total), 1) for i, ok in chosen]
+            q = jnp.concatenate([q_ref[i] for i, _ in chosen], axis=0)
+            scores = scale * dot(k_ref[j], q, NT)
+            peak = jnp.max(scores, axis=0, keepdims=True)
+            mass = jnp.sum(jnp.exp(scores - peak), axis=0, keepdims=True)
+            old_peak = jnp.concatenate([peaks[place, :] for place in places], axis=1)
+            old_mass = jnp.concatenate([sums[place, :] for place in places], axis=1)
+            new_peak = jnp.maximum(old_peak, peak)
+            new_mass = old_mass * jnp.exp(old_peak - new_peak) + mass * jnp.exp(peak - new_peak)
+            for u, place in enumerate(places):
+                peaks[place, :] = new_peak[:, u * rows : (u + 1) * rows]
+                sums[place, :] = new_mass[:, u * rows : (u + 1) * rows]
+
+        in_groups(n_key[j], visit)
+        return carry
+
+    lax.fori_loop(0, own, away, 0)
+    peak = peaks[:total, :]
+    out[...] = jnp.where(peak > 0.5 * NEG, peak + jnp.log(sums[:total, :]), NEG)
+
+
+def totals(plan, by_key, n_key, keys, queries):
     return pl.pallas_call(
         functools.partial(totals_kernel, plan),
         out_shape=sds((plan.total, plan.rows), F32),
         in_specs=[SMEM, SMEM, VMEM, VMEM],
         out_specs=VMEM,
-        scratch_shapes=[pltpu.VMEM((plan.total, plan.rows), F32)] * 2,
-        cost_estimate=lasts(7),
+        scratch_shapes=[pltpu.VMEM((plan.total + 8, plan.rows), F32)] * 2,
+        cost_estimate=lasts(6),
         compiler_params=within(keys, queries),
         name="totals",
-    )(by_query, n_query, keys, queries)
+    )(by_key, n_key, keys, queries)
 
 
 def rows_kernel(plan, g_ref, *refs):
@@ -386,21 +389,7 @@
     def away(s, carry):
         for x, r in enumerate(span):
             j = s * nz + r
-            count = n_key[j]
-            full = lax.div(count, KEY_GROUP)
-
-            def group(step, carry, x=x, j=j):
-                add(s, x, j, step * KEY_GROUP, KEY_GROUP)
-                return carry
-
-            lax.fori_loop(0, full, group, 0)
-            left = count - full * KEY_GROUP
-            for size in range(2, KEY_GROUP + 1, 2):
-
-                @pl.when((left > size - 2) & (left <= size))
-                def _(x=x, j=j, full=full, size=size):
-                    add(s, x, j, full * KEY_GROUP, size)
-
+            in_groups(n_key[j], lambda start, size, x=x, j=j: add(s, x, j, start, size))
         return carry
 
     lax.fori_loop(0, na, away, 0)
@@ -515,19 +504,19 @@
     def flat_heads_first(by_head):
         return jnp.concatenate([p[s : s + 1] for s in range(na) for p in by_head])
 
-    q_sent = head_stage(prep(plan, ids, queries, True))
-    k_near = frame_stage(prep(plan, ids, key_states, False))
-    g_near = frame_stage(prep_grad(plan, ids, grad_out, attn_out))
-    v_near = frame_stage(prep(plan, ids, value_states, False))
-    by_key, n_key, by_query, n_query = lists(plan, ids, frame_order, block_live)
+    q_sent = head_stage(prep_query(plan, ids, queries))
+    k_near, gv_near = prep_rest(plan, ids, key_states, grad_out, attn_out, value_states)
+    k_near = frame_stage(k_near)
+    gv_near = frame_stage(gv_near)
+    by_key, n_key = lists(plan, ids, frame_order, block_live)
     keys = flat_heads_first(head_stage(regroup(k_near)))
     q_own = flat_frames_first(frame_stage(regroup(q_sent)))
     q_all = jnp.concatenate(swapped([q_own] * nb))
-    g_own = flat_heads_first(head_stage(regroup(g_near)))
+    g_own = flat_heads_first(head_stage(regroup([p[:, : plan.rows + EXTRA] for p in gv_near])))
     g_all = jnp.concatenate(swapped([g_own] * nb))
-    values = head_stage(regroup(v_near))
-
-    lse_part = totals(plan, by_query, n_query, keys, q_all)
+    values = head_stage(regroup([p[:, plan.rows + EXTRA :] for p in gv_near]))
+
+    lse_part = totals(plan, by_key, n_key, keys, q_all)
     lse, delta = query_rows(plan, g_all, swapped([lse_part] * nb))
     spans = [range(0, 2), range(2, nz)]
     kv_home, dq = [], None

time: 131 us -> 126 us (0.962)
  the two profiles are of different devices: /device:TPU:4 before, /device:TPU:0 now
where the time goes in v2:
time: 126 us; the launch traced here: 125 us
  starting transfers between devices  41.6 us (33%)
  Pallas kernels  38.6 us (31%)
  waiting for transfers between devices  37.3 us (30%)
  local copies, waits for them, and re-layouts  6.24 us (5%)
    ppermute x12, starting transfers between devices, over_head(): return lax.ppermute(value, 'head', [(i, i ^ step) for i in range(count)])  21.5 us
    ppermute x22, waiting for transfers between devices, over_frame(): return lax.ppermute(value, 'frame', [(i, i ^ step) for i in range(count)])  21.2 us
    ppermute x22, starting transfers between devices, over_frame(): return lax.ppermute(value, 'frame', [(i, i ^ step) for i in range(count)])  20.1 us
    pallas_call x2, Pallas kernels, grads(): pl.pallas_call(functools.partial(grads_kernel, plan, span, first, last),...  18 us
    ppermute x12, waiting for transfers between devices, over_head(): return lax.ppermute(value, 'head', [(i, i ^ step) for i in range(count)])  16.1 us
    pallas_call x1, Pallas kernels, totals(): pl.pallas_call(functools.partial(totals_kernel, plan), out_shape=sds((pla...  7.77 us
    unnamed x50, local copies, waits for them, and re-layouts  5.89 us
    pallas_call x1, Pallas kernels, prep_rest(): pl.pallas_call(functools.partial(prep_rest_kernel, plan), out_shape=[sds(...  4.78 us
  transfers between devices with their start and end apart: 34, of which 15 were waited for; matrix products, arithmetic and copies ran while one was open for 1% of the time, Pallas kernels for 22%

profile of v2, /device:TPU:0, one launch (start us, length us, event | category | flops | bytes accessed | tf_op | source)
XLA Modules:
  0.0 125.3 jit_solution(14148284882493450456)
XLA Ops:
  0.6 0.1 pad_add_fusion.ids
  0.7 1.0 copy-done.4
  1.8 0.9 prep_q.1
  2.7 3.1 %collective-permute-start = (bf16[4,128,128]{2,1,0:T(8,128)(2,1)S(1)}, bf16[4,128,128]{2,1,0:T(8,128)(2,1)S(1)}, u32[]{:S(2)}, u32[]{:S(2)}) collective-permute-start(bf16[4,128,128]{2,1,0:T(8,128)(2,1)S(1)} %get-tuple-element.39), channel_id=1, source_target_pairs={{0,8},{8,0},{16,24},{24,16},{1,9},{9,1},{17,25},{25,17},{2,10},{10... | collective-permute-start | bytes 393224 | tf_op jit(solution)/shard_map/ppermute | solution.py:61
  5.8 2.6 %collective-permute-start.1 = (bf16[4,128,128]{2,1,0:T(8,128)(2,1)S(1)}, bf16[4,128,128]{2,1,0:T(8,128)(2,1)S(1)}, u32[]{:S(2)}, u32[]{:S(2)}) collective-permute-start(bf16[4,128,128]{2,1,0:T(8,128)(2,1)S(1)} %get-tuple-element.40), channel_id=1, source_target_pairs={{0,16},{8,24},{16,0},{24,8},{1,17},{9,25},{17,1},{25,9},{2,18},{10... | collective-permute-start | bytes 393224 | tf_op jit(solution)/shard_map/ppermute | solution.py:61
  8.4 1.0 copy-done
  9.4 1.0 copy-done.1
  10.5 1.0 copy-done.2
  11.5 1.0 copy-done.3
  12.6 4.8 %prep_rest.1 = (bf16[4,128,128]{2,1,0:T(8,128)(2,1)S(1)}, bf16[4,128,128]{2,1,0:T(8,128)(2,1)S(1)}, bf16[4,128,128]{2,1,0:T(8,128)(2,1)S(1)}, bf16[4,128,128]{2,...) custom-call(s32[3]{0:T(128)S(1)} %pad_add_fusion.ids, ...), custom_call_target="tpu_custom_call" | custom-call | bytes 8750000 | tf_op jit(solution)/shard_map/prep_rest/pallas_call | solution.py:141
  17.4 1.8 %collective-permute-start.14 = (bf16[4,128,128]{2,1,0:T(8,128)(2,1)S(1)}, bf16[4,128,128]{2,1,0:T(8,128)(2,1)S(1)}, u32[]{:S(2)}, u32[]{:S(2)}) collective-permute-start(bf16[4,128,128]{2,1,0:T(8,128)(2,1)S(1)} %get-tuple-element.47), channel_id=1, source_target_pairs={{0,2},{1,3},{2,0},{3,1},{4,6},{5,7},{6,4},{7,5},{8,10},{9,11},{10,... | collective-permute-start | bytes 393224 | tf_op jit(solution)/shard_map/ppermute | solution.py:66
  19.1 1.5 %collective-permute-start.15 = (bf16[4,128,128]{2,1,0:T(8,128)(2,1)S(1)}, bf16[4,128,128]{2,1,0:T(8,128)(2,1)S(1)}, u32[]{:S(2)}, u32[]{:S(2)}) collective-permute-start(bf16[4,128,128]{2,1,0:T(8,128)(2,1)S(1)} %get-tuple-element.48), channel_id=1, source_target_pairs={{0,4},{1,5},{2,6},{3,7},{4,0},{5,1},{6,2},{7,3},{8,12},{9,13},{10,... | collective-permute-start | bytes 393224 | tf_op jit(solution)/shard_map/ppermute | solution.py:66
  20.6 0.1 copy.10.live_ref
  20.8 3.6 %lists.1 = (s32[16,42]{1,0:T(8,128)S(1)}, s32[16]{0:T(128)S(1)}) custom-call(s32[3]{0:T(128)S(1)} %pad_add_fusion.ids, s32[8]{0:T(128)S(1)} %copy-done.5, s32[8,4,4]{2,1,0:T(4,128)S(1)} %copy.10.live_ref), custom_call_target="tpu_custom_call" | custom-call | bytes 10500000 | tf_op jit(solution)/shard_map/lists/pallas_call | solution.py:204
  24.5 0.3 collective-permute-start.16
  24.8 1.8 %collective-permute-start.7 = (bf16[4,264,128]{2,1,0:T(8,128)(2,1)S(1)}, bf16[4,264,128]{2,1,0:T(8,128)(2,1)S(1)}, u32[]{:S(2)}, u32[]{:S(2)}) collective-permute-start(bf16[4,264,128]{2,1,0:T(8,128)(2,1)S(1)} %get-tuple-element.43), channel_id=1, source_target_pairs={{0,2},{1,3},{2,0},{3,1},{4,6},{5,7},{6,4},{7,5},{8,10},{9,11},{10,... | collective-permute-start | bytes 811016 | tf_op jit(solution)/shard_map/ppermute | solution.py:66
  26.7 1.6 %collective-permute-start.8 = (bf16[4,264,128]{2,1,0:T(8,128)(2,1)S(1)}, bf16[4,264,128]{2,1,0:T(8,128)(2,1)S(1)}, u32[]{:S(2)}, u32[]{:S(2)}) collective-permute-start(bf16[4,264,128]{2,1,0:T(8,128)(2,1)S(1)} %get-tuple-element.44), channel_id=1, source_target_pairs={{0,4},{1,5},{2,6},{3,7},{4,0},{5,1},{6,2},{7,3},{8,12},{9,13},{10,... | collective-permute-start | bytes 811016 | tf_op jit(solution)/shard_map/ppermute | solution.py:66
  28.3 0.3 collective-permute-start.9
  28.6 1.8 %collective-permute-start.3 = (bf16[4,128,128]{2,1,0:T(8,128)(2,1)S(1)}, bf16[4,128,128]{2,1,0:T(8,128)(2,1)S(1)}, u32[]{:S(2)}, u32[]{:S(2)}) collective-permute-start(bf16[4,128,128]{2,1,0:T(8,128)(2,1)S(1)} %pad_maximum_fusion.3), channel_id=1, source_target_pairs={{0,2},{1,3},{2,0},{3,1},{4,6},{5,7},{6,4},{7,5},{8,10},{9,11},{10,... | collective-permute-start | bytes 393224 | tf_op jit(solution)/shard_map/ppermute | solution.py:66
  30.4 1.4 %collective-permute-done.16 = bf16[4,128,128]{2,1,0:T(8,128)(2,1)S(1)} collective-permute-done((bf16[4,128,128]{2,1,0:T(8,128)(2,1)S(1)}, bf16[4,128,128]{2,1,0:T(8,128)(2,1)S(1)}, u32[]{:S(2)}, u32[]{:S(2)}) %collective-permute-start.16) | collective-permute-done | bytes 131104 | tf_op jit(solution)/shard_map/ppermute | solution.py:66
  31.9 0.7 collective-permute-start.17
  32.7 4.2 %collective-permute-done.17 = bf16[4,128,128]{2,1,0:T(8,128)(2,1)S(1)} collective-permute-done((bf16[4,128,128]{2,1,0:T(8,128)(2,1)S(1)}, bf16[4,128,128]{2,1,0:T(8,128)(2,1)S(1)}, u32[]{:S(2)}, u32[]{:S(2)}) %collective-permute-start.17) | collective-permute-done | bytes 131104 | tf_op jit(solution)/shard_map/ppermute | solution.py:61
  36.9 0.5 collective-permute-start.4
  37.4 5.4 %collective-permute-done.3 = bf16[4,128,128]{2,1,0:T(8,128)(2,1)S(1)} collective-permute-done((bf16[4,128,128]{2,1,0:T(8,128)(2,1)S(1)}, bf16[4,128,128]{2,1,0:T(8,128)(2,1)S(1)}, u32[]{:S(2)}, u32[]{:S(2)}) %collective-permute-start.3) | collective-permute-done | bytes 131104 | tf_op jit(solution)/shard_map/ppermute | solution.py:66
  42.8 1.5 %collective-permute-start.5 = (bf16[4,128,128]{2,1,0:T(8,128)(2,1)S(1)}, bf16[4,128,128]{2,1,0:T(8,128)(2,1)S(1)}, u32[]{:S(2)}, u32[]{:S(2)}) collective-permute-start(bf16[4,128,128]{2,1,0:T(8,128)(2,1)S(1)} %pad_maximum_fusion.5), channel_id=1, source_target_pairs={{0,6},{1,7},{2,4},{3,5},{4,2},{5,3},{6,0},{7,1},{8,14},{9,15},{10,... | collective-permute-start | bytes 393224 | tf_op jit(solution)/shard_map/ppermute | solution.py:66
  44.3 1.7 %collective-permute-start.18 = (bf16[4,128,128]{2,1,0:T(8,128)(2,1)S(1)}, bf16[4,128,128]{2,1,0:T(8,128)(2,1)S(1)}, u32[]{:S(2)}, u32[]{:S(2)}) collective-permute-start(bf16[4,128,128]{2,1,0:T(8,128)(2,1)S(1)} %pad_maximum_fusion.7), channel_id=1, source_target_pairs={{0,16},{8,24},{16,0},{24,8},{1,17},{9,25},{17,1},{25,9},{2,18},{10... | collective-permute-start | bytes 393224 | tf_op jit(solution)/shard_map/ppermute | solution.py:61
  46.1 2.6 %collective-permute-done.5 = bf16[4,128,128]{2,1,0:T(8,128)(2,1)S(1)} collective-permute-done((bf16[4,128,128]{2,1,0:T(8,128)(2,1)S(1)}, bf16[4,128,128]{2,1,0:T(8,128)(2,1)S(1)}, u32[]{:S(2)}, u32[]{:S(2)}) %collective-permute-start.5) | collective-permute-done | bytes 131104 | tf_op jit(solution)/shard_map/ppermute | solution.py:66
  48.7 3.5 %collective-permute-start.19 = (bf16[4,128,128]{2,1,0:T(8,128)(2,1)S(1)}, bf16[4,128,128]{2,1,0:T(8,128)(2,1)S(1)}, u32[]{:S(2)}, u32[]{:S(2)}) collective-permute-start(bf16[4,128,128]{2,1,0:T(8,128)(2,1)S(1)} %pad_maximum_fusion.8), channel_id=1, source_target_pairs={{0,24},{8,16},{16,8},{24,0},{1,25},{9,17},{17,9},{25,1},{2,26},{10... | collective-permute-start | bytes 393224 | tf_op jit(solution)/shard_map/ppermute | solution.py:61
  52.3 1.4 %collective-permute-done.18 = bf16[4,128,128]{2,1,0:T(8,128)(2,1)S(1)} collective-permute-done((bf16[4,128,128]{2,1,0:T(8,128)(2,1)S(1)}, bf16[4,128,128]{2,1,0:T(8,128)(2,1)S(1)}, u32[]{:S(2)}, u32[]{:S(2)}) %collective-permute-start.18) | collective-permute-done | bytes 131104 | tf_op jit(solution)/shard_map/ppermute | solution.py:61
  53.7 1.8 %collective-permute-done.19 = bf16[4,128,128]{2,1,0:T(8,128)(2,1)S(1)} collective-permute-done((bf16[4,128,128]{2,1,0:T(8,128)(2,1)S(1)}, bf16[4,128,128]{2,1,0:T(8,128)(2,1)S(1)}, u32[]{:S(2)}, u32[]{:S(2)}) %collective-permute-start.19) | collective-permute-done | bytes 131104 | tf_op jit(solution)/shard_map/ppermute | solution.py:61
  55.8 1.6 %collective-permute-start.10 = (bf16[4,136,128]{2,1,0:T(8,128)(2,1)S(1)}, bf16[4,136,128]{2,1,0:T(8,128)(2,1)S(1)}, u32[]{:S(2)}, u32[]{:S(2)}) collective-permute-start(bf16[4,136,128]{2,1,0:T(8,128)(2,1)S(1)} %pad_maximum_fusion), channel_id=1, source_target_pairs={{0,8},{8,0},{16,24},{24,16},{1,9},{9,1},{17,25},{25,17},{2,10},{10... | collective-permute-start | bytes 417800 | tf_op jit(solution)/shard_map/ppermute | solution.py:61
  57.5 2.6 %collective-permute-start.11 = (bf16[4,136,128]{2,1,0:T(8,128)(2,1)S(1)}, bf16[4,136,128]{2,1,0:T(8,128)(2,1)S(1)}, u32[]{:S(2)}, u32[]{:S(2)}) collective-permute-start(bf16[4,136,128]{2,1,0:T(8,128)(2,1)S(1)} %pad_maximum_fusion.1), channel_id=1, source_target_pairs={{0,16},{8,24},{16,0},{24,8},{1,17},{9,25},{17,1},{25,9},{2,18},{10... | collective-permute-start | bytes 417800 | tf_op jit(solution)/shard_map/ppermute | solution.py:61
  60.1 0.8 collective-permute-start.12
  61.0 0.9 collective-permute-done.10
  61.9 7.6 %collective-permute-done.11 = bf16[4,136,128]{2,1,0:T(8,128)(2,1)S(1)} collective-permute-done((bf16[4,136,128]{2,1,0:T(8,128)(2,1)S(1)}, bf16[4,136,128]{2,1,0:T(8,128)(2,1)S(1)}, u32[]{:S(2)}, u32[]{:S(2)}) %collective-permute-start.11) | collective-permute-done | bytes 139296 | tf_op jit(solution)/shard_map/ppermute | solution.py:61
  69.7 0.1 collective-permute-start.13
  69.8 3.2 %collective-permute-start.21 = (bf16[4,128,128]{2,1,0:T(8,128)(2,1)S(1)}, bf16[4,128,128]{2,1,0:T(8,128)(2,1)S(1)}, u32[]{:S(2)}, u32[]{:S(2)}) collective-permute-start(bf16[4,128,128]{2,1,0:T(8,128)(2,1)S(1)} %pad_maximum_fusion.9), channel_id=1, source_target_pairs={{0,16},{8,24},{16,0},{24,8},{1,17},{9,25},{17,1},{25,9},{2,18},{10... | collective-permute-start | bytes 393224 | tf_op jit(solution)/shard_map/ppermute | solution.py:61
  73.1 1.5 %collective-permute-start.22 = (bf16[4,128,128]{2,1,0:T(8,128)(2,1)S(1)}, bf16[4,128,128]{2,1,0:T(8,128)(2,1)S(1)}, u32[]{:S(2)}, u32[]{:S(2)}) collective-permute-start(bf16[4,128,128]{2,1,0:T(8,128)(2,1)S(1)} %pad_maximum_fusion.10), channel_id=1, source_target_pairs={{0,24},{8,16},{16,8},{24,0},{1,25},{9,17},{17,9},{25,1},{2,26},{10... | collective-permute-start | bytes 393224 | tf_op jit(solution)/shard_map/ppermute | solution.py:61
  74.6 0.1 collective-permute-start.23
  74.7 0.1 constant_dynamic-update-slice_fusion.7.q_ref
  74.8 7.8 %totals.1.refs_0_ = f32[32,128]{1,0:T(8,128)S(1)} custom-call(s32[16,42]{1,0:T(8,128)S(1)} %get-tuple-element.36.by_key, s32[16]{0:T(128)S(1)} %get-tuple-element.37.n_key, bf16[16,128,128]{2,1,0:T(8,128)(2,1)S(1)} %constant_dynamic-update-slice_fusion.48.k_ref, bf16[32,128,128]{2,1,0:T(8,128)(2,1)S(1)} %constant_dynamic-update-slice_fusion.7.q_ref), custom_call_target="tpu_custom_call" | custom-call | bytes 21000000 | tf_op jit(solution)/shard_map/totals/pallas_call | solution.py:288
  82.5 0.1 collective-permute-start.20
  82.6 0.1 constant_dynamic-update-slice_fusion.31.g_ref
  82.7 1.1 collective-permute-done.20.refs_1_
  83.8 0.3 query_rows.1
  84.1 0.3 collective-permute-done.23.refs_1_
  84.4 8.7 %shard_map.94 = (bf16[2,2,128,128]{3,2,1,0:T(8,128)(2,1)S(1)}, bf16[2,2,128,128]{3,2,1,0:T(8,128)(2,1)S(1)}, bf16[2,2,128,128]{3,2,1,0:T(8,128)(2,1)S(1)}, bf16[...) custom-call(s32[16,42]{1,0:T(8,128)S(1)} %get-tuple-element.36.by_key, s32[16]{0:T(128)S(1)} %get-tuple-element.37.n_key, ...), custom_call_target="tpu_custom_call" | custom-call | bytes 24500000 | tf_op jit(solution)/shard_map/pallas_call | solution.py:418
  93.0 9.3 %shard_map.95 = (bf16[2,2,128,128]{3,2,1,0:T(8,128)(2,1)S(1)}, bf16[2,2,128,128]{3,2,1,0:T(8,128)(2,1)S(1)}, bf16[2,2,128,128]{3,2,1,0:T(8,128)(2,1)S(1)}, bf16[...) custom-call(s32[16,42]{1,0:T(8,128)S(1)} %get-tuple-element.36.by_key, ...), custom_call_target="tpu_custom_call" | custom-call | bytes 24500000 | tf_op jit(solution)/shard_map/pallas_call | solution.py:418
  102.3 0.1 collective-permute-start.24
  102.4 1.9 %collective-permute-start.31 = (bf16[2,2,128,128]{3,2,1,0:T(8,128)(2,1)S(1)}, bf16[2,2,128,128]{3,2,1,0:T(8,128)(2,1)S(1)}, u32[]{:S(2)}, u32[]{:S(2)}) collective-permute-start(bf16[2,2,128,128]{3,2,1,0:T(8,128)(2,1)S(1)} %get-tuple-element.64), channel_id=1, source_target_pairs={{0,2},{1,3},{2,0},{3,1},{4,6},{5,7},{6,4},{7,5},{8,10},{9,11},{10,... | collective-permute-start | bytes 393224 | tf_op jit(solution)/shard_map/ppermute | solution.py:66
  104.3 1.7 %collective-permute-start.33 = (bf16[2,2,128,128]{3,2,1,0:T(8,128)(2,1)S(1)}, bf16[2,2,128,128]{3,2,1,0:T(8,128)(2,1)S(1)}, u32[]{:S(2)}, u32[]{:S(2)}) collective-permute-start(bf16[2,2,128,128]{3,2,1,0:T(8,128)(2,1)S(1)} %get-tuple-element.66), channel_id=1, source_target_pairs={{0,6},{1,7},{2,4},{3,5},{4,2},{5,3},{6,0},{7,1},{8,14},{9,15},{10,... | collective-permute-start | bytes 393224 | tf_op jit(solution)/shard_map/ppermute | solution.py:66
  106.0 1.8 %collective-permute-start.28 = (bf16[2,2,128,128]{3,2,1,0:T(8,128)(2,1)S(1)}, bf16[2,2,128,128]{3,2,1,0:T(8,128)(2,1)S(1)}, u32[]{:S(2)}, u32[]{:S(2)}) collective-permute-start(bf16[2,2,128,128]{3,2,1,0:T(8,128)(2,1)S(1)} %get-tuple-element.60), channel_id=1, source_target_pairs={{0,2},{1,3},{2,0},{3,1},{4,6},{5,7},{6,4},{7,5},{8,10},{9,11},{10,... | collective-permute-start | bytes 393224 | tf_op jit(solution)/shard_map/ppermute | solution.py:66
  107.8 0.2 pack.1
  108.0 0.5 collective-permute-done.31.refs_5_
  108.5 1.2 collective-permute-start.30
  109.7 3.6 %collective-permute-done.32.refs_6_ = bf16[2,2,128,128]{3,2,1,0:T(8,128)(2,1)S(1)} collective-permute-done((bf16[2,2,128,128]{3,2,1,0:T(8,128)(2,1)S(1)}, bf16[2,2,128,128]{3,2,1,0:T(8,128)(2,1)S(1)}, u32[]{:S(2)}, u32[]{:S(2)}) %collective-permute-start.32) | collective-permute-done | bytes 131104 | tf_op jit(solution)/shard_map/ppermute | solution.py:66
  113.4 0.2 collective-permute-start.25
  113.6 0.1 collective-permute-start.26
  113.7 1.3 %collective-permute-done.28.refs_1_ = bf16[2,2,128,128]{3,2,1,0:T(8,128)(2,1)S(1)} collective-permute-done((bf16[2,2,128,128]{3,2,1,0:T(8,128)(2,1)S(1)}, bf16[2,2,128,128]{3,2,1,0:T(8,128)(2,1)S(1)}, u32[]{:S(2)}, u32[]{:S(2)}) %collective-permute-start.28) | collective-permute-done | bytes 131104 | tf_op jit(solution)/shard_map/ppermute | solution.py:66
  115.0 1.8 %collective-permute-start.27 = (bf16[1,4,128,128]{3,2,1,0:T(8,128)(2,1)S(1)}, bf16[1,4,128,128]{3,2,1,0:T(8,128)(2,1)S(1)}, u32[]{:S(2)}, u32[]{:S(2)}) collective-permute-start(bf16[1,4,128,128]{3,2,1,0:T(8,128)(2,1)S(1)} %get-tuple-element.58), channel_id=1, source_target_pairs={{0,6},{1,7},{2,4},{3,5},{4,2},{5,3},{6,0},{7,1},{8,14},{9,15},{10,... | collective-permute-start | bytes 393224 | tf_op jit(solution)/shard_map/ppermute | solution.py:66
  116.9 2.1 %collective-permute-done.29.refs_2_ = bf16[2,2,128,128]{3,2,1,0:T(8,128)(2,1)S(1)} collective-permute-done((bf16[2,2,128,128]{3,2,1,0:T(8,128)(2,1)S(1)}, bf16[2,2,128,128]{3,2,1,0:T(8,128)(2,1)S(1)}, u32[]{:S(2)}, u32[]{:S(2)}) %collective-permute-start.29) | collective-permute-done | bytes 131104 | tf_op jit(solution)/shard_map/ppermute | solution.py:66
  119.0 1.7 %shard_map.97 = (bf16[512,512]{1,0:T(8,128)(2,1)}, bf16[512,512]{1,0:T(8,128)(2,1)}) custom-call(s32[3]{0:T(128)S(1)} %pad_add_fusion.ids, bf16[2,2,128,128]{3,2,1,0:T(8,128)(2,1)S(1)} %get-tuple-element.59.refs_0_, bf16[2,2,128,128]{3,2,1,0:T(8,128)(2,1)S(1)} %collective-permute-done.28.refs_1_, ...), custom_call_target="tpu_custom_call" | custom-call | bytes 5250000 | tf_op jit(solution)/shard_map/pallas_call | solution.py:467
  120.7 3.2 %collective-permute-done.26.refs_2_ = bf16[1,4,128,128]{3,2,1,0:T(8,128)(2,1)S(1)} collective-permute-done((bf16[1,4,128,128]{3,2,1,0:T(8,128)(2,1)S(1)}, bf16[1,4,128,128]{3,2,1,0:T(8,128)(2,1)S(1)}, u32[]{:S(2)}, u32[]{:S(2)}) %collective-permute-start.26) | collective-permute-done | bytes 131104 | tf_op jit(solution)/shard_map/ppermute | solution.py:66
  123.8 1.4 %shard_map.96 = bf16[512,512]{1,0:T(8,128)(2,1)} custom-call(s32[3]{0:T(128)S(1)} %pad_add_fusion.ids, bf16[1,4,128,128]{3,2,1,0:T(8,128)(2,1)S(1)} %get-tuple-element.55.refs_0_, bf16[1,4,128,128]{3,2,1,0:T(8,128)(2,1)S(1)} %collective-permute-done.25.refs_1_, bf16[1,4,128,128]{3,2,1,0:T(8,128)(2,1)S(1)} %collective-permute-done.26.refs_2_, ...), custom_call_target="tpu_custom_call" | custom-call | bytes 5250000 | tf_op jit(solution)/shard_map/pallas_call | solution.py:467
  (93 shorter events, 1.1 us)
Async XLA Ops:
  0.7 1.0 copy-start.4
  1.8 18.9 %copy-start.6 = (s32[8,4,4]{0,2,1:T(4,128)S(1)}, s32[8,4,4]{0,2,1:T(4,128)}, u32[]{:S(2)}) copy-start(s32[8,4,4]{0,2,1:T(4,128)} %param.13) | copy-start | bytes 1540
  2.7 21.8 %collective-permute-start = (bf16[4,128,128]{2,1,0:T(8,128)(2,1)S(1)}, bf16[4,128,128]{2,1,0:T(8,128)(2,1)S(1)}, u32[]{:S(2)}, u32[]{:S(2)}) collective-permute-start(bf16[4,128,128]{2,1,0:T(8,128)(2,1)S(1)} %get-tuple-element.39), channel_id=1, source_target_pairs={{0,8},{8,0},{16,24},{24,16},{1,9},{9,1},{17,25},{25,17},{2,10},{10... | collective-permute-start | bytes 393224 | tf_op jit(solution)/shard_map/ppermute | solution.py:61
  5.8 19.0 %collective-permute-start.1 = (bf16[4,128,128]{2,1,0:T(8,128)(2,1)S(1)}, bf16[4,128,128]{2,1,0:T(8,128)(2,1)S(1)}, u32[]{:S(2)}, u32[]{:S(2)}) collective-permute-start(bf16[4,128,128]{2,1,0:T(8,128)(2,1)S(1)} %get-tuple-element.40), channel_id=1, source_target_pairs={{0,16},{8,24},{16,0},{24,8},{1,17},{9,25},{17,1},{25,9},{2,18},{10... | collective-permute-start | bytes 393224 | tf_op jit(solution)/shard_map/ppermute | solution.py:61
  8.4 18.3 %collective-permute-start.2 = (bf16[4,128,128]{2,1,0:T(8,128)(2,1)S(1)}, bf16[4,128,128]{2,1,0:T(8,128)(2,1)S(1)}, u32[]{:S(2)}, u32[]{:S(2)}) collective-permute-start(bf16[4,128,128]{2,1,0:T(8,128)(2,1)S(1)} %get-tuple-element.41), channel_id=1, source_target_pairs={{0,24},{8,16},{16,8},{24,0},{1,25},{9,17},{17,9},{25,1},{2,26},{10... | collective-permute-start | bytes 393224 | tf_op jit(solution)/shard_map/ppermute | solution.py:61
  8.4 1.0 copy-start
  9.4 1.0 copy-start.1
  10.5 1.0 copy-start.2
  11.5 1.0 copy-start.3
  12.6 8.3 %copy-start.5 = (s32[8]{0:T(128)S(1)}, s32[8]{0:T(128)}, u32[]{:S(2)}) copy-start(s32[8]{0:T(128)} %order.1) | copy-start | bytes 100
  17.4 10.9 %collective-permute-start.14 = (bf16[4,128,128]{2,1,0:T(8,128)(2,1)S(1)}, bf16[4,128,128]{2,1,0:T(8,128)(2,1)S(1)}, u32[]{:S(2)}, u32[]{:S(2)}) collective-permute-start(bf16[4,128,128]{2,1,0:T(8,128)(2,1)S(1)} %get-tuple-element.47), channel_id=1, source_target_pairs={{0,2},{1,3},{2,0},{3,1},{4,6},{5,7},{6,4},{7,5},{8,10},{9,11},{10,... | collective-permute-start | bytes 393224 | tf_op jit(solution)/shard_map/ppermute | solution.py:66
  19.1 9.5 %collective-permute-start.15 = (bf16[4,128,128]{2,1,0:T(8,128)(2,1)S(1)}, bf16[4,128,128]{2,1,0:T(8,128)(2,1)S(1)}, u32[]{:S(2)}, u32[]{:S(2)}) collective-permute-start(bf16[4,128,128]{2,1,0:T(8,128)(2,1)S(1)} %get-tuple-element.48), channel_id=1, source_target_pairs={{0,4},{1,5},{2,6},{3,7},{4,0},{5,1},{6,2},{7,3},{8,12},{9,13},{10,... | collective-permute-start | bytes 393224 | tf_op jit(solution)/shard_map/ppermute | solution.py:66
  24.5 7.3 %collective-permute-start.16 = (bf16[4,128,128]{2,1,0:T(8,128)(2,1)S(1)}, bf16[4,128,128]{2,1,0:T(8,128)(2,1)S(1)}, u32[]{:S(2)}, u32[]{:S(2)}) collective-permute-start(bf16[4,128,128]{2,1,0:T(8,128)(2,1)S(1)} %get-tuple-element.49), channel_id=1, source_target_pairs={{0,6},{1,7},{2,4},{3,5},{4,2},{5,3},{6,0},{7,1},{8,14},{9,15},{10,... | collective-permute-start | bytes 393224 | tf_op jit(solution)/shard_map/ppermute | solution.py:66
  24.8 30.9 %collective-permute-start.7 = (bf16[4,264,128]{2,1,0:T(8,128)(2,1)S(1)}, bf16[4,264,128]{2,1,0:T(8,128)(2,1)S(1)}, u32[]{:S(2)}, u32[]{:S(2)}) collective-permute-start(bf16[4,264,128]{2,1,0:T(8,128)(2,1)S(1)} %get-tuple-element.43), channel_id=1, source_target_pairs={{0,2},{1,3},{2,0},{3,1},{4,6},{5,7},{6,4},{7,5},{8,10},{9,11},{10,... | collective-permute-start | bytes 811016 | tf_op jit(solution)/shard_map/ppermute | solution.py:66
  26.7 29.1 %collective-permute-start.8 = (bf16[4,264,128]{2,1,0:T(8,128)(2,1)S(1)}, bf16[4,264,128]{2,1,0:T(8,128)(2,1)S(1)}, u32[]{:S(2)}, u32[]{:S(2)}) collective-permute-start(bf16[4,264,128]{2,1,0:T(8,128)(2,1)S(1)} %get-tuple-element.44), channel_id=1, source_target_pairs={{0,4},{1,5},{2,6},{3,7},{4,0},{5,1},{6,2},{7,3},{8,12},{9,13},{10,... | collective-permute-start | bytes 811016 | tf_op jit(solution)/shard_map/ppermute | solution.py:66
  28.3 27.5 %collective-permute-start.9 = (bf16[4,264,128]{2,1,0:T(8,128)(2,1)S(1)}, bf16[4,264,128]{2,1,0:T(8,128)(2,1)S(1)}, u32[]{:S(2)}, u32[]{:S(2)}) collective-permute-start(bf16[4,264,128]{2,1,0:T(8,128)(2,1)S(1)} %get-tuple-element.45), channel_id=1, source_target_pairs={{0,6},{1,7},{2,4},{3,5},{4,2},{5,3},{6,0},{7,1},{8,14},{9,15},{10,... | collective-permute-start | bytes 811016 | tf_op jit(solution)/shard_map/ppermute | solution.py:66
  28.6 14.1 %collective-permute-start.3 = (bf16[4,128,128]{2,1,0:T(8,128)(2,1)S(1)}, bf16[4,128,128]{2,1,0:T(8,128)(2,1)S(1)}, u32[]{:S(2)}, u32[]{:S(2)}) collective-permute-start(bf16[4,128,128]{2,1,0:T(8,128)(2,1)S(1)} %pad_maximum_fusion.3), channel_id=1, source_target_pairs={{0,2},{1,3},{2,0},{3,1},{4,6},{5,7},{6,4},{7,5},{8,10},{9,11},{10,... | collective-permute-start | bytes 393224 | tf_op jit(solution)/shard_map/ppermute | solution.py:66
  31.9 5.0 %collective-permute-start.17 = (bf16[4,128,128]{2,1,0:T(8,128)(2,1)S(1)}, bf16[4,128,128]{2,1,0:T(8,128)(2,1)S(1)}, u32[]{:S(2)}, u32[]{:S(2)}) collective-permute-start(bf16[4,128,128]{2,1,0:T(8,128)(2,1)S(1)} %pad_maximum_fusion.6), channel_id=1, source_target_pairs={{0,8},{8,0},{16,24},{24,16},{1,9},{9,1},{17,25},{25,17},{2,10},{10... | collective-permute-start | bytes 393224 | tf_op jit(solution)/shard_map/ppermute | solution.py:61
  36.9 7.4 %collective-permute-start.4 = (bf16[4,128,128]{2,1,0:T(8,128)(2,1)S(1)}, bf16[4,128,128]{2,1,0:T(8,128)(2,1)S(1)}, u32[]{:S(2)}, u32[]{:S(2)}) collective-permute-start(bf16[4,128,128]{2,1,0:T(8,128)(2,1)S(1)} %pad_maximum_fusion.4), channel_id=1, source_target_pairs={{0,4},{1,5},{2,6},{3,7},{4,0},{5,1},{6,2},{7,3},{8,12},{9,13},{10,... | collective-permute-start | bytes 393224 | tf_op jit(solution)/shard_map/ppermute | solution.py:66
  42.8 5.9 %collective-permute-start.5 = (bf16[4,128,128]{2,1,0:T(8,128)(2,1)S(1)}, bf16[4,128,128]{2,1,0:T(8,128)(2,1)S(1)}, u32[]{:S(2)}, u32[]{:S(2)}) collective-permute-start(bf16[4,128,128]{2,1,0:T(8,128)(2,1)S(1)} %pad_maximum_fusion.5), channel_id=1, source_target_pairs={{0,6},{1,7},{2,4},{3,5},{4,2},{5,3},{6,0},{7,1},{8,14},{9,15},{10,... | collective-permute-start | bytes 393224 | tf_op jit(solution)/shard_map/ppermute | solution.py:66
  44.3 9.3 %collective-permute-start.18 = (bf16[4,128,128]{2,1,0:T(8,128)(2,1)S(1)}, bf16[4,128,128]{2,1,0:T(8,128)(2,1)S(1)}, u32[]{:S(2)}, u32[]{:S(2)}) collective-permute-start(bf16[4,128,128]{2,1,0:T(8,128)(2,1)S(1)} %pad_maximum_fusion.7), channel_id=1, source_target_pairs={{0,16},{8,24},{16,0},{24,8},{1,17},{9,25},{17,1},{25,9},{2,18},{10... | collective-permute-start | bytes 393224 | tf_op jit(solution)/shard_map/ppermute | solution.py:61
  48.7 6.9 %collective-permute-start.19 = (bf16[4,128,128]{2,1,0:T(8,128)(2,1)S(1)}, bf16[4,128,128]{2,1,0:T(8,128)(2,1)S(1)}, u32[]{:S(2)}, u32[]{:S(2)}) collective-permute-start(bf16[4,128,128]{2,1,0:T(8,128)(2,1)S(1)} %pad_maximum_fusion.8), channel_id=1, source_target_pairs={{0,24},{8,16},{16,8},{24,0},{1,25},{9,17},{17,9},{25,1},{2,26},{10... | collective-permute-start | bytes 393224 | tf_op jit(solution)/shard_map/ppermute | solution.py:61
  53.7 21.0 %collective-permute-start.6 = (bf16[16,128,128]{2,1,0:T(8,128)(2,1)S(1)}, bf16[16,128,128]{2,1,0:T(8,128)(2,1)S(1)}, u32[]{:S(2)}, u32[]{:S(2)}) collective-permute-start(bf16[16,128,128]{2,1,0:T(8,128)(2,1)S(1)} %get-tuple-element.142), channel_id=1, source_target_pairs={{0,1},{1,0},{2,3},{3,2},{4,5},{5,4},{6,7},{7,6},{8,9},{9,8},{10,11... | collective-permute-start | bytes 1572872 | tf_op jit(solution)/shard_map/ppermute | solution.py:66
  55.8 6.0 %collective-permute-start.10 = (bf16[4,136,128]{2,1,0:T(8,128)(2,1)S(1)}, bf16[4,136,128]{2,1,0:T(8,128)(2,1)S(1)}, u32[]{:S(2)}, u32[]{:S(2)}) collective-permute-start(bf16[4,136,128]{2,1,0:T(8,128)(2,1)S(1)} %pad_maximum_fusion), channel_id=1, source_target_pairs={{0,8},{8,0},{16,24},{24,16},{1,9},{9,1},{17,25},{25,17},{2,10},{10... | collective-permute-start | bytes 417800 | tf_op jit(solution)/shard_map/ppermute | solution.py:61
  57.5 12.0 %collective-permute-start.11 = (bf16[4,136,128]{2,1,0:T(8,128)(2,1)S(1)}, bf16[4,136,128]{2,1,0:T(8,128)(2,1)S(1)}, u32[]{:S(2)}, u32[]{:S(2)}) collective-permute-start(bf16[4,136,128]{2,1,0:T(8,128)(2,1)S(1)} %pad_maximum_fusion.1), channel_id=1, source_target_pairs={{0,16},{8,24},{16,0},{24,8},{1,17},{9,25},{17,1},{25,9},{2,18},{10... | collective-permute-start | bytes 417800 | tf_op jit(solution)/shard_map/ppermute | solution.py:61
  60.1 9.3 %collective-permute-start.12 = (bf16[4,136,128]{2,1,0:T(8,128)(2,1)S(1)}, bf16[4,136,128]{2,1,0:T(8,128)(2,1)S(1)}, u32[]{:S(2)}, u32[]{:S(2)}) collective-permute-start(bf16[4,136,128]{2,1,0:T(8,128)(2,1)S(1)} %pad_maximum_fusion.2), channel_id=1, source_target_pairs={{0,24},{8,16},{16,8},{24,0},{1,25},{9,17},{17,9},{25,1},{2,26},{10... | collective-permute-start | bytes 417800 | tf_op jit(solution)/shard_map/ppermute | solution.py:61
  69.7 12.9 %collective-permute-start.13 = (bf16[16,136,128]{2,1,0:T(8,128)(2,1)S(1)}, bf16[16,136,128]{2,1,0:T(8,128)(2,1)S(1)}, u32[]{:S(2)}, u32[]{:S(2)}) collective-permute-start(bf16[16,136,128]{2,1,0:T(8,128)(2,1)S(1)} %get-tuple-element.105), channel_id=1, source_target_pairs={{0,1},{1,0},{2,3},{3,2},{4,5},{5,4},{6,7},{7,6},{8,9},{9,8},{10,11... | collective-permute-start | bytes 1671176 | tf_op jit(solution)/shard_map/ppermute | solution.py:66
  69.8 23.2 %collective-permute-start.21 = (bf16[4,128,128]{2,1,0:T(8,128)(2,1)S(1)}, bf16[4,128,128]{2,1,0:T(8,128)(2,1)S(1)}, u32[]{:S(2)}, u32[]{:S(2)}) collective-permute-start(bf16[4,128,128]{2,1,0:T(8,128)(2,1)S(1)} %pad_maximum_fusion.9), channel_id=1, source_target_pairs={{0,16},{8,24},{16,0},{24,8},{1,17},{9,25},{17,1},{25,9},{2,18},{10... | collective-permute-start | bytes 393224 | tf_op jit(solution)/shard_map/ppermute | solution.py:61
  73.1 20.0 %collective-permute-start.22 = (bf16[4,128,128]{2,1,0:T(8,128)(2,1)S(1)}, bf16[4,128,128]{2,1,0:T(8,128)(2,1)S(1)}, u32[]{:S(2)}, u32[]{:S(2)}) collective-permute-start(bf16[4,128,128]{2,1,0:T(8,128)(2,1)S(1)} %pad_maximum_fusion.10), channel_id=1, source_target_pairs={{0,24},{8,16},{16,8},{24,0},{1,25},{9,17},{17,9},{25,1},{2,26},{10... | collective-permute-start | bytes 393224 | tf_op jit(solution)/shard_map/ppermute | solution.py:61
  74.6 9.8 %collective-permute-start.23 = (bf16[4,128,128]{2,1,0:T(8,128)(2,1)S(1)}, bf16[4,128,128]{2,1,0:T(8,128)(2,1)S(1)}, u32[]{:S(2)}, u32[]{:S(2)}) collective-permute-start(bf16[4,128,128]{2,1,0:T(8,128)(2,1)S(1)} %pad_maximum_fusion.12), channel_id=1, source_target_pairs={{0,8},{8,0},{16,24},{24,16},{1,9},{9,1},{17,25},{25,17},{2,10},{10... | collective-permute-start | bytes 393224 | tf_op jit(solution)/shard_map/ppermute | solution.py:61
  82.5 1.2 collective-permute-start.20
  102.3 5.5 %collective-permute-start.24 = (f32[16,128,128]{2,1,0:T(8,128)S(1)}, f32[16,128,128]{2,1,0:T(8,128)S(1)}, u32[]{:S(2)}, u32[]{:S(2)}) collective-permute-start(f32[16,128,128]{2,1,0:T(8,128)S(1)} %get-tuple-element.54), channel_id=1, source_target_pairs={{0,1},{1,0},{2,3},{3,2},{4,5},{5,4},{6,7},{7,6},{8,9},{9,8},{10,11... | collective-permute-start | bytes 3145736 | tf_op jit(solution)/shard_map/ppermute | solution.py:66
  102.4 6.1 %collective-permute-start.31 = (bf16[2,2,128,128]{3,2,1,0:T(8,128)(2,1)S(1)}, bf16[2,2,128,128]{3,2,1,0:T(8,128)(2,1)S(1)}, u32[]{:S(2)}, u32[]{:S(2)}) collective-permute-start(bf16[2,2,128,128]{3,2,1,0:T(8,128)(2,1)S(1)} %get-tuple-element.64), channel_id=1, source_target_pairs={{0,2},{1,3},{2,0},{3,1},{4,6},{5,7},{6,4},{7,5},{8,10},{9,11},{10,... | collective-permute-start | bytes 393224 | tf_op jit(solution)/shard_map/ppermute | solution.py:66
  104.3 9.0 %collective-permute-start.32 = (bf16[2,2,128,128]{3,2,1,0:T(8,128)(2,1)S(1)}, bf16[2,2,128,128]{3,2,1,0:T(8,128)(2,1)S(1)}, u32[]{:S(2)}, u32[]{:S(2)}) collective-permute-start(bf16[2,2,128,128]{3,2,1,0:T(8,128)(2,1)S(1)} %get-tuple-element.65), channel_id=1, source_target_pairs={{0,4},{1,5},{2,6},{3,7},{4,0},{5,1},{6,2},{7,3},{8,12},{9,13},{10,... | collective-permute-start | bytes 393224 | tf_op jit(solution)/shard_map/ppermute | solution.py:66
  104.3 9.3 %collective-permute-start.33 = (bf16[2,2,128,128]{3,2,1,0:T(8,128)(2,1)S(1)}, bf16[2,2,128,128]{3,2,1,0:T(8,128)(2,1)S(1)}, u32[]{:S(2)}, u32[]{:S(2)}) collective-permute-start(bf16[2,2,128,128]{3,2,1,0:T(8,128)(2,1)S(1)} %get-tuple-element.66), channel_id=1, source_target_pairs={{0,6},{1,7},{2,4},{3,5},{4,2},{5,3},{6,0},{7,1},{8,14},{9,15},{10,... | collective-permute-start | bytes 393224 | tf_op jit(solution)/shard_map/ppermute | solution.py:66
  106.0 9.0 %collective-permute-start.28 = (bf16[2,2,128,128]{3,2,1,0:T(8,128)(2,1)S(1)}, bf16[2,2,128,128]{3,2,1,0:T(8,128)(2,1)S(1)}, u32[]{:S(2)}, u32[]{:S(2)}) collective-permute-start(bf16[2,2,128,128]{3,2,1,0:T(8,128)(2,1)S(1)} %get-tuple-element.60), channel_id=1, source_target_pairs={{0,2},{1,3},{2,0},{3,1},{4,6},{5,7},{6,4},{7,5},{8,10},{9,11},{10,... | collective-permute-start | bytes 393224 | tf_op jit(solution)/shard_map/ppermute | solution.py:66
  107.8 11.2 %collective-permute-start.29 = (bf16[2,2,128,128]{3,2,1,0:T(8,128)(2,1)S(1)}, bf16[2,2,128,128]{3,2,1,0:T(8,128)(2,1)S(1)}, u32[]{:S(2)}, u32[]{:S(2)}) collective-permute-start(bf16[2,2,128,128]{3,2,1,0:T(8,128)(2,1)S(1)} %get-tuple-element.61), channel_id=1, source_target_pairs={{0,4},{1,5},{2,6},{3,7},{4,0},{5,1},{6,2},{7,3},{8,12},{9,13},{10,... | collective-permute-start | bytes 393224 | tf_op jit(solution)/shard_map/ppermute | solution.py:66
  108.5 10.5 %collective-permute-start.30 = (bf16[2,2,128,128]{3,2,1,0:T(8,128)(2,1)S(1)}, bf16[2,2,128,128]{3,2,1,0:T(8,128)(2,1)S(1)}, u32[]{:S(2)}, u32[]{:S(2)}) collective-permute-start(bf16[2,2,128,128]{3,2,1,0:T(8,128)(2,1)S(1)} %get-tuple-element.62), channel_id=1, source_target_pairs={{0,6},{1,7},{2,4},{3,5},{4,2},{5,3},{6,0},{7,1},{8,14},{9,15},{10,... | collective-permute-start | bytes 393224 | tf_op jit(solution)/shard_map/ppermute | solution.py:66
  113.4 7.3 %collective-permute-start.25 = (bf16[1,4,128,128]{3,2,1,0:T(8,128)(2,1)S(1)}, bf16[1,4,128,128]{3,2,1,0:T(8,128)(2,1)S(1)}, u32[]{:S(2)}, u32[]{:S(2)}) collective-permute-start(bf16[1,4,128,128]{3,2,1,0:T(8,128)(2,1)S(1)} %get-tuple-element.56), channel_id=1, source_target_pairs={{0,2},{1,3},{2,0},{3,1},{4,6},{5,7},{6,4},{7,5},{8,10},{9,11},{10,... | collective-permute-start | bytes 393224 | tf_op jit(solution)/shard_map/ppermute | solution.py:66
  113.6 10.3 %collective-permute-start.26 = (bf16[1,4,128,128]{3,2,1,0:T(8,128)(2,1)S(1)}, bf16[1,4,128,128]{3,2,1,0:T(8,128)(2,1)S(1)}, u32[]{:S(2)}, u32[]{:S(2)}) collective-permute-start(bf16[1,4,128,128]{3,2,1,0:T(8,128)(2,1)S(1)} %get-tuple-element.57), channel_id=1, source_target_pairs={{0,4},{1,5},{2,6},{3,7},{4,0},{5,1},{6,2},{7,3},{8,12},{9,13},{10,... | collective-permute-start | bytes 393224 | tf_op jit(solution)/shard_map/ppermute | solution.py:66
  115.0 8.8 %collective-permute-start.27 = (bf16[1,4,128,128]{3,2,1,0:T(8,128)(2,1)S(1)}, bf16[1,4,128,128]{3,2,1,0:T(8,128)(2,1)S(1)}, u32[]{:S(2)}, u32[]{:S(2)}) collective-permute-start(bf16[1,4,128,128]{3,2,1,0:T(8,128)(2,1)S(1)} %get-tuple-element.58), channel_id=1, source_target_pairs={{0,6},{1,7},{2,4},{3,5},{4,2},{5,3},{6,0},{7,1},{8,14},{9,15},{10,... | collective-permute-start | bytes 393224 | tf_op jit(solution)/shard_map/ppermute | solution.py:66
